TPU v7x, 256 devices: a whole 4x4x8 slice. The times are simulated.
256 devices in a mesh: section: 4 (over y_lo, core), expert: 64 (over z, x, y_hi).
Axes of the slice: x: 4, y: 4 (y_hi: 2, y_lo: 2; y = y_hi * 2 + y_lo), z: 8, core: 2. Of those that a mesh axis runs over, the one named last changes fastest.
Arguments:
- tokens: bfloat16 [4, 8192, 2048], P('section', 'expert'), may hold values from -6 to 6
- cotangent: bfloat16 [4, 8192, 2048], P('section', 'expert'), may hold values from -3 to 3
- routes: int32 [4, 8192, 8], P('section', 'expert'), may hold values from 0 to 63, all different within a row; in each aligned block of 128 rows (0 to 127, 128 to 255, ..., all dimensions but the last counted through in order) at most 18 rows name the same one
- route_weights: bfloat16 [4, 8192, 8], P('section', 'expert'), may hold values from 0.099609375 to 1
- weights: bfloat16 [3, 64, 2048, 384], P(None, 'expert'), may hold values from -0.125 to 0.125
Outputs:
- token_grads: bfloat16 [4, 8192, 2048], P('section', 'expert')
- gate_grads: bfloat16 [4, 8192, 8], P('section', 'expert')
- weight_grads: float32 [3, 64, 2048, 384], P(None, 'expert', 'section')
Inputs may be any that keep to these rules, and one draw needn't show every extreme that they name: `routes`: the 8 experts of a token differ. Among the 128 tokens of one device no expert is named more than 18 times, a bound that some block reaches.
All inputs are finite; a program needn't handle non-finite values.
Results may differ from a plain program's by a relative error of at most 0.0085.
Values may be sent and summed in bfloat16 or wider, within the bound.
No kernel may reach another device: no remote copies, remote signals or barrier semaphores. Data moves between devices by JAX's collectives and lax.ppermute only.
A program may use at most 128 MiB of HBM per device.

v0:
```python
import jax
import jax.numpy as jnp
from jax import lax
from jax.sharding import PartitionSpec as P

D = 2048
TOP_K = 8


def sent_together(arrays, axis, split_dim, concat_dim, along):
    columns = [a.reshape(*a.shape[:along], -1) for a in arrays]
    both = jnp.concatenate(columns, axis=along)
    filled, at, gathered = (
        lax.all_to_all(both, axis, split_axis=split_dim, concat_axis=concat_dim, tiled=True),
        0,
        [],
    )
    for a, column in zip(arrays, columns):
        section = filled[..., at : at + column.shape[along]]
        gathered.append(section.reshape(*section.shape[:along], *a.shape[along:]))
        at += column.shape[along]
    return tuple(gathered)


def slot_assign(route_block, experts, capacity):
    flat_ids = route_block.reshape(-1)
    pair_count = flat_ids.shape[0]
    one_hot = (flat_ids[:, None] == jnp.arange(experts, dtype=jnp.int32)[None, :]).astype(jnp.int32)
    before = jnp.cumsum(one_hot, axis=0) - one_hot
    slot_of = jnp.sum(before * one_hot, axis=1)
    slot_table = jnp.full((experts, capacity), pair_count, jnp.int32)
    slot_table = slot_table.at[flat_ids, slot_of].set(jnp.arange(pair_count, dtype=jnp.int32))
    return (slot_of.reshape(route_block.shape), slot_table)


def forward_part(in_rows, expert_w):
    gate_pre = jnp.dot(in_rows, expert_w[0], preferred_element_type=jnp.float32)
    up_pre = jnp.dot(in_rows, expert_w[1], preferred_element_type=jnp.float32)
    return (gate_pre, up_pre)


def backward_part(in_rows, gate_pre, up_pre, cot_rows, weight_rows, expert_w):
    sigmoid_v = jax.nn.sigmoid(gate_pre)
    silu_v = gate_pre * sigmoid_v
    hidden = (silu_v * up_pre).astype(jnp.bfloat16)
    back_proj = jnp.dot(cot_rows, expert_w[2], preferred_element_type=jnp.float32)
    row_gate = jnp.sum(hidden.astype(jnp.float32) * back_proj, axis=1).astype(jnp.bfloat16)
    weight = weight_rows.astype(jnp.float32)[:, None]
    d_hidden = weight * back_proj
    d_gate_pre = (d_hidden * up_pre * sigmoid_v * (1.0 + gate_pre * (1.0 - sigmoid_v))).astype(
        jnp.bfloat16
    )
    d_up_pre = (d_hidden * silu_v).astype(jnp.bfloat16)
    scaled = (weight * cot_rows.astype(jnp.float32)).astype(jnp.bfloat16)
    contract_rows = (((0,), (0,)), ((), ()))
    weight_part = jnp.stack(
        [
            lax.dot_general(in_rows, d_gate_pre, contract_rows, preferred_element_type=jnp.float32),
            lax.dot_general(in_rows, d_up_pre, contract_rows, preferred_element_type=jnp.float32),
            lax.dot_general(scaled, hidden, contract_rows, preferred_element_type=jnp.float32),
        ]
    )
    contract_ff = (((1,), (1,)), ((), ()))
    row_grads = (
        lax.dot_general(d_gate_pre, expert_w[0], contract_ff, preferred_element_type=jnp.float32)
        + lax.dot_general(d_up_pre, expert_w[1], contract_ff, preferred_element_type=jnp.float32)
    ).astype(jnp.bfloat16)
    return (row_gate, row_grads, weight_part)


def per_device(tokens, cotangent, routes, route_weights, weights):
    experts = lax.axis_size("expert")
    tok_count = tokens.shape[1]
    capacity = min(tok_count, max(2, (9 * tok_count * TOP_K + 8 * experts - 1) // (8 * experts)))
    route_block = routes[0]
    slots, slot_table = slot_assign(route_block, experts, capacity)
    token_ix = slot_table // TOP_K
    zero_row = jnp.zeros((1, D), tokens.dtype)
    send_in = jnp.concatenate([tokens[0], zero_row])[token_ix]
    send_cot = jnp.concatenate([cotangent[0], zero_row])[token_ix]
    send_weight = jnp.concatenate(
        [route_weights[0].reshape(-1), jnp.zeros((1,), route_weights.dtype)]
    )[slot_table]
    expert_w = weights[:, 0]
    recv_in = lax.all_to_all(send_in, "expert", split_axis=0, concat_axis=0, tiled=True)
    in_rows = recv_in.reshape(-1, D)
    gate_pre, up_pre = forward_part(in_rows, expert_w)
    recv_cot, recv_weight = sent_together((send_cot, send_weight), "expert", 0, 0, 2)
    row_gate, row_grads, weight_part = backward_part(
        in_rows, gate_pre, up_pre, recv_cot.reshape(-1, D), recv_weight.reshape(-1), expert_w
    )
    back_rows, back_gate = (
        lax.all_to_all(
            row_grads.reshape(experts, capacity, D),
            "expert",
            split_axis=0,
            concat_axis=0,
            tiled=True,
        ),
        lax.all_to_all(
            row_gate.reshape(experts, capacity), "expert", split_axis=0, concat_axis=0, tiled=True
        ),
    )
    flat_rows = back_rows.reshape(experts * capacity, D)
    flat_index = route_block * capacity + slots
    accum = jnp.zeros((tok_count, D), jnp.float32)
    for position in range(TOP_K):
        accum = accum + flat_rows[flat_index[:, position]].astype(jnp.float32)
    token_grads = accum.astype(jnp.bfloat16)[None]
    gate_grads = back_gate.reshape(-1)[flat_index][None]
    partial_sum = weight_part[:, None]
    sections = lax.axis_size("section")
    summed = lax.psum_scatter(
        partial_sum.astype(jnp.bfloat16), "section", scatter_dimension=2, tiled=True
    ).astype(jnp.float32)
    weight_grads = summed / sections
    return (token_grads, gate_grads, weight_grads)


def solution(mesh):
    placed = (
        P("section", "expert", None),
        P("section", "expert", None),
        P("section", "expert", None),
        P("section", "expert", None),
        P(None, "expert", None, None),
    )
    return jax.shard_map(
        per_device,
        mesh=mesh,
        in_specs=placed,
        out_specs=(
            P("section", "expert", None),
            P("section", "expert", None),
            P(None, "expert", "section", None),
        ),
        check_vma=False,
    )
```

profile of v0, /device:TPU:8, one launch (start us, length us, event | category | flops | bytes accessed | tf_op | source)
XLA Modules:
  0.0 638.3 jit_solution(6865568840645223838)
XLA Ops:
  8.3 18.0 %reduce-window.6 = s32[64,8,128]{2,1,0:T(8,128)S(1)} reduce-window(s32[64,8,128]{2,1,0:T(8,128)S(1)} %fusion.26, s32[]{:T(128)} %constant.18.clone.1), window={size=1x1x128 pad=0_0x0_0x127_0}, to_apply=%region_0.0 | reduce-window | flops 8323072 | bytes 524292 | tf_op jit(solution)/shard_map/reduce-window
  34.2 6.1 gather_fusion.2
  40.3 7.6 %reshape.331 = bf16[64,18,2048]{2,1,0:T(8,128)(2,1)} reshape(bf16[1152,2048]{1,0:T(8,128)(2,1)} %gather_fusion.2) | data formatting | bytes 9437184 | tf_op jit(solution)/shard_map/gather | solution.py:79
  47.8 14.0 %all-to-all-start.1 = ((bf16[64,18,2048]{2,1,0:T(8,128)(2,1)}), bf16[64,18,2048]{2,1,0:T(8,128)(2,1)}, u32[]{:S(2)}, u32[]{:S(2)}) async-start(bf16[64,18,2048]{2,1,0:T(8,128)(2,1)} %reshape.331), calls=%async_computation.1 | async-start | bytes 12582912 | tf_op jit(solution)/shard_map/all_to_all | solution.py:85
  62.4 7.3 %gather_fusion.1 = bf16[1152]{0:T(1024)(128)(2,1)S(1)} fusion(bf16[1025]{0:T(1024)(128)(2,1)S(1)} %pad_maximum_fusion.2, s32[2048]{0:T(1024)S(1)} %pad_clamp_fusion), kind=kCustom, calls=%fused_computation.1 | custom fusion | bytes 9216 | tf_op jit(solution)/shard_map/gather | solution.py:81
  70.0 6.1 gather_fusion
  76.1 7.6 %reshape.315 = bf16[64,18,2048]{2,1,0:T(8,128)(2,1)} reshape(bf16[1152,2048]{1,0:T(8,128)(2,1)} %gather_fusion) | data formatting | bytes 9437184 | tf_op jit(solution)/shard_map/gather | solution.py:80
  83.7 6.6 %pad_maximum_fusion = bf16[64,18,2049]{2,1,0:T(8,128)(2,1)} fusion(bf16[64,18,1]{2,1,0:T(8,128)(2,1)S(1)} %reshape.427, bf16[64,18,2048]{2,1,0:T(8,128)(2,1)} %reshape.315), kind=kLoop, calls=%fused_computation.16 | loop fusion | flops 9441792 | bytes 9441792 | tf_op jit(solution)/shard_map/concatenate | solution.py:12
  90.3 114.9 %all-to-all-done.1 = bf16[64,18,2048]{2,1,0:T(8,128)(2,1)} async-done(((bf16[64,18,2048]{2,1,0:T(8,128)(2,1)}), bf16[64,18,2048]{2,1,0:T(8,128)(2,1)}, u32[]{:S(2)}, u32[]{:S(2)}) %all-to-all-start.1) | async-done | bytes 4718624 | tf_op jit(solution)/shard_map/all_to_all | solution.py:85
  205.3 5.9 all-to-all-start
  211.2 7.7 %reshape.296 = bf16[1152,2048]{1,0:T(8,128)(2,1)} reshape(bf16[64,18,2048]{2,1,0:T(8,128)(2,1)} %all-to-all-done.1) | data formatting | bytes 9437184 | tf_op jit(solution)/shard_map/reshape | solution.py:86
  218.9 6.5 %fusion.10 = f32[1152,384]{0,1:T(8,128)} fusion(bf16[1152,2048]{1,0:T(8,128)(2,1)} %reshape.296, bf16[3,1,2048,384]{3,2,1,0:T(8,128)(2,1)} %param.9), kind=kOutput, calls=%fused_computation.35 | convolution fusion | flops 1811939328 | bytes 8060928 | tf_op jit(solution)/shard_map/dot_general | solution.py:37
  225.4 5.0 fusion.13
  230.4 129.2 %all-to-all-done = bf16[64,18,2049]{2,1,0:T(8,128)(2,1)} async-done(((bf16[64,18,2049]{2,1,0:T(8,128)(2,1)}), bf16[64,18,2049]{2,1,0:T(8,128)(2,1)}, u32[]{:S(2)}, u32[]{:S(2)}) %all-to-all-start) | async-done | bytes 4720928 | tf_op jit(solution)/shard_map/all_to_all | solution.py:14
  359.6 6.5 %slice.92 = bf16[64,18,2048]{2,1,0:T(8,128)(2,1)} slice(bf16[64,18,2049]{2,1,0:T(8,128)(2,1)} %all-to-all-done), slice={[0:64], [0:18], [0:2048]} | slice | bytes 9437184 | tf_op jit(solution)/shard_map/slice | solution.py:19
  366.1 7.9 %reshape.295 = bf16[1152,2048]{1,0:T(8,128)(2,1)} reshape(bf16[64,18,2048]{2,1,0:T(8,128)(2,1)} %slice.92) | data formatting | bytes 9437184 | tf_op jit(solution)/shard_map/reshape | solution.py:90
  375.5 8.0 %multiply_reduce_fusion = (bf16[1152]{0:T(1024)(128)(2,1)S(1)}, bf16[1152,384]{0,1:T(8,128)(2,1)S(1)}, bf16[1152,384]{0,1:T(8,128)(2,1)S(1)}, bf16[1152,384]{0,1:T(8,128)(2,1)}) fusion(f32[1152,384]{0,1:T(8,128)} %fusion.13, f32[1152,384]{0,1:T(8,128)} %fusion.10, f32[1152]{0:T(1024)S(1)} %reshape.306, bf16[1152,2048]{1,0:T(8,128)(2,1)} %reshape.295, ...), kind=kOutput, calls=%fused_computation.27 | convolution fusion | flops 1820343168 | bytes 12491520 | tf_op jit(solution)/shard_map/dot_general | solution.py:46
  387.4 7.4 %all-to-all-start.3 = ((bf16[64,1,18]{2,1,0:T(2,128)(2,1)}), bf16[64,1,18]{2,1,0:T(2,128)(2,1)S(1)}, u32[]{:S(2)}, u32[]{:S(2)}) async-start(bf16[64,1,18]{2,1,0:T(2,128)(2,1)} %convert_element_type.203), calls=%async_computation.3 | async-start | bytes 65536 | tf_op jit(solution)/shard_map/all_to_all | solution.py:100
  399.0 6.3 fusion
  409.2 7.6 %reshape.297 = bf16[64,18,2048]{2,1,0:T(8,128)(2,1)} reshape(bf16[1152,2048]{1,0:T(8,128)(2,1)} %fusion) | data formatting | bytes 9437184 | tf_op jit(solution)/shard_map/reshape | solution.py:94
  416.8 13.2 %all-to-all-start.2 = ((bf16[64,18,2048]{2,1,0:T(8,128)(2,1)}), bf16[64,18,2048]{2,1,0:T(8,128)(2,1)}, u32[]{:S(2)}, u32[]{:S(2)}) async-start(bf16[64,18,2048]{2,1,0:T(8,128)(2,1)} %reshape.297), calls=%async_computation.2 | async-start | bytes 12582912 | tf_op jit(solution)/shard_map/all_to_all | solution.py:93
  430.1 5.3 fusion.5
  438.8 6.8 %gather_fusion.11 = bf16[1024]{0:T(1024)(128)(2,1)S(1)} fusion(bf16[1152]{0:T(1024)(128)(2,1)S(1)} %reshape.300, s32[1024]{0:T(1024)S(1)} %broadcast_clamp_fusion), kind=kCustom, calls=%fused_computation.11 | custom fusion | bytes 8192 | tf_op jit(solution)/shard_map/gather | solution.py:110
  446.4 125.3 %all-to-all-done.2 = bf16[64,18,2048]{2,1,0:T(8,128)(2,1)} async-done(((bf16[64,18,2048]{2,1,0:T(8,128)(2,1)}), bf16[64,18,2048]{2,1,0:T(8,128)(2,1)}, u32[]{:S(2)}, u32[]{:S(2)}) %all-to-all-start.2) | async-done | bytes 4718624 | tf_op jit(solution)/shard_map/all_to_all | solution.py:93
  571.7 17.4 %reshape.298 = bf16[1152,2048]{1,0:T(8,128)(2,1)} reshape(bf16[64,18,2048]{2,1,0:T(8,128)(2,1)} %all-to-all-done.2) | data formatting | bytes 9437184 | tf_op jit(solution)/shard_map/reshape | solution.py:104
  589.0 4.4 gather_fusion.10
  593.4 4.4 gather_fusion.9
  597.8 4.4 gather_fusion.8
  602.2 4.4 gather_fusion.7
  611.0 4.4 gather_fusion.5
  615.4 5.2 gather_fusion.4
  620.6 5.2 gather_fusion.3
  (83 shorter events, 37.4 us)
Async XLA Ops:
  47.8 14.0 %copy-start.5 = (bf16[1,128,8]{1,2,0:T(8,128)(2,1)S(1)}, bf16[1,128,8]{1,2,0:T(8,128)(2,1)}, u32[]{:S(2)}) copy-start(bf16[1,128,8]{1,2,0:T(8,128)(2,1)} %param.8) | copy-start | bytes 6148
  47.8 157.4 %all-to-all-start.1 = ((bf16[64,18,2048]{2,1,0:T(8,128)(2,1)}), bf16[64,18,2048]{2,1,0:T(8,128)(2,1)}, u32[]{:S(2)}, u32[]{:S(2)}) async-start(bf16[64,18,2048]{2,1,0:T(8,128)(2,1)} %reshape.331), calls=%async_computation.1 | async-start | bytes 12582912 | tf_op jit(solution)/shard_map/all_to_all | solution.py:85
  62.4 7.6 %copy-start.4 = (bf16[1,128,2048]{2,1,0:T(8,128)(2,1)S(1)}, bf16[1,128,2048]{2,1,0:T(8,128)(2,1)}, u32[]{:S(2)}) copy-start(bf16[1,128,2048]{2,1,0:T(8,128)(2,1)} %param.6) | copy-start | bytes 1572868
  205.3 154.3 %all-to-all-start = ((bf16[64,18,2049]{2,1,0:T(8,128)(2,1)}), bf16[64,18,2049]{2,1,0:T(8,128)(2,1)}, u32[]{:S(2)}, u32[]{:S(2)}) async-start(bf16[64,18,2049]{2,1,0:T(8,128)(2,1)} %pad_maximum_fusion), calls=%async_computation | async-start | bytes 13369344 | tf_op jit(solution)/shard_map/all_to_all | solution.py:14
  218.9 6.5 %copy-start = (bf16[1152,2048]{1,0:T(8,128)(2,1)S(1)}, bf16[1152,2048]{1,0:T(8,128)(2,1)}, u32[]{:S(2)}) copy-start(bf16[1152,2048]{1,0:T(8,128)(2,1)} %reshape.296) | copy-start | bytes 14155780
  374.0 9.4 %slice-start.2 = ((s8[4718592]{0:T(1024)(128)(4,1)}), s8[524288]{0:T(1024)(128)(4,1)S(1)}, s32[]{:S(2)}) async-start(s8[4718592]{0:T(1024)(128)(4,1)} %bitcast.84), calls=%async_computation.8 | async-start | bytes 1048576
  375.5 8.0 %slice-start.3 = ((s8[4718592]{0:T(1024)(128)(4,1)}), s8[4194304]{0:T(1024)(128)(4,1)S(1)}, s32[]{:S(2)}) async-start(s8[4718592]{0:T(1024)(128)(4,1)} %bitcast.84), calls=%async_computation.9 | async-start | bytes 8388608
  387.4 29.4 %all-to-all-start.3 = ((bf16[64,1,18]{2,1,0:T(2,128)(2,1)}), bf16[64,1,18]{2,1,0:T(2,128)(2,1)S(1)}, u32[]{:S(2)}, u32[]{:S(2)}) async-start(bf16[64,1,18]{2,1,0:T(2,128)(2,1)} %convert_element_type.203), calls=%async_computation.3 | async-start | bytes 65536 | tf_op jit(solution)/shard_map/all_to_all | solution.py:100
  394.8 4.2 copy-start.2
  394.8 10.5 %slice-start = ((s8[4718592]{0:T(1024)(128)(4,1)}), s8[4194304]{0:T(1024)(128)(4,1)S(1)}, s32[]{:S(2)}) async-start(s8[4718592]{0:T(1024)(128)(4,1)} %bitcast.82), calls=%async_computation.6 | async-start | bytes 8388608
  399.0 6.3 slice-start.1
  416.8 13.3 %copy-start.3 = (bf16[1152,384]{0,1:T(8,128)(2,1)S(1)}, bf16[1152,384]{0,1:T(8,128)(2,1)}, u32[]{:S(2)}) copy-start(bf16[1152,384]{0,1:T(8,128)(2,1)} %get-tuple-element.23) | copy-start | bytes 2654212
  416.8 154.9 %all-to-all-start.2 = ((bf16[64,18,2048]{2,1,0:T(8,128)(2,1)}), bf16[64,18,2048]{2,1,0:T(8,128)(2,1)}, u32[]{:S(2)}, u32[]{:S(2)}) async-start(bf16[64,18,2048]{2,1,0:T(8,128)(2,1)} %reshape.297), calls=%async_computation.2 | async-start | bytes 12582912 | tf_op jit(solution)/shard_map/all_to_all | solution.py:93
  430.0 198.4 %reduce-scatter.2.cloned.1.call-start = ((), (), s32[]{:S(2)}) async-start(), calls=%async_computation.5 | async-start | bytes 5898240 | tf_op jit(solution)/shard_map/reduce_scatter | solution.py:113
  430.0 5.3 copy-start.1
Sparse Core Ops, SparseCore 0:
  438.0 79.1 reduce-scatter.1
where the time goes:
time: 642 us; the launch traced here: 638 us
  waiting for transfers between devices  369 us (57%)
  local copies, waits for them, and re-layouts  135 us (21%)
  matrix products  42.2 us (7%)
  starting transfers between devices  40.5 us (6%)
  other arithmetic  36.3 us (6%)
  between operations  14.7 us (2%)
    all_to_all x1, waiting for transfers between devices, sent_together(): lax.all_to_all(both, axis, split_axis=split_dim, concat_axis=concat_dim,...  129 us
    all_to_all x1, waiting for transfers between devices, per_device(): lax.all_to_all(row_grads.reshape(experts, capacity, D), 'expert', split_a...  125 us
    all_to_all x1, waiting for transfers between devices, per_device(): lax.all_to_all(send_in, 'expert', split_axis=0, concat_axis=0, tiled=True)  115 us
    gather x8, local copies, waits for them, and re-layouts, per_device(): accum = accum + flat_rows[flat_index[:, position]].astype(jnp.float32)  36.7 us
    another operation x3, other arithmetic  18.2 us
    reshape x1, local copies, waits for them, and re-layouts, per_device(): flat_rows = back_rows.reshape(experts * capacity, D)  17.4 us
    all_to_all x1, starting transfers between devices, per_device(): lax.all_to_all(send_in, 'expert', split_axis=0, concat_axis=0, tiled=True)  14 us
    gather x2, local copies, waits for them, and re-layouts, per_device(): send_cot = jnp.concatenate([cotangent[0], zero_row])[token_ix]  13.7 us
  transfers between devices with their start and end apart: 5, of which 3 were waited for; matrix products, arithmetic and copies ran while one was open for 22% of the time, Pallas kernels for 0%

commit v1 on v0

v1 whole, which is shorter than its diff:
```python
import functools

import jax
import jax.numpy as jnp
from jax import lax
from jax.experimental import pallas as pl
from jax.experimental.pallas import tpu as pltpu
from jax.sharding import PartitionSpec as P

D = 2048
FF = 384
TOP_K = 8
TOK = 128
CAP = 18
PLANES = 8
PLANE = 8
META = 8
ROWS = TOK + META
HALF = 64
NEAR = (0, -1, 1)
FAR = (-2, 2, -3, 3, 4)
NEAR_ROWS = 56
FAR_ROWS = 96
COLS = 512
BF = jnp.bfloat16
F32 = jnp.float32
VMEM_LIMIT = 56 * 1024 * 1024


def params():
    return pltpu.CompilerParams(vmem_limit_bytes=VMEM_LIMIT)


def cost(flops, nbytes):
    return pl.CostEstimate(flops=flops, bytes_accessed=nbytes, transcendentals=0)


def forward_pairs():
    return [(e, (e + PLANE) % (PLANES * PLANE)) for e in range(PLANES * PLANE)]


def backward_pairs():
    return [(e, (e - PLANE) % (PLANES * PLANE)) for e in range(PLANES * PLANE)]


def after(value, *done):
    return lax.optimization_barrier((value, *done))[0]


def plane_groups():
    groups = []
    for parity in range(2):
        for core in range(2):
            for z in range(PLANES):
                groups.append(
                    [
                        ((parity ^ (j % 2)) * 2 + core) * 64 + z * PLANE + j
                        for j in range(PLANE)
                    ]
                )
    return groups


def exchange(rows, per_dest):
    sent = rows.reshape(PLANE, per_dest, D)
    got = lax.all_to_all(
        sent, ("section", "expert"), 0, 0, axis_index_groups=plane_groups(), tiled=True
    )
    return got.reshape(PLANE * per_dest, D)


def pack_body(tok_ref, routes_ref, weight_ref, out_ref):
    out_ref[0:TOK, :] = tok_ref[...]
    tail = jnp.concatenate(
        [routes_ref[...].astype(F32), weight_ref[...].astype(F32), jnp.zeros((META, COLS - 256), F32)],
        axis=1,
    )
    keep = jnp.where(pl.program_id(0) == 0, 1.0, 0.0)
    out_ref[TOK:ROWS, :] = (tail * keep).astype(BF)


def pack(tok, routes_t, weight_t):
    return pl.pallas_call(
        pack_body,
        grid=(D // COLS,),
        in_specs=[
            pl.BlockSpec((TOK, COLS), lambda i: (0, i)),
            pl.BlockSpec((META, TOK), lambda i: (0, 0)),
            pl.BlockSpec((META, TOK), lambda i: (0, 0)),
        ],
        out_specs=pl.BlockSpec((ROWS, COLS), lambda i: (0, i)),
        out_shape=jax.ShapeDtypeStruct((ROWS, D), BF),
        compiler_params=params(),
        cost_estimate=cost(0, 4 * ROWS * D),
        name="pack_rows",
    )(tok, routes_t, weight_t)


def placement(q, per_dest):
    tokens = q.shape[1]
    rows = PLANE * per_dest
    wide = jnp.broadcast_to(q[:, None, :], (PLANE, per_dest, tokens)).reshape(rows, tokens)
    code = lax.broadcasted_iota(jnp.int32, (PLANE, per_dest, tokens), 1).reshape(rows, tokens)
    return wide == code


def select_tok_body(per_dest, count, z_ref, *refs):
    blocks = refs[: len(refs) - 6]
    out_ref, q_ref, w_ref, r_ref, place, x_ref = refs[len(refs) - 6 :]
    split = count == len(FAR)
    metas = [b for b in blocks if b.shape[0] != HALF]

    @pl.when(pl.program_id(0) == 0)
    def _():
        first = z_ref[0] // PLANE * PLANE
        ids = lax.broadcasted_iota(jnp.int32, (PLANE, TOK), 0) + first
        earlier = (
            lax.broadcasted_iota(jnp.int32, (TOK, TOK), 0)
            < lax.broadcasted_iota(jnp.int32, (TOK, TOK), 1)
        ).astype(F32).astype(BF)
        for b, ref in enumerate(metas):
            base = ref.shape[0] - META
            routes = ref[base : base + META, 0:TOK].astype(F32)
            weight = ref[base : base + META, TOK : 2 * TOK].astype(F32)
            ids_f = ids.astype(F32)
            member = jnp.zeros((PLANE, TOK), F32)
            scale = jnp.zeros((PLANE, TOK), F32)
            for k in range(TOP_K):
                hit = ids_f == routes[k : k + 1, :]
                member = jnp.where(hit, 1.0, member)
                scale = jnp.where(hit, weight[k : k + 1, :], scale)
            slot = jnp.dot(member.astype(BF), earlier, preferred_element_type=F32)
            q = jnp.where(member > 0.0, slot + float(b * CAP), -1.0).astype(jnp.int32)
            q_ref[:, b * TOK : (b + 1) * TOK] = q
            w_ref[:, b * TOK : (b + 1) * TOK] = scale
            r_ref[:, b * TOK : (b + 1) * TOK] = routes
        place[...] = jnp.where(placement(q_ref[...], per_dest), 1.0, 0.0).astype(BF)

    at = 0
    for ref in blocks:
        size = HALF if split and ref.shape[0] in (HALF, HALF + META) else TOK
        x_ref[at : at + size, :] = ref[0:size, :]
        at += size
    out_ref[...] = jnp.dot(place[...], x_ref[...], preferred_element_type=F32).astype(BF)


def select_tok(z, blocks, per_dest, count):
    rows = PLANE * per_dest
    tokens = count * TOK
    const = lambda i: (0, 0)
    small = pl.BlockSpec((PLANE, tokens), const)
    return pl.pallas_call(
        functools.partial(select_tok_body, per_dest, count),
        grid=(D // COLS,),
        in_specs=[pl.BlockSpec(memory_space=pltpu.SMEM)]
        + [pl.BlockSpec((b.shape[0], COLS), lambda i: (0, i)) for b in blocks],
        out_specs=[pl.BlockSpec((rows, COLS), lambda i: (0, i)), small, small, small],
        out_shape=[
            jax.ShapeDtypeStruct((rows, D), BF),
            jax.ShapeDtypeStruct((PLANE, tokens), jnp.int32),
            jax.ShapeDtypeStruct((PLANE, tokens), F32),
            jax.ShapeDtypeStruct((PLANE, tokens), F32),
        ],
        scratch_shapes=[pltpu.VMEM((rows, tokens), BF), pltpu.VMEM((tokens, COLS), BF)],
        compiler_params=params(),
        cost_estimate=cost(2 * rows * tokens * D, 2 * D * (rows + tokens)),
        name="select_tokens",
    )(z, *blocks)


def select_cot_body(per_dest, count, q_ref, w_ref, *refs):
    blocks = refs[: len(refs) - 3]
    out_ref, place, x_ref = refs[len(refs) - 3 :]
    rows, tokens = place.shape

    @pl.when(pl.program_id(0) == 0)
    def _():
        wide = jnp.broadcast_to(w_ref[...][:, None, :], (PLANE, per_dest, tokens)).reshape(rows, tokens)
        place[...] = jnp.where(placement(q_ref[...], per_dest), wide, 0.0).astype(BF)

    at = 0
    for ref in blocks:
        size = ref.shape[0]
        x_ref[at : at + size, :] = ref[...]
        at += size
    out_ref[...] = jnp.dot(place[...], x_ref[...], preferred_element_type=F32).astype(BF)


def select_cot(q, w, blocks, per_dest, count):
    rows = PLANE * per_dest
    tokens = count * TOK
    small = pl.BlockSpec((PLANE, tokens), lambda i: (0, 0))
    return pl.pallas_call(
        functools.partial(select_cot_body, per_dest, count),
        grid=(D // COLS,),
        in_specs=[small, small]
        + [pl.BlockSpec((b.shape[0], COLS), lambda i: (0, i)) for b in blocks],
        out_specs=pl.BlockSpec((rows, COLS), lambda i: (0, i)),
        out_shape=jax.ShapeDtypeStruct((rows, D), BF),
        scratch_shapes=[pltpu.VMEM((rows, tokens), BF), pltpu.VMEM((tokens, COLS), BF)],
        compiler_params=params(),
        cost_estimate=cost(2 * rows * tokens * D, 2 * D * (rows + tokens)),
        name="select_cotangents",
    )(q, w, *blocks)


def weight_spec(which):
    return pl.BlockSpec((None, None, D, FF), lambda i: (which, 0, 0, 0))


def forward_body(x_ref, wg_ref, wu_ref, g_ref, u_ref):
    g_ref[...] = jnp.dot(x_ref[...], wg_ref[...], preferred_element_type=F32)
    u_ref[...] = jnp.dot(x_ref[...], wu_ref[...], preferred_element_type=F32)


def forward(x, weights, tile):
    rows = x.shape[0]
    out = jax.ShapeDtypeStruct((rows, FF), F32)
    spec = pl.BlockSpec((tile, FF), lambda i: (i, 0))
    return pl.pallas_call(
        forward_body,
        grid=(rows // tile,),
        in_specs=[pl.BlockSpec((tile, D), lambda i: (i, 0)), weight_spec(0), weight_spec(1)],
        out_specs=[spec, spec],
        out_shape=[out, out],
        compiler_params=params(),
        cost_estimate=cost(4 * rows * D * FF, 2 * D * (rows + 2 * FF)),
        name="expert_forward",
    )(x, weights, weights)


def backward_body(per_dest, gate_row, sc_ref, g_ref, u_ref, wg_ref, wu_ref, wd_ref,
                  rows_ref, dg_ref, du_ref, h_ref, total):
    tile = sc_ref.shape[0]
    back = jnp.dot(sc_ref[...], wd_ref[...], preferred_element_type=F32)
    gate = g_ref[...]
    up = u_ref[...]
    sig = jax.nn.sigmoid(gate)
    silu = gate * sig
    hidden = (silu * up).astype(BF)
    d_gate = (back * up * sig * (1.0 + gate * (1.0 - sig))).astype(BF)
    d_up = (back * silu).astype(BF)
    h_ref[...] = hidden
    dg_ref[...] = d_gate
    du_ref[...] = d_up
    by_ff = (((1,), (1,)), ((), ()))
    total[...] = lax.dot_general(d_gate, wg_ref[...], by_ff, preferred_element_type=F32)
    total[...] += lax.dot_general(d_up, wu_ref[...], by_ff, preferred_element_type=F32)
    product = hidden.astype(F32) * back
    ones = jnp.ones((8, FF), F32)
    pick = lax.broadcasted_iota(jnp.int32, (8, per_dest), 0) == gate_row % 8
    for d in range(tile // per_dest):
        part = lax.dot_general(
            ones, product[d * per_dest : (d + 1) * per_dest, :], by_ff,
            preferred_element_type=F32, precision=lax.Precision.HIGHEST,
        )
        at = d * per_dest + gate_row // 8 * 8
        total[at : at + 8, 0:per_dest] += jnp.where(pick, part, 0.0)
    rows_ref[...] = total[...].astype(BF)


def backward(scaled, gate, up, weights, tile, per_dest, gate_row):
    rows = scaled.shape[0]
    wide = pl.BlockSpec((tile, D), lambda i: (i, 0))
    slim = pl.BlockSpec((tile, FF), lambda i: (i, 0))
    small = jax.ShapeDtypeStruct((rows, FF), BF)
    return pl.pallas_call(
        functools.partial(backward_body, per_dest, gate_row),
        grid=(rows // tile,),
        in_specs=[wide, slim, slim, weight_spec(0), weight_spec(1), weight_spec(2)],
        out_specs=[wide, slim, slim, slim],
        out_shape=[jax.ShapeDtypeStruct((rows, D), BF), small, small, small],
        scratch_shapes=[pltpu.VMEM((tile, D), F32)],
        compiler_params=params(),
        cost_estimate=cost(6 * rows * D * FF, 4 * D * rows + 6 * D * FF),
        name="expert_backward",
    )(scaled, gate, up, weights, weights, weights)


def weight_grad_body(xn, xf, sn, sf, dgn, dgf, dun, duf, hn, hf, out_ref):
    by_rows = (((0,), (0,)), ((), ()))

    def both(a, b, c, d):
        return lax.dot_general(a[...], c[...], by_rows, preferred_element_type=F32) + lax.dot_general(
            b[...], d[...], by_rows, preferred_element_type=F32
        )

    out_ref[0] = both(xn, xf, dgn, dgf).astype(BF)
    out_ref[1] = both(xn, xf, dun, duf).astype(BF)
    out_ref[2] = both(sn, sf, hn, hf).astype(BF)


def weight_grad(near, far):
    tile = 512
    args, specs = [], []
    for a, b in zip(near, far):
        for v in (a, b):
            args.append(v)
            if v.shape[1] == D:
                specs.append(pl.BlockSpec((v.shape[0], tile), lambda i: (0, i)))
            else:
                specs.append(pl.BlockSpec(v.shape, lambda i: (0, 0)))
    rows = near[0].shape[0] + far[0].shape[0]
    return pl.pallas_call(
        weight_grad_body,
        grid=(D // tile,),
        in_specs=specs,
        out_specs=pl.BlockSpec((3, None, tile, FF), lambda i: (0, 0, i, 0)),
        out_shape=jax.ShapeDtypeStruct((3, 1, D, FF), BF),
        compiler_params=params(),
        cost_estimate=cost(6 * rows * D * FF, 4 * rows * D + 6 * D * FF),
        name="weight_grads",
    )(*args)


def combine_body(per_dest, count, gate_row, z_ref, q_ref, w_ref, r_ref, x_ref, *refs):
    place = refs[-1]
    outs = refs[:-1]
    rows, tokens = place.shape
    first_step = pl.program_id(0) == 0

    @pl.when(first_step)
    def _():
        place[...] = jnp.where(placement(q_ref[...], per_dest), 1.0, 0.0).astype(BF)

    summed = lax.dot_general(
        place[...], x_ref[...], (((0,), (0,)), ((), ())), preferred_element_type=F32
    ).astype(BF)
    at = 0
    for ref in outs:
        size = ref.shape[0] if ref.shape[0] == HALF else ref.shape[0] - META
        ref[0:size, :] = summed[at : at + size, :]
        if ref.shape[0] != HALF:
            ref[size : size + META, :] = jnp.zeros((META, COLS), BF)
        at += size

    @pl.when(first_step)
    def _():
        first = z_ref[0] // PLANE * PLANE
        find = (
            lax.broadcasted_iota(jnp.int32, (PLANE, rows), 1)
            == lax.broadcasted_iota(jnp.int32, (PLANE, rows), 0) * per_dest + gate_row
        )
        gates = jnp.dot(
            jnp.where(find, 1.0, 0.0).astype(BF), x_ref[:, 0:TOK], preferred_element_type=F32
        )
        by_code = jnp.zeros((PLANE, tokens), F32)
        line = lax.broadcasted_iota(jnp.int32, (PLANE, TOK), 0)
        lane = lax.broadcasted_iota(jnp.int32, (PLANE, TOK), 1)
        code = lax.broadcasted_iota(jnp.int32, (TOK, tokens), 0)
        for j in range(PLANE):
            own = jnp.where((line == j) & (lane < count * CAP), gates, 0.0).astype(BF)
            hit = jnp.where(code == q_ref[j : j + 1, :], 1.0, 0.0).astype(BF)
            by_code = by_code + jnp.dot(own, hit, preferred_element_type=F32)
        weight = w_ref[...]
        by_code = jnp.where(weight > 0.0, by_code / jnp.where(weight > 0.0, weight, 1.0), 0.0)
        routes = r_ref[...]
        by_k = jnp.zeros((PLANE, tokens), F32)
        for j in range(PLANE):
            mine = routes == (first + j).astype(F32)
            by_k = jnp.where(mine, by_code[j : j + 1, :], by_k)
        b = 0
        for ref in outs:
            if ref.shape[0] == HALF:
                continue
            size = ref.shape[0] - META
            ref[size : size + META, 0:TOK] = by_k[:, b * TOK : (b + 1) * TOK].astype(BF)
            b += 1


def combine(z, q, w, r, x, sizes, per_dest, count, gate_row):
    rows = PLANE * per_dest
    tokens = count * TOK
    small = pl.BlockSpec((PLANE, tokens), lambda i: (0, 0))
    return pl.pallas_call(
        functools.partial(combine_body, per_dest, count, gate_row),
        grid=(D // COLS,),
        in_specs=[
            pl.BlockSpec(memory_space=pltpu.SMEM),
            small,
            small,
            small,
            pl.BlockSpec((rows, COLS), lambda i: (0, i)),
        ],
        out_specs=[pl.BlockSpec((n, COLS), lambda i: (0, i)) for n in sizes],
        out_shape=[jax.ShapeDtypeStruct((n, D), BF) for n in sizes],
        scratch_shapes=[pltpu.VMEM((rows, tokens), BF)],
        compiler_params=params(),
        cost_estimate=cost(2 * rows * tokens * D, 2 * D * (rows + tokens)),
        name="combine_rows",
    )(z, q, w, r, x)


def ring_gather(own):
    fw, bw = forward_pairs(), backward_pairs()
    got = {0: own}
    down = up = own
    for step in (1, 2, 3):
        down = lax.ppermute(down, "expert", fw)
        up = lax.ppermute(up, "expert", bw)
        got[-step], got[step] = down, up
    top = lax.ppermute(down[:HALF], "expert", fw)
    low = lax.ppermute(up[HALF:], "expert", bw)
    near = [got[k] for k in NEAR]
    far = [got[k] for k in FAR[:-1]] + [top, low]
    return near, far


def added(a, b):
    return (a.astype(F32) + b.astype(F32)).astype(BF)


def ring_scatter(near, far):
    fw, bw = forward_pairs(), backward_pairs()
    part = dict(zip(NEAR, near)) | dict(zip(FAR[:-1], far[:-2]))
    top = lax.ppermute(far[-2], "expert", fw)
    low = lax.ppermute(far[-1], "expert", bw)
    ahead = added(part[3], jnp.pad(top, ((0, META + HALF), (0, 0))))
    behind = added(part[-3], jnp.pad(low, ((HALF, 0), (0, 0))))
    for step in (2, 1):
        ahead = added(part[step], lax.ppermute(ahead, "expert", fw))
        behind = added(part[-step], lax.ppermute(behind, "expert", bw))
    ahead = lax.ppermute(ahead, "expert", fw)
    behind = lax.ppermute(behind, "expert", bw)
    return part[0].astype(F32) + ahead.astype(F32) + behind.astype(F32)


def per_device(tokens, cotangent, routes, route_weights, weights):
    z = lax.axis_index("expert").reshape(1).astype(jnp.int32)
    own = pack(tokens[0], routes[0].T, route_weights[0].T)
    tok_near, tok_far = ring_gather(own)
    cot_near, cot_far = ring_gather(after(cotangent[0], tok_far[-1], tok_far[-2]))

    send_near, qn, wn, rn = select_tok(z, tok_near, NEAR_ROWS, len(NEAR))
    xn = exchange(send_near, NEAR_ROWS)
    send_far, qf, wf, rf = select_tok(z, tok_far, FAR_ROWS, len(FAR))
    xf = exchange(send_far, FAR_ROWS)
    sn = exchange(select_cot(qn, wn, cot_near, NEAR_ROWS, len(NEAR)), NEAR_ROWS)
    sf = exchange(select_cot(qf, wf, cot_far, FAR_ROWS, len(FAR)), FAR_ROWS)

    tile_n, tile_f = 4 * NEAR_ROWS, 2 * FAR_ROWS
    gn, un = forward(xn, weights, tile_n)
    gf, uf = forward(xf, weights, tile_f)
    near_gate, far_gate = len(NEAR) * CAP, len(FAR) * CAP
    rows_n, dgn, dun, hn = backward(sn, gn, un, weights, tile_n, NEAR_ROWS, near_gate)
    rows_f, dgf, duf, hf = backward(sf, gf, uf, weights, tile_f, FAR_ROWS, far_gate)
    back_f = exchange(rows_f, FAR_ROWS)
    back_n = exchange(rows_n, NEAR_ROWS)

    part = weight_grad((xn, sn, dgn, dun, after(hn, back_f)), (xf, sf, dgf, duf, hf))
    summed = lax.psum_scatter(part, "section", scatter_dimension=2, tiled=True)
    weight_grads = summed.astype(F32) / lax.axis_size("section")

    far_sizes = [ROWS] * 4 + [HALF, HALF + META]
    far_parts = combine(z, qf, wf, rf, back_f, far_sizes, FAR_ROWS, len(FAR), far_gate)
    near_parts = combine(z, qn, wn, rn, back_n, [ROWS] * 3, NEAR_ROWS, len(NEAR), near_gate)
    total = ring_scatter(near_parts, far_parts)
    token_grads = total[:TOK].astype(BF)[None]
    gate_grads = total[TOK:, :TOK].T.astype(BF)[None]
    return token_grads, gate_grads, weight_grads


def solution(mesh):
    placed = (
        P("section", "expert", None),
        P("section", "expert", None),
        P("section", "expert", None),
        P("section", "expert", None),
        P(None, "expert", None, None),
    )
    return jax.shard_map(
        per_device,
        mesh=mesh,
        in_specs=placed,
        out_specs=(
            P("section", "expert", None),
            P("section", "expert", None),
            P(None, "expert", "section", None),
        ),
        check_vma=False,
    )
```

time: 642 us -> 346 us (0.54)
  the two profiles are of different devices: /device:TPU:8 before, /device:TPU:98 now
where the time goes in v1:
time: 346 us; the launch traced here: 345 us
  waiting for transfers between devices  153 us (44%)
  Pallas kernels  83.4 us (24%)
  starting transfers between devices  78.3 us (23%)
  between operations  14.3 us (4%)
  local copies, waits for them, and re-layouts  10.4 us (3%)
  other arithmetic  5.97 us (2%)
    all_to_all x6, waiting for transfers between devices, exchange(): lax.all_to_all(sent, ('section', 'expert'), 0, 0, axis_index_groups=plane...  48.5 us
    ppermute x6, waiting for transfers between devices, ring_gather(): down = lax.ppermute(down, 'expert', fw)  41.4 us
    all_to_all x6, starting transfers between devices, exchange(): lax.all_to_all(sent, ('section', 'expert'), 0, 0, axis_index_groups=plane...  39.4 us
    ppermute x6, waiting for transfers between devices, ring_gather(): up = lax.ppermute(up, 'expert', bw)  23.6 us
    pallas_call x2, Pallas kernels, backward(): pl.pallas_call(functools.partial(backward_body, per_dest, gate_row), grid...  20.7 us
    ppermute x6, starting transfers between devices, ring_gather(): down = lax.ppermute(down, 'expert', fw)  20.5 us
    pallas_call x1, Pallas kernels, weight_grad(): pl.pallas_call(weight_grad_body, grid=(D // tile,), in_specs=specs, out_s...  14.1 us
    pallas_call x2, Pallas kernels, forward(): pl.pallas_call(forward_body, grid=(rows // tile,), in_specs=[pl.BlockSpec...  12.4 us
  transfers between devices with their start and end apart: 31, of which 19 were waited for; matrix products, arithmetic and copies ran while one was open for 1% of the time, Pallas kernels for 18%

profile of v1, /device:TPU:98, one launch (start us, length us, event | category | flops | bytes accessed | tf_op | source)
XLA Modules:
  0.0 345.0 jit_solution(6226362521847429407)
XLA Ops:
  13.5 12.2 %collective-permute-done.refs_1_ = bf16[136,2048]{1,0:T(8,128)(2,1)S(1)} collective-permute-done((bf16[136,2048]{1,0:T(8,128)(2,1)}, bf16[136,2048]{1,0:T(8,128)(2,1)S(1)}, u32[]{:S(2)}, u32[]{:S(2)}) %collective-permute-start) | collective-permute-done | bytes 557088 | tf_op jit(solution)/shard_map/ppermute | solution.py:399
  29.8 4.7 %select_tokens.2 = (bf16[448,2048]{1,0:T(8,128)(2,1)}, s32[8,384]{1,0:T(8,128)}, f32[8,384]{1,0:T(8,128)}, f32[8,384]{1,0:T(8,128)}) custom-call(s32[1]{0:T(128)} %bitcast.z_ref, bf16[136,2048]{1,0:T(8,128)(2,1)} %pack_rows.1.refs_0_, bf16[136,2048]{1,0:T(8,128)(2,1)} %copy-done.19, bf16[136,2048]{1,0:T(8,128)(2,1)} %copy-done.21), custom_call_target="tpu_custom_call" | custom-call | flops 704643072 | bytes 3407872 | tf_op jit(solution)/shard_map/select_tokens/pallas_call | solution.py:152
  34.6 7.4 %all-to-all-start.1 = ((bf16[8,56,2048]{2,1,0:T(8,128)(2,1)}), bf16[8,56,2048]{2,1,0:T(8,128)(2,1)S(1)}, u32[]{:S(2)}, u32[]{:S(2)}) async-start(bf16[8,56,2048]{2,1,0:T(8,128)(2,1)} %bitcast.38), calls=%async_computation.1 | async-start | bytes 3670016 | tf_op jit(solution)/shard_map/all_to_all | solution.py:66
  45.2 10.6 %collective-permute-done.2.refs_1_ = bf16[136,2048]{1,0:T(8,128)(2,1)S(1)} collective-permute-done((bf16[136,2048]{1,0:T(8,128)(2,1)S(1)}, bf16[136,2048]{1,0:T(8,128)(2,1)S(1)}, u32[]{:S(2)}, u32[]{:S(2)}) %collective-permute-start.2) | collective-permute-done | bytes 557088 | tf_op jit(solution)/shard_map/ppermute | solution.py:400
  59.1 9.7 %collective-permute-done.3.refs_3_ = bf16[136,2048]{1,0:T(8,128)(2,1)S(1)} collective-permute-done((bf16[136,2048]{1,0:T(8,128)(2,1)S(1)}, bf16[136,2048]{1,0:T(8,128)(2,1)S(1)}, u32[]{:S(2)}, u32[]{:S(2)}) %collective-permute-start.3) | collective-permute-done | bytes 557088 | tf_op jit(solution)/shard_map/ppermute | solution.py:400
  72.2 3.9 %collective-permute-done.7.refs_4_ = bf16[64,2048]{1,0:T(8,128)(2,1)S(1)} collective-permute-done((bf16[64,2048]{1,0:T(8,128)(2,1)S(1)}, bf16[64,2048]{1,0:T(8,128)(2,1)S(1)}, u32[]{:S(2)}, u32[]{:S(2)}) %collective-permute-start.7) | collective-permute-done | bytes 262176 | tf_op jit(solution)/shard_map/ppermute | solution.py:402
  77.5 6.5 %select_tokens.3 = (bf16[768,2048]{1,0:T(8,128)(2,1)}, s32[8,640]{1,0:T(8,128)}, f32[8,640]{1,0:T(8,128)}, f32[8,640]{1,0:T(8,128)}) custom-call(s32[1]{0:T(128)} %bitcast.z_ref, bf16[136,2048]{1,0:T(8,128)(2,1)} %copy-done.18, bf16[136,2048]{1,0:T(8,128)(2,1)} %copy-done.17, bf16[136,2048]{1,0:T(8,128)(2,1)} %copy-done.16, bf16[136,2048]{1,0:T(8,128)(2,1)} %copy-done.13, ...), custom_call_target="tpu_custom_call" | custom-call | flops 2013265920 | bytes 5767168 | tf_op jit(solution)/shard_map/select_tokens/pallas_call | solution.py:152
  85.3 6.9 %all-to-all-start.4 = ((bf16[8,96,2048]{2,1,0:T(8,128)(2,1)}), bf16[8,96,2048]{2,1,0:T(8,128)(2,1)S(1)}, u32[]{:S(2)}, u32[]{:S(2)}) async-start(bf16[8,96,2048]{2,1,0:T(8,128)(2,1)} %bitcast.34), calls=%async_computation.4 | async-start | bytes 6291456 | tf_op jit(solution)/shard_map/all_to_all | solution.py:66
  95.9 9.2 %collective-permute-done.8.refs_1_ = bf16[128,2048]{1,0:T(8,128)(2,1)S(1)} collective-permute-done((bf16[128,2048]{1,0:T(8,128)(2,1)}, bf16[128,2048]{1,0:T(8,128)(2,1)S(1)}, u32[]{:S(2)}, u32[]{:S(2)}) %collective-permute-start.8) | collective-permute-done | bytes 524320 | tf_op jit(solution)/shard_map/ppermute | solution.py:399
  109.5 10.5 %collective-permute-done.10.refs_0_ = bf16[128,2048]{1,0:T(8,128)(2,1)S(1)} collective-permute-done((bf16[128,2048]{1,0:T(8,128)(2,1)S(1)}, bf16[128,2048]{1,0:T(8,128)(2,1)S(1)}, u32[]{:S(2)}, u32[]{:S(2)}) %collective-permute-start.10) | collective-permute-done | bytes 524320 | tf_op jit(solution)/shard_map/ppermute | solution.py:399
  123.7 9.5 %collective-permute-done.12.refs_2_ = bf16[128,2048]{1,0:T(8,128)(2,1)S(1)} collective-permute-done((bf16[128,2048]{1,0:T(8,128)(2,1)S(1)}, bf16[128,2048]{1,0:T(8,128)(2,1)S(1)}, u32[]{:S(2)}, u32[]{:S(2)}) %collective-permute-start.12) | collective-permute-done | bytes 524320 | tf_op jit(solution)/shard_map/ppermute | solution.py:399
  140.9 3.8 %collective-permute-done.15.refs_5_ = bf16[64,2048]{1,0:T(8,128)(2,1)S(1)} collective-permute-done((bf16[64,2048]{1,0:T(8,128)(2,1)S(1)}, bf16[64,2048]{1,0:T(8,128)(2,1)S(1)}, u32[]{:S(2)}, u32[]{:S(2)}) %collective-permute-start.15) | collective-permute-done | bytes 262176 | tf_op jit(solution)/shard_map/ppermute | solution.py:403
  145.4 6.0 %select_cotangents.3 = bf16[768,2048]{1,0:T(8,128)(2,1)} custom-call(s32[8,640]{1,0:T(8,128)} %get-tuple-element.44.q_ref, f32[8,640]{1,0:T(8,128)} %get-tuple-element.45.w_ref, bf16[128,2048]{1,0:T(8,128)(2,1)} %copy-done.23, bf16[128,2048]{1,0:T(8,128)(2,1)} %copy-done.24, bf16[128,2048]{1,0:T(8,128)(2,1)} %copy-done.14, bf16[128,2048]{1,0:T(8,128)(2,1)} %copy-done.15, ...), custom_call_target="tpu_custom_call" | custom-call | flops 2013265920 | bytes 5767168 | tf_op jit(solution)/shard_map/select_cotangents/pallas_call | solution.py:193
  153.2 6.3 %all-to-all-start.3 = ((bf16[8,96,2048]{2,1,0:T(8,128)(2,1)}), bf16[8,96,2048]{2,1,0:T(8,128)(2,1)S(1)}, u32[]{:S(2)}, u32[]{:S(2)}) async-start(bf16[8,96,2048]{2,1,0:T(8,128)(2,1)} %bitcast.37), calls=%async_computation.3 | async-start | bytes 6291456 | tf_op jit(solution)/shard_map/all_to_all | solution.py:66
  159.5 4.5 %select_cotangents.2 = bf16[448,2048]{1,0:T(8,128)(2,1)} custom-call(s32[8,384]{1,0:T(8,128)} %get-tuple-element.34.q_ref, f32[8,384]{1,0:T(8,128)} %get-tuple-element.35.w_ref, bf16[128,2048]{1,0:T(8,128)(2,1)} %bitcast.43, bf16[128,2048]{1,0:T(8,128)(2,1)} %copy-done.11, bf16[128,2048]{1,0:T(8,128)(2,1)} %copy-done.12), custom_call_target="tpu_custom_call" | custom-call | flops 704643072 | bytes 3407872 | tf_op jit(solution)/shard_map/select_cotangents/pallas_call | solution.py:193
  164.0 27.7 %all-to-all-done.3 = bf16[8,96,2048]{2,1,0:T(8,128)(2,1)S(1)} async-done(((bf16[8,96,2048]{2,1,0:T(8,128)(2,1)}), bf16[8,96,2048]{2,1,0:T(8,128)(2,1)S(1)}, u32[]{:S(2)}, u32[]{:S(2)}) %all-to-all-start.3) | async-done | bytes 3145760 | tf_op jit(solution)/shard_map/all_to_all | solution.py:66
  193.4 5.2 %all-to-all-start = ((bf16[8,56,2048]{2,1,0:T(8,128)(2,1)}), bf16[8,56,2048]{2,1,0:T(8,128)(2,1)}, u32[]{:S(2)}, u32[]{:S(2)}) async-start(bf16[8,56,2048]{2,1,0:T(8,128)(2,1)} %bitcast.31), calls=%async_computation | async-start | bytes 3670016 | tf_op jit(solution)/shard_map/all_to_all | solution.py:66
  198.6 7.2 %expert_forward.3 = (f32[768,384]{1,0:T(8,128)}, f32[768,384]{1,0:T(8,128)}) custom-call(bf16[768,2048]{1,0:T(8,128)(2,1)} %bitcast.29, bf16[3,1,2048,384]{3,2,1,0:T(8,128)(2,1)} %wd_ref.3, bf16[3,1,2048,384]{3,2,1,0:T(8,128)(2,1)} %wd_ref.3), custom_call_target="tpu_custom_call" | custom-call | flops 2415919104 | bytes 6291456 | tf_op jit(solution)/shard_map/expert_forward/pallas_call | solution.py:220
  205.8 12.2 %expert_backward.3 = (bf16[768,2048]{1,0:T(8,128)(2,1)}, bf16[768,384]{1,0:T(8,128)(2,1)}, bf16[768,384]{1,0:T(8,128)(2,1)}, bf16[768,384]{1,0:T(8,128)(2,1)}) custom-call(bf16[768,2048]{1,0:T(8,128)(2,1)} %bitcast.27, f32[768,384]{1,0:T(8,128)} %get-tuple-element.48.g_ref, f32[768,384]{1,0:T(8,128)} %get-tuple-element.49.u_ref, ...), custom_call_target="tpu_custom_call" | custom-call | flops 3623878656 | bytes 11010048 | tf_op jit(solution)/shard_map/expert_backward/pallas_call | solution.py:267
  218.0 6.9 %all-to-all-start.5 = ((bf16[8,96,2048]{2,1,0:T(8,128)(2,1)}), bf16[8,96,2048]{2,1,0:T(8,128)(2,1)S(1)}, u32[]{:S(2)}, u32[]{:S(2)}) async-start(bf16[8,96,2048]{2,1,0:T(8,128)(2,1)} %bitcast.36), calls=%async_computation.5 | async-start | bytes 6291456 | tf_op jit(solution)/shard_map/all_to_all | solution.py:66
  225.0 5.2 %expert_forward.2 = (f32[448,384]{1,0:T(8,128)}, f32[448,384]{1,0:T(8,128)}) custom-call(bf16[448,2048]{1,0:T(8,128)(2,1)} %bitcast.32, bf16[3,1,2048,384]{3,2,1,0:T(8,128)(2,1)} %wd_ref.3, bf16[3,1,2048,384]{3,2,1,0:T(8,128)(2,1)} %wd_ref.3), custom_call_target="tpu_custom_call" | custom-call | flops 1409286144 | bytes 4980736 | tf_op jit(solution)/shard_map/expert_forward/pallas_call | solution.py:220
  230.2 8.5 %expert_backward.2 = (bf16[448,2048]{1,0:T(8,128)(2,1)}, bf16[448,384]{1,0:T(8,128)(2,1)}, bf16[448,384]{1,0:T(8,128)(2,1)}, bf16[448,384]{1,0:T(8,128)(2,1)}) custom-call(bf16[448,2048]{1,0:T(8,128)(2,1)} %bitcast.8.sc_ref.sn, f32[448,384]{1,0:T(8,128)} %get-tuple-element.39.g_ref, f32[448,384]{1,0:T(8,128)} %get-tuple-element.40.u_ref, ...), custom_call_target="tpu_custom_call" | custom-call | flops 2113929216 | bytes 8388608 | tf_op jit(solution)/shard_map/expert_backward/pallas_call | solution.py:267
  238.6 20.7 %all-to-all-done.5 = bf16[8,96,2048]{2,1,0:T(8,128)(2,1)S(1)} async-done(((bf16[8,96,2048]{2,1,0:T(8,128)(2,1)}), bf16[8,96,2048]{2,1,0:T(8,128)(2,1)S(1)}, u32[]{:S(2)}, u32[]{:S(2)}) %all-to-all-start.5) | async-done | bytes 3145760 | tf_op jit(solution)/shard_map/all_to_all | solution.py:66
  259.4 14.1 %weight_grads.1 = bf16[3,1,2048,384]{3,2,1,0:T(8,128)(2,1)} custom-call(bf16[448,2048]{1,0:T(8,128)(2,1)} %bitcast.33, bf16[768,2048]{1,0:T(8,128)(2,1)} %bitcast.30, bf16[448,2048]{1,0:T(8,128)(2,1)} %bitcast.8.sc_ref.sn, bf16[768,2048]{1,0:T(8,128)(2,1)} %bitcast.28, bf16[448,384]{1,0:T(8,128)(2,1)} %get-tuple-element.58.dgn, ...), custom_call_target="tpu_custom_call" | custom-call | flops 5737807872 | bytes 14680064 | tf_op jit(solution)/shard_map/weight_grads/pallas_call | solution.py:304
  273.5 6.3 %combine_rows.3 = (bf16[136,2048]{1,0:T(8,128)(2,1)}, bf16[136,2048]{1,0:T(8,128)(2,1)}, bf16[136,2048]{1,0:T(8,128)(2,1)}, bf16[136,2048]{1,0:T(8,128)(2,1)}, b...) custom-call(s32[1]{0:T(128)} %bitcast.z_ref, s32[8,640]{1,0:T(8,128)} %get-tuple-element.44.q_ref, ...), custom_call_target="tpu_custom_call" | custom-call | flops 2013265920 | bytes 5767168 | tf_op jit(solution)/shard_map/combine_rows/pallas_call | solution.py:375
  280.8 6.6 %all-to-all-start.2 = ((bf16[8,56,2048]{2,1,0:T(8,128)(2,1)}), bf16[8,56,2048]{2,1,0:T(8,128)(2,1)S(1)}, u32[]{:S(2)}, u32[]{:S(2)}) async-start(bf16[8,56,2048]{2,1,0:T(8,128)(2,1)} %bitcast.11), calls=%async_computation.2 | async-start | bytes 3670016 | tf_op jit(solution)/shard_map/all_to_all | solution.py:66
  290.8 5.4 %collective-permute-done.20 = bf16[72,2048]{1,0:T(8,128)(2,1)S(1)} collective-permute-done((bf16[72,2048]{1,0:T(8,128)(2,1)S(1)}, bf16[72,2048]{1,0:T(8,128)(2,1)S(1)}, u32[]{:S(2)}, u32[]{:S(2)}) %collective-permute-start.20) | collective-permute-done | bytes 294944 | tf_op jit(solution)/shard_map/ppermute | solution.py:417
  297.2 4.0 %collective-permute-done.17 = bf16[136,2048]{1,0:T(8,128)(2,1)S(1)} collective-permute-done((bf16[136,2048]{1,0:T(8,128)(2,1)S(1)}, bf16[136,2048]{1,0:T(8,128)(2,1)S(1)}, u32[]{:S(2)}, u32[]{:S(2)}) %collective-permute-start.17) | collective-permute-done | bytes 557088 | tf_op jit(solution)/shard_map/ppermute | solution.py:421
  303.6 5.3 %collective-permute-done.21 = bf16[136,2048]{1,0:T(8,128)(2,1)S(1)} collective-permute-done((bf16[136,2048]{1,0:T(8,128)(2,1)S(1)}, bf16[136,2048]{1,0:T(8,128)(2,1)S(1)}, u32[]{:S(2)}, u32[]{:S(2)}) %collective-permute-start.21) | collective-permute-done | bytes 557088 | tf_op jit(solution)/shard_map/ppermute | solution.py:422
  311.2 5.0 %combine_rows.2 = (bf16[136,2048]{1,0:T(8,128)(2,1)}, bf16[136,2048]{1,0:T(8,128)(2,1)}, bf16[136,2048]{1,0:T(8,128)(2,1)}) custom-call(s32[1]{0:T(128)} %bitcast.z_ref, s32[8,384]{1,0:T(8,128)} %get-tuple-element.34.q_ref, f32[8,384]{1,0:T(8,128)} %get-tuple-element.35.w_ref, f32[8,384]{1,0:T(8,128)} %get-tuple-element.36.r_ref, bf16[448,2048]{1,0:T(8,128)(2,1)} %bitcast.39), custom_call_target="tpu_custom_call" | custom-call | flops 704643072 | bytes 3407872 | tf_op jit(solution)/shard_map/combine_rows/pallas_call | solution.py:375
  322.9 4.4 %collective-permute-done.19 = bf16[136,2048]{1,0:T(8,128)(2,1)S(1)} collective-permute-done((bf16[136,2048]{1,0:T(8,128)(2,1)S(1)}, bf16[136,2048]{1,0:T(8,128)(2,1)S(1)}, u32[]{:S(2)}, u32[]{:S(2)}) %collective-permute-start.19) | collective-permute-done | bytes 557088 | tf_op jit(solution)/shard_map/ppermute | solution.py:423
  327.2 6.4 %collective-permute-done.23 = bf16[136,2048]{1,0:T(8,128)(2,1)S(1)} collective-permute-done((bf16[136,2048]{1,0:T(8,128)(2,1)S(1)}, bf16[136,2048]{1,0:T(8,128)(2,1)S(1)}, u32[]{:S(2)}, u32[]{:S(2)}) %collective-permute-start.23) | collective-permute-done | bytes 557088 | tf_op jit(solution)/shard_map/ppermute | solution.py:424
  (117 shorter events, 67.8 us)
Async XLA Ops:
  10.4 15.3 %collective-permute-start = (bf16[136,2048]{1,0:T(8,128)(2,1)}, bf16[136,2048]{1,0:T(8,128)(2,1)S(1)}, u32[]{:S(2)}, u32[]{:S(2)}) collective-permute-start(bf16[136,2048]{1,0:T(8,128)(2,1)} %pack_rows.1.refs_0_), channel_id=1, source_target_pairs={{0,8},{1,9},{2,10},{3,11},{4,12},{5,13},{6,14},{7,15},{8,16},{9,17... | collective-permute-start | bytes 1671176 | tf_op jit(solution)/shard_map/ppermute | solution.py:399
  13.5 15.5 %collective-permute-start.1 = (bf16[136,2048]{1,0:T(8,128)(2,1)}, bf16[136,2048]{1,0:T(8,128)(2,1)S(1)}, u32[]{:S(2)}, u32[]{:S(2)}) collective-permute-start(bf16[136,2048]{1,0:T(8,128)(2,1)} %pack_rows.1.refs_0_), channel_id=1, source_target_pairs={{0,56},{1,57},{2,58},{3,59},{4,60},{5,61},{6,62},{7,63},{8,0},{9,1... | collective-permute-start | bytes 1671176 | tf_op jit(solution)/shard_map/ppermute | solution.py:400
  34.6 49.5 %all-to-all-start.1 = ((bf16[8,56,2048]{2,1,0:T(8,128)(2,1)}), bf16[8,56,2048]{2,1,0:T(8,128)(2,1)S(1)}, u32[]{:S(2)}, u32[]{:S(2)}) async-start(bf16[8,56,2048]{2,1,0:T(8,128)(2,1)} %bitcast.38), calls=%async_computation.1 | async-start | bytes 3670016 | tf_op jit(solution)/shard_map/all_to_all | solution.py:66
  42.0 13.8 %collective-permute-start.2 = (bf16[136,2048]{1,0:T(8,128)(2,1)S(1)}, bf16[136,2048]{1,0:T(8,128)(2,1)S(1)}, u32[]{:S(2)}, u32[]{:S(2)}) collective-permute-start(bf16[136,2048]{1,0:T(8,128)(2,1)S(1)} %copy-done.22), channel_id=1, source_target_pairs={{0,56},{1,57},{2,58},{3,59},{4,60},{5,61},{6,62},{7,63},{8,0},{9,1... | collective-permute-start | bytes 1671176 | tf_op jit(solution)/shard_map/ppermute | solution.py:400
  42.0 13.8 %collective-permute-start.5 = (bf16[136,2048]{1,0:T(8,128)(2,1)S(1)}, bf16[136,2048]{1,0:T(8,128)(2,1)S(1)}, u32[]{:S(2)}, u32[]{:S(2)}) collective-permute-start(bf16[136,2048]{1,0:T(8,128)(2,1)S(1)} %copy-done.20), channel_id=1, source_target_pairs={{0,8},{1,9},{2,10},{3,11},{4,12},{5,13},{6,14},{7,15},{8,16},{9,17... | collective-permute-start | bytes 1671176 | tf_op jit(solution)/shard_map/ppermute | solution.py:399
  55.8 12.9 %collective-permute-start.3 = (bf16[136,2048]{1,0:T(8,128)(2,1)S(1)}, bf16[136,2048]{1,0:T(8,128)(2,1)S(1)}, u32[]{:S(2)}, u32[]{:S(2)}) collective-permute-start(bf16[136,2048]{1,0:T(8,128)(2,1)S(1)} %collective-permute-done.2.refs_1_), channel_id=1, source_target_pairs={{0,56},{1,57},{2,58},{3,59},{4,60},{5,61},{6,62},{7,63},{8,0},{9,1... | collective-permute-start | bytes 1671176 | tf_op jit(solution)/shard_map/ppermute | solution.py:400
  55.9 13.0 %collective-permute-start.6 = (bf16[136,2048]{1,0:T(8,128)(2,1)S(1)}, bf16[136,2048]{1,0:T(8,128)(2,1)S(1)}, u32[]{:S(2)}, u32[]{:S(2)}) collective-permute-start(bf16[136,2048]{1,0:T(8,128)(2,1)S(1)} %collective-permute-done.5.refs_0_), channel_id=1, source_target_pairs={{0,8},{1,9},{2,10},{3,11},{4,12},{5,13},{6,14},{7,15},{8,16},{9,17... | collective-permute-start | bytes 1671176 | tf_op jit(solution)/shard_map/ppermute | solution.py:399
  68.8 8.0 %collective-permute-start.4 = (bf16[72,2048]{1,0:T(8,128)(2,1)S(1)}, bf16[72,2048]{1,0:T(8,128)(2,1)S(1)}, u32[]{:S(2)}, u32[]{:S(2)}) collective-permute-start(bf16[72,2048]{1,0:T(8,128)(2,1)S(1)} %slice.26), channel_id=1, source_target_pairs={{0,56},{1,57},{2,58},{3,59},{4,60},{5,61},{6,62},{7,63},{8,0},{9,1... | collective-permute-start | bytes 884744 | tf_op jit(solution)/shard_map/ppermute | solution.py:403
  68.9 7.2 %collective-permute-start.7 = (bf16[64,2048]{1,0:T(8,128)(2,1)S(1)}, bf16[64,2048]{1,0:T(8,128)(2,1)S(1)}, u32[]{:S(2)}, u32[]{:S(2)}) collective-permute-start(bf16[64,2048]{1,0:T(8,128)(2,1)S(1)} %slice.27), channel_id=1, source_target_pairs={{0,8},{1,9},{2,10},{3,11},{4,12},{5,13},{6,14},{7,15},{8,16},{9,17... | collective-permute-start | bytes 786440 | tf_op jit(solution)/shard_map/ppermute | solution.py:402
  85.3 66.1 %all-to-all-start.4 = ((bf16[8,96,2048]{2,1,0:T(8,128)(2,1)}), bf16[8,96,2048]{2,1,0:T(8,128)(2,1)S(1)}, u32[]{:S(2)}, u32[]{:S(2)}) async-start(bf16[8,96,2048]{2,1,0:T(8,128)(2,1)} %bitcast.34), calls=%async_computation.4 | async-start | bytes 6291456 | tf_op jit(solution)/shard_map/all_to_all | solution.py:66
  92.2 12.9 %collective-permute-start.8 = (bf16[128,2048]{1,0:T(8,128)(2,1)}, bf16[128,2048]{1,0:T(8,128)(2,1)S(1)}, u32[]{:S(2)}, u32[]{:S(2)}) collective-permute-start(bf16[128,2048]{1,0:T(8,128)(2,1)} %bitcast.41), channel_id=1, source_target_pairs={{0,8},{1,9},{2,10},{3,11},{4,12},{5,13},{6,14},{7,15},{8,16},{9,17... | collective-permute-start | bytes 1572872 | tf_op jit(solution)/shard_map/ppermute | solution.py:399
  95.9 13.6 %collective-permute-start.9 = (bf16[128,2048]{1,0:T(8,128)(2,1)}, bf16[128,2048]{1,0:T(8,128)(2,1)S(1)}, u32[]{:S(2)}, u32[]{:S(2)}) collective-permute-start(bf16[128,2048]{1,0:T(8,128)(2,1)} %bitcast.42), channel_id=1, source_target_pairs={{0,56},{1,57},{2,58},{3,59},{4,60},{5,61},{6,62},{7,63},{8,0},{9,1... | collective-permute-start | bytes 1572872 | tf_op jit(solution)/shard_map/ppermute | solution.py:400
  105.9 14.1 %collective-permute-start.10 = (bf16[128,2048]{1,0:T(8,128)(2,1)S(1)}, bf16[128,2048]{1,0:T(8,128)(2,1)S(1)}, u32[]{:S(2)}, u32[]{:S(2)}) collective-permute-start(bf16[128,2048]{1,0:T(8,128)(2,1)S(1)} %collective-permute-done.8.refs_1_), channel_id=1, source_target_pairs={{0,8},{1,9},{2,10},{3,11},{4,12},{5,13},{6,14},{7,15},{8,16},{9,17... | collective-permute-start | bytes 1572872 | tf_op jit(solution)/shard_map/ppermute | solution.py:399
  109.5 14.2 %collective-permute-start.11 = (bf16[128,2048]{1,0:T(8,128)(2,1)S(1)}, bf16[128,2048]{1,0:T(8,128)(2,1)S(1)}, u32[]{:S(2)}, u32[]{:S(2)}) collective-permute-start(bf16[128,2048]{1,0:T(8,128)(2,1)S(1)} %collective-permute-done.9.refs_2_), channel_id=1, source_target_pairs={{0,56},{1,57},{2,58},{3,59},{4,60},{5,61},{6,62},{7,63},{8,0},{9,1... | collective-permute-start | bytes 1572872 | tf_op jit(solution)/shard_map/ppermute | solution.py:400
  120.0 24.7 %copy-start.23 = (bf16[128,2048]{1,0:T(8,128)(2,1)}, bf16[128,2048]{1,0:T(8,128)(2,1)S(1)}, u32[]{:S(2)}) copy-start(bf16[128,2048]{1,0:T(8,128)(2,1)S(1)} %collective-permute-done.10.refs_0_) | copy-start | bytes 1572868
  120.0 13.2 %collective-permute-start.12 = (bf16[128,2048]{1,0:T(8,128)(2,1)S(1)}, bf16[128,2048]{1,0:T(8,128)(2,1)S(1)}, u32[]{:S(2)}, u32[]{:S(2)}) collective-permute-start(bf16[128,2048]{1,0:T(8,128)(2,1)S(1)} %collective-permute-done.10.refs_0_), channel_id=1, source_target_pairs={{0,8},{1,9},{2,10},{3,11},{4,12},{5,13},{6,14},{7,15},{8,16},{9,17... | collective-permute-start | bytes 1572872 | tf_op jit(solution)/shard_map/ppermute | solution.py:399
  123.7 13.3 %collective-permute-start.13 = (bf16[128,2048]{1,0:T(8,128)(2,1)S(1)}, bf16[128,2048]{1,0:T(8,128)(2,1)S(1)}, u32[]{:S(2)}, u32[]{:S(2)}) collective-permute-start(bf16[128,2048]{1,0:T(8,128)(2,1)S(1)} %collective-permute-done.11.refs_1_), channel_id=1, source_target_pairs={{0,56},{1,57},{2,58},{3,59},{4,60},{5,61},{6,62},{7,63},{8,0},{9,1... | collective-permute-start | bytes 1572872 | tf_op jit(solution)/shard_map/ppermute | solution.py:400
  133.3 7.7 %collective-permute-start.14 = (bf16[64,2048]{1,0:T(8,128)(2,1)S(1)}, bf16[64,2048]{1,0:T(8,128)(2,1)S(1)}, u32[]{:S(2)}, u32[]{:S(2)}) collective-permute-start(bf16[64,2048]{1,0:T(8,128)(2,1)S(1)} %slice.28), channel_id=1, source_target_pairs={{0,8},{1,9},{2,10},{3,11},{4,12},{5,13},{6,14},{7,15},{8,16},{9,17... | collective-permute-start | bytes 786440 | tf_op jit(solution)/shard_map/ppermute | solution.py:402
  137.1 7.7 %collective-permute-start.15 = (bf16[64,2048]{1,0:T(8,128)(2,1)S(1)}, bf16[64,2048]{1,0:T(8,128)(2,1)S(1)}, u32[]{:S(2)}, u32[]{:S(2)}) collective-permute-start(bf16[64,2048]{1,0:T(8,128)(2,1)S(1)} %slice.29), channel_id=1, source_target_pairs={{0,56},{1,57},{2,58},{3,59},{4,60},{5,61},{6,62},{7,63},{8,0},{9,1... | collective-permute-start | bytes 786440 | tf_op jit(solution)/shard_map/ppermute | solution.py:403
  153.2 38.6 %all-to-all-start.3 = ((bf16[8,96,2048]{2,1,0:T(8,128)(2,1)}), bf16[8,96,2048]{2,1,0:T(8,128)(2,1)S(1)}, u32[]{:S(2)}, u32[]{:S(2)}) async-start(bf16[8,96,2048]{2,1,0:T(8,128)(2,1)} %bitcast.37), calls=%async_computation.3 | async-start | bytes 6291456 | tf_op jit(solution)/shard_map/all_to_all | solution.py:66
  193.4 24.7 %all-to-all-start = ((bf16[8,56,2048]{2,1,0:T(8,128)(2,1)}), bf16[8,56,2048]{2,1,0:T(8,128)(2,1)}, u32[]{:S(2)}, u32[]{:S(2)}) async-start(bf16[8,56,2048]{2,1,0:T(8,128)(2,1)} %bitcast.31), calls=%async_computation | async-start | bytes 3670016 | tf_op jit(solution)/shard_map/all_to_all | solution.py:66
  218.0 41.3 %all-to-all-start.5 = ((bf16[8,96,2048]{2,1,0:T(8,128)(2,1)}), bf16[8,96,2048]{2,1,0:T(8,128)(2,1)S(1)}, u32[]{:S(2)}, u32[]{:S(2)}) async-start(bf16[8,96,2048]{2,1,0:T(8,128)(2,1)} %bitcast.36), calls=%async_computation.5 | async-start | bytes 6291456 | tf_op jit(solution)/shard_map/all_to_all | solution.py:66
  225.0 110.3 %reduce-scatter.2.cloned.1.call-start = ((), (), s32[]{:S(2)}) async-start(), calls=%async_computation.7 | async-start | bytes 5898240 | tf_op jit(solution)/shard_map/reduce_scatter | solution.py:451
  279.8 8.9 %collective-permute-start.16 = (bf16[64,2048]{1,0:T(8,128)(2,1)}, bf16[64,2048]{1,0:T(8,128)(2,1)S(1)}, u32[]{:S(2)}, u32[]{:S(2)}) collective-permute-start(bf16[64,2048]{1,0:T(8,128)(2,1)} %get-tuple-element.53), channel_id=1, source_target_pairs={{0,8},{1,9},{2,10},{3,11},{4,12},{5,13},{6,14},{7,15},{8,16},{9,17... | collective-permute-start | bytes 786440 | tf_op jit(solution)/shard_map/ppermute | solution.py:416
  280.8 29.2 %all-to-all-start.2 = ((bf16[8,56,2048]{2,1,0:T(8,128)(2,1)}), bf16[8,56,2048]{2,1,0:T(8,128)(2,1)S(1)}, u32[]{:S(2)}, u32[]{:S(2)}) async-start(bf16[8,56,2048]{2,1,0:T(8,128)(2,1)} %bitcast.11), calls=%async_computation.2 | async-start | bytes 3670016 | tf_op jit(solution)/shard_map/all_to_all | solution.py:66
  287.4 8.8 %collective-permute-start.20 = (bf16[72,2048]{1,0:T(8,128)(2,1)S(1)}, bf16[72,2048]{1,0:T(8,128)(2,1)S(1)}, u32[]{:S(2)}, u32[]{:S(2)}) collective-permute-start(bf16[72,2048]{1,0:T(8,128)(2,1)S(1)} %copy-done.25), channel_id=1, source_target_pairs={{0,56},{1,57},{2,58},{3,59},{4,60},{5,61},{6,62},{7,63},{8,0},{9,1... | collective-permute-start | bytes 884744 | tf_op jit(solution)/shard_map/ppermute | solution.py:417
  288.7 12.5 %collective-permute-start.17 = (bf16[136,2048]{1,0:T(8,128)(2,1)S(1)}, bf16[136,2048]{1,0:T(8,128)(2,1)S(1)}, u32[]{:S(2)}, u32[]{:S(2)}) collective-permute-start(bf16[136,2048]{1,0:T(8,128)(2,1)S(1)} %add_convert_fusion.6), channel_id=1, source_target_pairs={{0,8},{1,9},{2,10},{3,11},{4,12},{5,13},{6,14},{7,15},{8,16},{9,17... | collective-permute-start | bytes 1671176 | tf_op jit(solution)/shard_map/ppermute | solution.py:421
  296.3 12.7 %collective-permute-start.21 = (bf16[136,2048]{1,0:T(8,128)(2,1)S(1)}, bf16[136,2048]{1,0:T(8,128)(2,1)S(1)}, u32[]{:S(2)}, u32[]{:S(2)}) collective-permute-start(bf16[136,2048]{1,0:T(8,128)(2,1)S(1)} %add_convert_fusion.3), channel_id=1, source_target_pairs={{0,56},{1,57},{2,58},{3,59},{4,60},{5,61},{6,62},{7,63},{8,0},{9,1... | collective-permute-start | bytes 1671176 | tf_op jit(solution)/shard_map/ppermute | solution.py:422
  301.4 14.7 %collective-permute-start.18 = (bf16[136,2048]{1,0:T(8,128)(2,1)S(1)}, bf16[136,2048]{1,0:T(8,128)(2,1)S(1)}, u32[]{:S(2)}, u32[]{:S(2)}) collective-permute-start(bf16[136,2048]{1,0:T(8,128)(2,1)S(1)} %add_convert_fusion.5), channel_id=1, source_target_pairs={{0,8},{1,9},{2,10},{3,11},{4,12},{5,13},{6,14},{7,15},{8,16},{9,17... | collective-permute-start | bytes 1671176 | tf_op jit(solution)/shard_map/ppermute | solution.py:421
  309.1 12.5 %collective-permute-start.22 = (bf16[136,2048]{1,0:T(8,128)(2,1)S(1)}, bf16[136,2048]{1,0:T(8,128)(2,1)}, u32[]{:S(2)}, u32[]{:S(2)}) collective-permute-start(bf16[136,2048]{1,0:T(8,128)(2,1)S(1)} %add_convert_fusion.2), channel_id=1, source_target_pairs={{0,56},{1,57},{2,58},{3,59},{4,60},{5,61},{6,62},{7,63},{8,0},{9,1... | collective-permute-start | bytes 1671176 | tf_op jit(solution)/shard_map/ppermute | solution.py:422
  317.4 9.8 %collective-permute-start.19 = (bf16[136,2048]{1,0:T(8,128)(2,1)S(1)}, bf16[136,2048]{1,0:T(8,128)(2,1)S(1)}, u32[]{:S(2)}, u32[]{:S(2)}) collective-permute-start(bf16[136,2048]{1,0:T(8,128)(2,1)S(1)} %add_convert_fusion.4), channel_id=1, source_target_pairs={{0,8},{1,9},{2,10},{3,11},{4,12},{5,13},{6,14},{7,15},{8,16},{9,17... | collective-permute-start | bytes 1671176 | tf_op jit(solution)/shard_map/ppermute | solution.py:423
  322.8 10.8 %collective-permute-start.23 = (bf16[136,2048]{1,0:T(8,128)(2,1)S(1)}, bf16[136,2048]{1,0:T(8,128)(2,1)S(1)}, u32[]{:S(2)}, u32[]{:S(2)}) collective-permute-start(bf16[136,2048]{1,0:T(8,128)(2,1)S(1)} %add_convert_fusion.1), channel_id=1, source_target_pairs={{0,56},{1,57},{2,58},{3,59},{4,60},{5,61},{6,62},{7,63},{8,0},{9,1... | collective-permute-start | bytes 1671176 | tf_op jit(solution)/shard_map/ppermute | solution.py:424
  (29 other events, 224.4 us)
Sparse Core Ops, SparseCore 0:
  273.6 48.9 reduce-scatter.1

commit v2 on v1

--- a/solution.py
+++ b/solution.py
@@ -21,10 +21,10 @@
 FAR = (-2, 2, -3, 3, 4)
 NEAR_ROWS = 56
 FAR_ROWS = 96
-COLS = 512
+COLS = 1024
 BF = jnp.bfloat16
 F32 = jnp.float32
-VMEM_LIMIT = 56 * 1024 * 1024
+VMEM_LIMIT = 32 * 1024 * 1024
 
 
 def params():
@@ -43,8 +43,8 @@
     return [(e, (e - PLANE) % (PLANES * PLANE)) for e in range(PLANES * PLANE)]
 
 
-def after(value, *done):
-    return lax.optimization_barrier((value, *done))[0]
+def ordered(*values):
+    return lax.optimization_barrier(values)
 
 
 def plane_groups():
@@ -71,24 +71,15 @@
 
 def pack_body(tok_ref, routes_ref, weight_ref, out_ref):
     out_ref[0:TOK, :] = tok_ref[...]
-    tail = jnp.concatenate(
-        [routes_ref[...].astype(F32), weight_ref[...].astype(F32), jnp.zeros((META, COLS - 256), F32)],
+    out_ref[TOK:ROWS, :] = jnp.concatenate(
+        [routes_ref[...].astype(F32), weight_ref[...].astype(F32), jnp.zeros((META, D - 2 * TOK), F32)],
         axis=1,
-    )
-    keep = jnp.where(pl.program_id(0) == 0, 1.0, 0.0)
-    out_ref[TOK:ROWS, :] = (tail * keep).astype(BF)
+    ).astype(BF)
 
 
 def pack(tok, routes_t, weight_t):
     return pl.pallas_call(
         pack_body,
-        grid=(D // COLS,),
-        in_specs=[
-            pl.BlockSpec((TOK, COLS), lambda i: (0, i)),
-            pl.BlockSpec((META, TOK), lambda i: (0, 0)),
-            pl.BlockSpec((META, TOK), lambda i: (0, 0)),
-        ],
-        out_specs=pl.BlockSpec((ROWS, COLS), lambda i: (0, i)),
         out_shape=jax.ShapeDtypeStruct((ROWS, D), BF),
         compiler_params=params(),
         cost_estimate=cost(0, 4 * ROWS * D),
@@ -204,113 +195,173 @@
     )(q, w, *blocks)
 
 
-def weight_spec(which):
-    return pl.BlockSpec((None, None, D, FF), lambda i: (which, 0, 0, 0))
-
-
-def forward_body(x_ref, wg_ref, wu_ref, g_ref, u_ref):
-    g_ref[...] = jnp.dot(x_ref[...], wg_ref[...], preferred_element_type=F32)
-    u_ref[...] = jnp.dot(x_ref[...], wu_ref[...], preferred_element_type=F32)
-
-
-def forward(x, weights, tile):
+def resident():
+    return pl.BlockSpec(memory_space=pltpu.VMEM)
+
+
+def join_body(g_ref, u_ref, d_ref, out_ref, down_ref):
+    out_ref[:, 0:FF] = g_ref[...]
+    out_ref[:, FF : 2 * FF] = u_ref[...]
+    down_ref[...] = d_ref[...]
+
+
+def join_weights(weights):
+    rows = D // 2
+
+    def part(which):
+        return pl.BlockSpec((None, None, rows, FF), lambda i: (which, 0, i, 0))
+
+    return pl.pallas_call(
+        join_body,
+        grid=(2,),
+        in_specs=[part(0), part(1), part(2)],
+        out_specs=[
+            pl.BlockSpec((rows, 2 * FF), lambda i: (i, 0)),
+            pl.BlockSpec((rows, FF), lambda i: (i, 0)),
+        ],
+        out_shape=[jax.ShapeDtypeStruct((D, 2 * FF), BF), jax.ShapeDtypeStruct((D, FF), BF)],
+        compiler_params=params(),
+        cost_estimate=cost(0, 12 * D * FF),
+        name="join_weights",
+    )(weights, weights, weights)
+
+
+def forward_body(x_ref, w_ref, p_ref):
+    p_ref[...] = jnp.dot(x_ref[...], w_ref[...], preferred_element_type=F32)
+
+
+def forward(x, joined, tile):
     rows = x.shape[0]
-    out = jax.ShapeDtypeStruct((rows, FF), F32)
-    spec = pl.BlockSpec((tile, FF), lambda i: (i, 0))
     return pl.pallas_call(
         forward_body,
         grid=(rows // tile,),
-        in_specs=[pl.BlockSpec((tile, D), lambda i: (i, 0)), weight_spec(0), weight_spec(1)],
-        out_specs=[spec, spec],
-        out_shape=[out, out],
+        in_specs=[pl.BlockSpec((tile, D), lambda i: (i, 0)), resident()],
+        out_specs=pl.BlockSpec((tile, 2 * FF), lambda i: (i, 0)),
+        out_shape=jax.ShapeDtypeStruct((rows, 2 * FF), F32),
         compiler_params=params(),
         cost_estimate=cost(4 * rows * D * FF, 2 * D * (rows + 2 * FF)),
         name="expert_forward",
-    )(x, weights, weights)
-
-
-def backward_body(per_dest, gate_row, sc_ref, g_ref, u_ref, wg_ref, wu_ref, wd_ref,
-                  rows_ref, dg_ref, du_ref, h_ref, total):
+    )(x, joined)
+
+
+def backward_body(per_dest, gate_row, sc_ref, p_ref, w_ref, wd_ref, rows_ref, d_ref, h_ref):
     tile = sc_ref.shape[0]
     back = jnp.dot(sc_ref[...], wd_ref[...], preferred_element_type=F32)
-    gate = g_ref[...]
-    up = u_ref[...]
+    gate = p_ref[:, 0:FF]
+    up = p_ref[:, FF : 2 * FF]
     sig = jax.nn.sigmoid(gate)
     silu = gate * sig
     hidden = (silu * up).astype(BF)
     d_gate = (back * up * sig * (1.0 + gate * (1.0 - sig))).astype(BF)
     d_up = (back * silu).astype(BF)
     h_ref[...] = hidden
-    dg_ref[...] = d_gate
-    du_ref[...] = d_up
+    d_ref[:, 0:FF] = d_gate
+    d_ref[:, FF : 2 * FF] = d_up
     by_ff = (((1,), (1,)), ((), ()))
-    total[...] = lax.dot_general(d_gate, wg_ref[...], by_ff, preferred_element_type=F32)
-    total[...] += lax.dot_general(d_up, wu_ref[...], by_ff, preferred_element_type=F32)
+    rows_ref[...] = lax.dot_general(d_ref[...], w_ref[...], by_ff, preferred_element_type=F32).astype(BF)
     product = hidden.astype(F32) * back
-    ones = jnp.ones((8, FF), F32)
-    pick = lax.broadcasted_iota(jnp.int32, (8, per_dest), 0) == gate_row % 8
+    high = product.astype(BF)
+    low = (product - high.astype(F32)).astype(BF)
+    ones = jnp.ones((16, FF), BF)
+    line = lax.broadcasted_iota(jnp.int32, (16, per_dest), 0)
     for d in range(tile // per_dest):
-        part = lax.dot_general(
-            ones, product[d * per_dest : (d + 1) * per_dest, :], by_ff,
-            preferred_element_type=F32, precision=lax.Precision.HIGHEST,
-        )
-        at = d * per_dest + gate_row // 8 * 8
-        total[at : at + 8, 0:per_dest] += jnp.where(pick, part, 0.0)
-    rows_ref[...] = total[...].astype(BF)
-
-
-def backward(scaled, gate, up, weights, tile, per_dest, gate_row):
+        own = slice(d * per_dest, (d + 1) * per_dest)
+        part = lax.dot_general(ones, high[own], by_ff, preferred_element_type=F32)
+        part += lax.dot_general(ones, low[own], by_ff, preferred_element_type=F32)
+        row = d * per_dest + gate_row
+        at = row // 16 * 16
+        window = rows_ref[at : at + 16, 0:per_dest].astype(F32)
+        rows_ref[at : at + 16, 0:per_dest] = jnp.where(line == row - at, part, window).astype(BF)
+
+
+def backward(scaled, pre, joined, down, tile, per_dest, gate_row):
     rows = scaled.shape[0]
     wide = pl.BlockSpec((tile, D), lambda i: (i, 0))
     slim = pl.BlockSpec((tile, FF), lambda i: (i, 0))
-    small = jax.ShapeDtypeStruct((rows, FF), BF)
     return pl.pallas_call(
         functools.partial(backward_body, per_dest, gate_row),
         grid=(rows // tile,),
-        in_specs=[wide, slim, slim, weight_spec(0), weight_spec(1), weight_spec(2)],
-        out_specs=[wide, slim, slim, slim],
-        out_shape=[jax.ShapeDtypeStruct((rows, D), BF), small, small, small],
-        scratch_shapes=[pltpu.VMEM((tile, D), F32)],
+        in_specs=[
+            wide,
+            pl.BlockSpec((tile, 2 * FF), lambda i: (i, 0)),
+            resident(),
+            resident(),
+        ],
+        out_specs=[wide, pl.BlockSpec((tile, 2 * FF), lambda i: (i, 0)), slim],
+        out_shape=[
+            jax.ShapeDtypeStruct((rows, D), BF),
+            jax.ShapeDtypeStruct((rows, 2 * FF), BF),
+            jax.ShapeDtypeStruct((rows, FF), BF),
+        ],
         compiler_params=params(),
         cost_estimate=cost(6 * rows * D * FF, 4 * D * rows + 6 * D * FF),
         name="expert_backward",
-    )(scaled, gate, up, weights, weights, weights)
-
-
-def weight_grad_body(xn, xf, sn, sf, dgn, dgf, dun, duf, hn, hf, out_ref):
+    )(scaled, pre, joined, down)
+
+
+def weight_grad_body(sec_ref, xn, xf, sn, sf, dn, df, hn, hf, sent_ref, kept_ref):
     by_rows = (((0,), (0,)), ((), ()))
 
     def both(a, b, c, d):
-        return lax.dot_general(a[...], c[...], by_rows, preferred_element_type=F32) + lax.dot_general(
-            b[...], d[...], by_rows, preferred_element_type=F32
-        )
-
-    out_ref[0] = both(xn, xf, dgn, dgf).astype(BF)
-    out_ref[1] = both(xn, xf, dun, duf).astype(BF)
-    out_ref[2] = both(sn, sf, hn, hf).astype(BF)
-
-
-def weight_grad(near, far):
-    tile = 512
+        return (
+            lax.dot_general(a[...], c[...], by_rows, preferred_element_type=F32)
+            + lax.dot_general(b[...], d[...], by_rows, preferred_element_type=F32)
+        ).astype(BF)
+
+    inner = both(xn, xf, dn, df)
+    outer = both(sn, sf, hn, hf)
+
+    def store(ref):
+        ref[0] = inner[:, 0:FF]
+        ref[1] = inner[:, FF : 2 * FF]
+        ref[2] = outer
+
+    pl.when(pl.program_id(0) < 2)(lambda: store(sent_ref))
+    pl.when(pl.program_id(0) >= 2)(lambda: store(kept_ref))
+
+
+def weight_grad(section, near, far):
+    tile = D // 4
     args, specs = [], []
     for a, b in zip(near, far):
         for v in (a, b):
             args.append(v)
             if v.shape[1] == D:
-                specs.append(pl.BlockSpec((v.shape[0], tile), lambda i: (0, i)))
+                specs.append(
+                    pl.BlockSpec(
+                        (v.shape[0], tile), lambda i, sec: (0, sec[0] ^ (2 * i + 1 - 5 * (i // 2)))
+                    )
+                )
             else:
-                specs.append(pl.BlockSpec(v.shape, lambda i: (0, 0)))
+                specs.append(pl.BlockSpec(v.shape, lambda i, sec: (0, 0)))
     rows = near[0].shape[0] + far[0].shape[0]
+    out = jax.ShapeDtypeStruct((2, 3, tile, FF), BF)
     return pl.pallas_call(
         weight_grad_body,
-        grid=(D // tile,),
-        in_specs=specs,
-        out_specs=pl.BlockSpec((3, None, tile, FF), lambda i: (0, 0, i, 0)),
-        out_shape=jax.ShapeDtypeStruct((3, 1, D, FF), BF),
+        grid_spec=pltpu.PrefetchScalarGridSpec(
+            num_scalar_prefetch=1,
+            grid=(4,),
+            in_specs=specs,
+            out_specs=[
+                pl.BlockSpec((None, 3, tile, FF), lambda i, sec: (jnp.minimum(i, 1), 0, 0, 0)),
+                pl.BlockSpec((None, 3, tile, FF), lambda i, sec: (jnp.maximum(i - 2, 0), 0, 0, 0)),
+            ],
+        ),
+        out_shape=[out, out],
         compiler_params=params(),
         cost_estimate=cost(6 * rows * D * FF, 4 * rows * D + 6 * D * FF),
         name="weight_grads",
-    )(*args)
+    )(section, *args)
+
+
+def section_mean(sent, kept):
+    other_core = [(s, s ^ 1) for s in range(4)]
+    other_chip = [(s, s ^ 2) for s in range(4)]
+    got = lax.ppermute(sent, "section", other_core)
+    onward = added(kept[1], got[1])
+    last = lax.ppermute(onward, "section", other_chip)
+    total = kept[0].astype(F32) + got[0].astype(F32) + last.astype(F32)
+    return (total / 4.0)[:, None]
 
 
 def combine_body(per_dest, count, gate_row, z_ref, q_ref, w_ref, r_ref, x_ref, *refs):
@@ -427,37 +478,43 @@
 
 def per_device(tokens, cotangent, routes, route_weights, weights):
     z = lax.axis_index("expert").reshape(1).astype(jnp.int32)
+    section = lax.axis_index("section").reshape(1).astype(jnp.int32)
     own = pack(tokens[0], routes[0].T, route_weights[0].T)
     tok_near, tok_far = ring_gather(own)
-    cot_near, cot_far = ring_gather(after(cotangent[0], tok_far[-1], tok_far[-2]))
-
-    send_near, qn, wn, rn = select_tok(z, tok_near, NEAR_ROWS, len(NEAR))
-    xn = exchange(send_near, NEAR_ROWS)
-    send_far, qf, wf, rf = select_tok(z, tok_far, FAR_ROWS, len(FAR))
-    xf = exchange(send_far, FAR_ROWS)
-    sn = exchange(select_cot(qn, wn, cot_near, NEAR_ROWS, len(NEAR)), NEAR_ROWS)
-    sf = exchange(select_cot(qf, wf, cot_far, FAR_ROWS, len(FAR)), FAR_ROWS)
-
-    tile_n, tile_f = 4 * NEAR_ROWS, 2 * FAR_ROWS
-    gn, un = forward(xn, weights, tile_n)
-    gf, uf = forward(xf, weights, tile_f)
+    joined, down = join_weights(weights)
+    cot, tok_near[1], tok_near[2] = ordered(cotangent[0], tok_near[1], tok_near[2])
+    cot_near, cot_far = ring_gather(cot)
+
+    send, qn, wn, rn = select_tok(z, tok_near, NEAR_ROWS, len(NEAR))
+    xn = exchange(send, NEAR_ROWS)
+    send = select_cot(qn, wn, cot_near, NEAR_ROWS, len(NEAR))
+    send, xn, tok_far[0], tok_far[1] = ordered(send, xn, tok_far[0], tok_far[1])
+    sn = exchange(send, NEAR_ROWS)
+    send, qf, wf, rf = select_tok(z, tok_far, FAR_ROWS, len(FAR))
+    send, sn = ordered(send, sn)
+    xf = exchange(send, FAR_ROWS)
+    send, xf = ordered(select_cot(qf, wf, cot_far, FAR_ROWS, len(FAR)), xf)
+    sf = exchange(send, FAR_ROWS)
+
+    near_tile, far_tile = 4 * NEAR_ROWS, 4 * FAR_ROWS
+    pn = forward(xn, joined, near_tile)
+    pf = forward(xf, joined, far_tile)
     near_gate, far_gate = len(NEAR) * CAP, len(FAR) * CAP
-    rows_n, dgn, dun, hn = backward(sn, gn, un, weights, tile_n, NEAR_ROWS, near_gate)
-    rows_f, dgf, duf, hf = backward(sf, gf, uf, weights, tile_f, FAR_ROWS, far_gate)
+    rows_n, dn, hn = backward(sn, pn, joined, down, near_tile, NEAR_ROWS, near_gate)
+    sf, rows_n, pf = ordered(sf, rows_n, pf)
+    rows_f, df, hf = backward(sf, pf, joined, down, far_tile, FAR_ROWS, far_gate)
     back_f = exchange(rows_f, FAR_ROWS)
+    rows_n, back_f = ordered(rows_n, back_f)
     back_n = exchange(rows_n, NEAR_ROWS)
 
-    part = weight_grad((xn, sn, dgn, dun, after(hn, back_f)), (xf, sf, dgf, duf, hf))
-    summed = lax.psum_scatter(part, "section", scatter_dimension=2, tiled=True)
-    weight_grads = summed.astype(F32) / lax.axis_size("section")
-
+    sent, kept = weight_grad(section, (xn, sn, dn, hn), (xf, sf, df, hf))
     far_sizes = [ROWS] * 4 + [HALF, HALF + META]
     far_parts = combine(z, qf, wf, rf, back_f, far_sizes, FAR_ROWS, len(FAR), far_gate)
     near_parts = combine(z, qn, wn, rn, back_n, [ROWS] * 3, NEAR_ROWS, len(NEAR), near_gate)
     total = ring_scatter(near_parts, far_parts)
     token_grads = total[:TOK].astype(BF)[None]
     gate_grads = total[TOK:, :TOK].T.astype(BF)[None]
-    return token_grads, gate_grads, weight_grads
+    return token_grads, gate_grads, section_mean(sent, kept)
 
 
 def solution(mesh):

time: 346 us -> 313 us (0.905)
  the two profiles are of different devices: /device:TPU:98 before, /device:TPU:8 now
where the time goes in v2:
time: 313 us; the launch traced here: 312 us
  waiting for transfers between devices  155 us (50%)
  starting transfers between devices  63.9 us (20%)
  Pallas kernels  47.8 us (15%)
  local copies, waits for them, and re-layouts  32.8 us (10%)
  other arithmetic  10.9 us (3%)
    ppermute x6, waiting for transfers between devices, ring_gather(): up = lax.ppermute(up, 'expert', bw)  58.9 us
    all_to_all x6, waiting for transfers between devices, exchange(): lax.all_to_all(sent, ('section', 'expert'), 0, 0, axis_index_groups=plane...  52.6 us
    unnamed x72, local copies, waits for them, and re-layouts  31.4 us
    all_to_all x6, starting transfers between devices, exchange(): lax.all_to_all(sent, ('section', 'expert'), 0, 0, axis_index_groups=plane...  31.1 us
    ppermute x1, waiting for transfers between devices, section_mean(): last = lax.ppermute(onward, 'section', other_chip)  12.8 us
    pallas_call x2, Pallas kernels, backward(): pl.pallas_call(functools.partial(backward_body, per_dest, gate_row), grid...  12.5 us
    pallas_call x1, Pallas kernels, weight_grad(): pl.pallas_call(weight_grad_body, grid_spec=pltpu.PrefetchScalarGridSpec(n...  10.9 us
    ppermute x2, waiting for transfers between devices, ring_gather(): top = lax.ppermute(down[:HALF], 'expert', fw)  9.45 us
  transfers between devices with their start and end apart: 32, of which 21 were waited for; matrix products, arithmetic and copies ran while one was open for 3% of the time, Pallas kernels for 12%

profile of v2, /device:TPU:8, one launch (start us, length us, event | category | flops | bytes accessed | tf_op | source)
XLA Modules:
  0.0 311.6 jit_solution(5355550608700433125)
XLA Ops:
  3.1 5.9 %collective-permute-start.1 = (bf16[136,2048]{1,0:T(8,128)(2,1)S(1)}, bf16[136,2048]{1,0:T(8,128)(2,1)}, u32[]{:S(2)}, u32[]{:S(2)}) collective-permute-start(bf16[136,2048]{1,0:T(8,128)(2,1)S(1)} %pack_rows.1.refs_0_), channel_id=1, source_target_pairs={{0,56},{1,57},{2,58},{3,59},{4,60},{5,61},{6,62},{7,63},{8,0},{9,1... | collective-permute-start | bytes 1671176 | tf_op jit(solution)/shard_map/ppermute | solution.py:451
  9.0 11.9 %collective-permute-done.1.refs_2_ = bf16[136,2048]{1,0:T(8,128)(2,1)} collective-permute-done((bf16[136,2048]{1,0:T(8,128)(2,1)S(1)}, bf16[136,2048]{1,0:T(8,128)(2,1)}, u32[]{:S(2)}, u32[]{:S(2)}) %collective-permute-start.1) | collective-permute-done | bytes 557088 | tf_op jit(solution)/shard_map/ppermute | solution.py:451
  20.9 3.4 %collective-permute-done.refs_1_ = bf16[136,2048]{1,0:T(8,128)(2,1)S(1)} collective-permute-done((bf16[136,2048]{1,0:T(8,128)(2,1)S(1)}, bf16[136,2048]{1,0:T(8,128)(2,1)S(1)}, u32[]{:S(2)}, u32[]{:S(2)}) %collective-permute-start) | collective-permute-done | bytes 557088 | tf_op jit(solution)/shard_map/ppermute | solution.py:450
  28.4 5.5 %all-to-all-start = ((bf16[8,56,2048]{2,1,0:T(8,128)(2,1)}), bf16[8,56,2048]{2,1,0:T(8,128)(2,1)S(1)}, u32[]{:S(2)}, u32[]{:S(2)}) async-start(bf16[8,56,2048]{2,1,0:T(8,128)(2,1)} %bitcast.48), calls=%async_computation | async-start | bytes 3670016 | tf_op jit(solution)/shard_map/all_to_all | solution.py:66
  38.0 10.8 %collective-permute-done.3.refs_2_ = bf16[128,2048]{1,0:T(8,128)(2,1)S(1)} collective-permute-done((bf16[128,2048]{1,0:T(8,128)(2,1)S(1)}, bf16[128,2048]{1,0:T(8,128)(2,1)S(1)}, u32[]{:S(2)}, u32[]{:S(2)}) %collective-permute-start.3) | collective-permute-done | bytes 524320 | tf_op jit(solution)/shard_map/ppermute | solution.py:451
  53.3 4.8 %collective-permute-done.5.refs_1_ = bf16[136,2048]{1,0:T(8,128)(2,1)S(1)} collective-permute-done((bf16[136,2048]{1,0:T(8,128)(2,1)}, bf16[136,2048]{1,0:T(8,128)(2,1)S(1)}, u32[]{:S(2)}, u32[]{:S(2)}) %collective-permute-start.5) | collective-permute-done | bytes 557088 | tf_op jit(solution)/shard_map/ppermute | solution.py:451
  61.0 5.3 %all-to-all-start.1 = ((bf16[8,56,2048]{2,1,0:T(8,128)(2,1)}), bf16[8,56,2048]{2,1,0:T(8,128)(2,1)}, u32[]{:S(2)}, u32[]{:S(2)}) async-start(bf16[8,56,2048]{2,1,0:T(8,128)(2,1)} %bitcast.42), calls=%async_computation.1 | async-start | bytes 3670016 | tf_op jit(solution)/shard_map/all_to_all | solution.py:66
  68.4 10.6 %collective-permute-done.7.refs_3_ = bf16[136,2048]{1,0:T(8,128)(2,1)S(1)} collective-permute-done((bf16[136,2048]{1,0:T(8,128)(2,1)S(1)}, bf16[136,2048]{1,0:T(8,128)(2,1)S(1)}, u32[]{:S(2)}, u32[]{:S(2)}) %collective-permute-start.7) | collective-permute-done | bytes 557088 | tf_op jit(solution)/shard_map/ppermute | solution.py:451
  81.2 6.8 %collective-permute-done.8.refs_4_ = bf16[64,2048]{1,0:T(8,128)(2,1)S(1)} collective-permute-done((bf16[64,2048]{1,0:T(8,128)(2,1)S(1)}, bf16[64,2048]{1,0:T(8,128)(2,1)S(1)}, u32[]{:S(2)}, u32[]{:S(2)}) %collective-permute-start.8) | collective-permute-done | bytes 262176 | tf_op jit(solution)/shard_map/ppermute | solution.py:453
  87.9 3.8 %select_tokens.3 = (bf16[768,2048]{1,0:T(8,128)(2,1)S(1)}, s32[8,640]{1,0:T(8,128)S(1)}, f32[8,640]{1,0:T(8,128)S(1)}, f32[8,640]{1,0:T(8,128)S(1)}) custom-call(s32[1]{0:T(128)} %bitcast.z_ref, bf16[136,2048]{1,0:T(8,128)(2,1)S(1)} %collective-permute-done.4.refs_0_, bf16[136,2048]{1,0:T(8,128)(2,1)S(1)} %collective-permute-done.5.refs_1_, ...), custom_call_target="tpu_custom_call" | custom-call | flops 2013265920 | bytes 5767168 | tf_op jit(solution)/shard_map/select_tokens/pallas_call | solution.py:143
  94.0 5.3 %all-to-all-start.2 = ((bf16[8,96,2048]{2,1,0:T(8,128)(2,1)}), bf16[8,96,2048]{2,1,0:T(8,128)(2,1)S(1)}, u32[]{:S(2)}, u32[]{:S(2)}) async-start(bf16[8,96,2048]{2,1,0:T(8,128)(2,1)} %bitcast.45), calls=%async_computation.2 | async-start | bytes 6291456 | tf_op jit(solution)/shard_map/all_to_all | solution.py:66
  101.3 10.9 %collective-permute-done.11.refs_1_ = bf16[128,2048]{1,0:T(8,128)(2,1)S(1)} collective-permute-done((bf16[128,2048]{1,0:T(8,128)(2,1)}, bf16[128,2048]{1,0:T(8,128)(2,1)S(1)}, u32[]{:S(2)}, u32[]{:S(2)}) %collective-permute-start.11) | collective-permute-done | bytes 524320 | tf_op jit(solution)/shard_map/ppermute | solution.py:451
  114.2 10.0 %collective-permute-done.13.refs_3_ = bf16[128,2048]{1,0:T(8,128)(2,1)S(1)} collective-permute-done((bf16[128,2048]{1,0:T(8,128)(2,1)S(1)}, bf16[128,2048]{1,0:T(8,128)(2,1)S(1)}, u32[]{:S(2)}, u32[]{:S(2)}) %collective-permute-start.13) | collective-permute-done | bytes 524320 | tf_op jit(solution)/shard_map/ppermute | solution.py:451
  126.4 4.2 %collective-permute-done.15.refs_5_ = bf16[64,2048]{1,0:T(8,128)(2,1)S(1)} collective-permute-done((bf16[64,2048]{1,0:T(8,128)(2,1)S(1)}, bf16[64,2048]{1,0:T(8,128)(2,1)S(1)}, u32[]{:S(2)}, u32[]{:S(2)}) %collective-permute-start.15) | collective-permute-done | bytes 262176 | tf_op jit(solution)/shard_map/ppermute | solution.py:454
  133.4 3.4 %select_cotangents.3 = bf16[768,2048]{1,0:T(8,128)(2,1)S(1)} custom-call(s32[8,640]{1,0:T(8,128)S(1)} %get-tuple-element.55.q_ref, f32[8,640]{1,0:T(8,128)S(1)} %get-tuple-element.56.w_ref, bf16[128,2048]{1,0:T(8,128)(2,1)S(1)} %collective-permute-done.10.refs_0_, bf16[128,2048]{1,0:T(8,128)(2,1)S(1)} %collective-permute-done.11.refs_1_, ...), custom_call_target="tpu_custom_call" | custom-call | flops 2013265920 | bytes 5767168 | tf_op jit(solution)/shard_map/select_cotangents/pallas_call | solution.py:184
  140.2 5.8 %all-to-all-start.3 = ((bf16[8,96,2048]{2,1,0:T(8,128)(2,1)}), bf16[8,96,2048]{2,1,0:T(8,128)(2,1)}, u32[]{:S(2)}, u32[]{:S(2)}) async-start(bf16[8,96,2048]{2,1,0:T(8,128)(2,1)} %bitcast.47), calls=%async_computation.3 | async-start | bytes 6291456 | tf_op jit(solution)/shard_map/all_to_all | solution.py:66
  151.8 6.0 %expert_backward.2 = (bf16[448,2048]{1,0:T(8,128)(2,1)}, bf16[448,768]{1,0:T(8,128)(2,1)S(1)}, bf16[448,384]{1,0:T(8,128)(2,1)S(1)}) custom-call(bf16[448,2048]{1,0:T(8,128)(2,1)} %bitcast.10.sc_ref.sn, f32[448,768]{1,0:T(8,128)S(1)} %expert_forward.2.p_ref, bf16[2048,768]{1,0:T(8,128)(2,1)S(1)} %get-tuple-element.63.w_ref, ...), custom_call_target="tpu_custom_call" | custom-call | flops 2113929216 | bytes 8388608 | tf_op jit(solution)/shard_map/expert_backward/pallas_call | solution.py:281
  163.7 21.0 %all-to-all-done.3 = bf16[8,96,2048]{2,1,0:T(8,128)(2,1)} async-done(((bf16[8,96,2048]{2,1,0:T(8,128)(2,1)}), bf16[8,96,2048]{2,1,0:T(8,128)(2,1)}, u32[]{:S(2)}, u32[]{:S(2)}) %all-to-all-start.3) | async-done | bytes 3145760 | tf_op jit(solution)/shard_map/all_to_all | solution.py:66
  187.7 6.4 %expert_backward.3 = (bf16[768,2048]{1,0:T(8,128)(2,1)S(1)}, bf16[768,768]{1,0:T(8,128)(2,1)S(1)}, bf16[768,384]{1,0:T(8,128)(2,1)S(1)}) custom-call(bf16[768,2048]{1,0:T(8,128)(2,1)} %bitcast.14.sc_ref.sf, f32[768,768]{1,0:T(8,128)S(1)} %copy-done.28, bf16[2048,768]{1,0:T(8,128)(2,1)S(1)} %get-tuple-element.63.w_ref, bf16[2048,384]{1,0:T(8,128)(2,1)S(1)} %copy-done.15), custom_call_target="tpu_custom_call" | custom-call | flops 3623878656 | bytes 11010048 | tf_op jit(solution)/shard_map/expert_backward/pallas_call | solution.py:281
  197.9 4.9 %all-to-all-start.4 = ((bf16[8,96,2048]{2,1,0:T(8,128)(2,1)}), bf16[8,96,2048]{2,1,0:T(8,128)(2,1)}, u32[]{:S(2)}, u32[]{:S(2)}) async-start(bf16[8,96,2048]{2,1,0:T(8,128)(2,1)} %bitcast.46), calls=%async_computation.4 | async-start | bytes 6291456 | tf_op jit(solution)/shard_map/all_to_all | solution.py:66
  206.0 10.9 %weight_grads.1 = (bf16[2,3,512,384]{3,2,1,0:T(8,128)(2,1)}, bf16[2,3,512,384]{3,2,1,0:T(8,128)(2,1)S(1)}) custom-call(s32[1]{0:T(128)} %bitcast.22.sec_ref, bf16[448,2048]{1,0:T(8,128)(2,1)S(1)} %bitcast.41, bf16[768,2048]{1,0:T(8,128)(2,1)S(1)} %bitcast.44, bf16[448,2048]{1,0:T(8,128)(2,1)} %bitcast.10.sc_ref.sn, bf16[768,2048]{1,0:T(8,128)(2,1)} %bitcast.14.sc_ref.sf, ...), custom_call_target="tpu_custom_call" | custom-call | flops 5737807872 | bytes 14680064 | tf_op jit(solution)/shard_map/weight_grads/pallas_call | solution.py:339
  218.4 26.2 %all-to-all-done.4 = bf16[8,96,2048]{2,1,0:T(8,128)(2,1)} async-done(((bf16[8,96,2048]{2,1,0:T(8,128)(2,1)}), bf16[8,96,2048]{2,1,0:T(8,128)(2,1)}, u32[]{:S(2)}, u32[]{:S(2)}) %all-to-all-start.4) | async-done | bytes 3145760 | tf_op jit(solution)/shard_map/all_to_all | solution.py:66
  245.3 4.8 %combine_rows.3 = (bf16[136,2048]{1,0:T(8,128)(2,1)S(1)}, bf16[136,2048]{1,0:T(8,128)(2,1)S(1)}, bf16[136,2048]{1,0:T(8,128)(2,1)S(1)}, bf16[136,2048]{1,0:T(8,1...) custom-call(s32[1]{0:T(128)} %bitcast.z_ref, s32[8,640]{1,0:T(8,128)S(1)} %get-tuple-element.55.q_ref, ...), custom_call_target="tpu_custom_call" | custom-call | flops 2013265920 | bytes 5767168 | tf_op jit(solution)/shard_map/combine_rows/pallas_call | solution.py:426
  252.6 4.4 %collective-permute-done.20 = bf16[72,2048]{1,0:T(8,128)(2,1)S(1)} collective-permute-done((bf16[72,2048]{1,0:T(8,128)(2,1)S(1)}, bf16[72,2048]{1,0:T(8,128)(2,1)S(1)}, u32[]{:S(2)}, u32[]{:S(2)}) %collective-permute-start.20) | collective-permute-done | bytes 294944 | tf_op jit(solution)/shard_map/ppermute | solution.py:468
  257.1 3.8 %collective-permute-start.21 = (bf16[136,2048]{1,0:T(8,128)(2,1)S(1)}, bf16[136,2048]{1,0:T(8,128)(2,1)S(1)}, u32[]{:S(2)}, u32[]{:S(2)}) collective-permute-start(bf16[136,2048]{1,0:T(8,128)(2,1)S(1)} %add_convert_fusion.4), channel_id=1, source_target_pairs={{0,56},{1,57},{2,58},{3,59},{4,60},{5,61},{6,62},{7,63},{8,0},{9,1... | collective-permute-start | bytes 1671176 | tf_op jit(solution)/shard_map/ppermute | solution.py:473
  260.9 4.3 %all-to-all-start.5 = ((bf16[8,56,2048]{2,1,0:T(8,128)(2,1)}), bf16[8,56,2048]{2,1,0:T(8,128)(2,1)}, u32[]{:S(2)}, u32[]{:S(2)}) async-start(bf16[8,56,2048]{2,1,0:T(8,128)(2,1)} %bitcast.17), calls=%async_computation.5 | async-start | bytes 3670016 | tf_op jit(solution)/shard_map/all_to_all | solution.py:66
  266.3 3.6 %collective-permute-done.21 = bf16[136,2048]{1,0:T(8,128)(2,1)S(1)} collective-permute-done((bf16[136,2048]{1,0:T(8,128)(2,1)S(1)}, bf16[136,2048]{1,0:T(8,128)(2,1)S(1)}, u32[]{:S(2)}, u32[]{:S(2)}) %collective-permute-start.21) | collective-permute-done | bytes 557088 | tf_op jit(solution)/shard_map/ppermute | solution.py:473
  273.0 3.7 %collective-permute-start.22 = (bf16[136,2048]{1,0:T(8,128)(2,1)}, bf16[136,2048]{1,0:T(8,128)(2,1)S(1)}, u32[]{:S(2)}, u32[]{:S(2)}) collective-permute-start(bf16[136,2048]{1,0:T(8,128)(2,1)} %add_convert_fusion.3), channel_id=1, source_target_pairs={{0,56},{1,57},{2,58},{3,59},{4,60},{5,61},{6,62},{7,63},{8,0},{9,1... | collective-permute-start | bytes 1671176 | tf_op jit(solution)/shard_map/ppermute | solution.py:473
  282.7 5.4 %all-to-all-done.5 = bf16[8,56,2048]{2,1,0:T(8,128)(2,1)} async-done(((bf16[8,56,2048]{2,1,0:T(8,128)(2,1)}), bf16[8,56,2048]{2,1,0:T(8,128)(2,1)}, u32[]{:S(2)}, u32[]{:S(2)}) %all-to-all-start.5) | async-done | bytes 1835040 | tf_op jit(solution)/shard_map/all_to_all | solution.py:66
  288.2 3.0 combine_rows.2
  293.6 12.8 %collective-permute-done.25 = bf16[3,512,384]{2,1,0:T(8,128)(2,1)} collective-permute-done((bf16[3,512,384]{2,1,0:T(8,128)(2,1)}, bf16[3,512,384]{2,1,0:T(8,128)(2,1)}, u32[]{:S(2)}, u32[]{:S(2)}) %collective-permute-start.25) | collective-permute-done | bytes 1179680 | tf_op jit(solution)/shard_map/ppermute | solution.py:362
  306.5 3.5 %fusion.1 = f32[3,1,512,384]{3,2,1,0:T(8,128)} fusion(bf16[3,512,384]{2,1,0:T(8,128)(2,1)} %collective-permute-done.25, bf16[2,3,512,384]{3,2,1,0:T(8,128)(2,1)} %collective-permute-done.24, bf16[2,3,512,384]{3,2,1,0:T(8,128)(2,1)S(1)} %copy-done.12), kind=kLoop, calls=%fused_computation.2 | loop fusion | flops 3538944 | bytes 5898240
  (132 shorter events, 77.6 us)
Async XLA Ops:
  3.1 17.8 %collective-permute-start.1 = (bf16[136,2048]{1,0:T(8,128)(2,1)S(1)}, bf16[136,2048]{1,0:T(8,128)(2,1)}, u32[]{:S(2)}, u32[]{:S(2)}) collective-permute-start(bf16[136,2048]{1,0:T(8,128)(2,1)S(1)} %pack_rows.1.refs_0_), channel_id=1, source_target_pairs={{0,56},{1,57},{2,58},{3,59},{4,60},{5,61},{6,62},{7,63},{8,0},{9,1... | collective-permute-start | bytes 1671176 | tf_op jit(solution)/shard_map/ppermute | solution.py:451
  9.0 15.3 %collective-permute-start = (bf16[136,2048]{1,0:T(8,128)(2,1)S(1)}, bf16[136,2048]{1,0:T(8,128)(2,1)S(1)}, u32[]{:S(2)}, u32[]{:S(2)}) collective-permute-start(bf16[136,2048]{1,0:T(8,128)(2,1)S(1)} %pack_rows.1.refs_0_), channel_id=1, source_target_pairs={{0,8},{1,9},{2,10},{3,11},{4,12},{5,13},{6,14},{7,15},{8,16},{9,17... | collective-permute-start | bytes 1671176 | tf_op jit(solution)/shard_map/ppermute | solution.py:450
  28.4 31.3 %all-to-all-start = ((bf16[8,56,2048]{2,1,0:T(8,128)(2,1)}), bf16[8,56,2048]{2,1,0:T(8,128)(2,1)S(1)}, u32[]{:S(2)}, u32[]{:S(2)}) async-start(bf16[8,56,2048]{2,1,0:T(8,128)(2,1)} %bitcast.48), calls=%async_computation | async-start | bytes 3670016 | tf_op jit(solution)/shard_map/all_to_all | solution.py:66
  33.9 14.9 %collective-permute-start.3 = (bf16[128,2048]{1,0:T(8,128)(2,1)S(1)}, bf16[128,2048]{1,0:T(8,128)(2,1)S(1)}, u32[]{:S(2)}, u32[]{:S(2)}) collective-permute-start(bf16[128,2048]{1,0:T(8,128)(2,1)S(1)} %bitcast.50), channel_id=1, source_target_pairs={{0,56},{1,57},{2,58},{3,59},{4,60},{5,61},{6,62},{7,63},{8,0},{9,1... | collective-permute-start | bytes 1572872 | tf_op jit(solution)/shard_map/ppermute | solution.py:451
  34.4 16.1 %collective-permute-start.2 = (bf16[128,2048]{1,0:T(8,128)(2,1)S(1)}, bf16[128,2048]{1,0:T(8,128)(2,1)S(1)}, u32[]{:S(2)}, u32[]{:S(2)}) collective-permute-start(bf16[128,2048]{1,0:T(8,128)(2,1)S(1)} %bitcast.51), channel_id=1, source_target_pairs={{0,8},{1,9},{2,10},{3,11},{4,12},{5,13},{6,14},{7,15},{8,16},{9,17... | collective-permute-start | bytes 1572872 | tf_op jit(solution)/shard_map/ppermute | solution.py:450
  36.0 22.1 %collective-permute-start.5 = (bf16[136,2048]{1,0:T(8,128)(2,1)}, bf16[136,2048]{1,0:T(8,128)(2,1)S(1)}, u32[]{:S(2)}, u32[]{:S(2)}) collective-permute-start(bf16[136,2048]{1,0:T(8,128)(2,1)} %collective-permute-done.1.refs_2_), channel_id=1, source_target_pairs={{0,56},{1,57},{2,58},{3,59},{4,60},{5,61},{6,62},{7,63},{8,0},{9,1... | collective-permute-start | bytes 1671176 | tf_op jit(solution)/shard_map/ppermute | solution.py:451
  37.6 22.1 %collective-permute-start.4 = (bf16[136,2048]{1,0:T(8,128)(2,1)}, bf16[136,2048]{1,0:T(8,128)(2,1)S(1)}, u32[]{:S(2)}, u32[]{:S(2)}) collective-permute-start(bf16[136,2048]{1,0:T(8,128)(2,1)} %copy-done.24), channel_id=1, source_target_pairs={{0,8},{1,9},{2,10},{3,11},{4,12},{5,13},{6,14},{7,15},{8,16},{9,17... | collective-permute-start | bytes 1671176 | tf_op jit(solution)/shard_map/ppermute | solution.py:450
  61.0 33.0 %all-to-all-start.1 = ((bf16[8,56,2048]{2,1,0:T(8,128)(2,1)}), bf16[8,56,2048]{2,1,0:T(8,128)(2,1)}, u32[]{:S(2)}, u32[]{:S(2)}) async-start(bf16[8,56,2048]{2,1,0:T(8,128)(2,1)} %bitcast.42), calls=%async_computation.1 | async-start | bytes 3670016 | tf_op jit(solution)/shard_map/all_to_all | solution.py:66
  66.4 12.6 %collective-permute-start.7 = (bf16[136,2048]{1,0:T(8,128)(2,1)S(1)}, bf16[136,2048]{1,0:T(8,128)(2,1)S(1)}, u32[]{:S(2)}, u32[]{:S(2)}) collective-permute-start(bf16[136,2048]{1,0:T(8,128)(2,1)S(1)} %collective-permute-done.5.refs_1_), channel_id=1, source_target_pairs={{0,56},{1,57},{2,58},{3,59},{4,60},{5,61},{6,62},{7,63},{8,0},{9,1... | collective-permute-start | bytes 1671176 | tf_op jit(solution)/shard_map/ppermute | solution.py:451
  66.6 13.6 %collective-permute-start.6 = (bf16[136,2048]{1,0:T(8,128)(2,1)S(1)}, bf16[136,2048]{1,0:T(8,128)(2,1)S(1)}, u32[]{:S(2)}, u32[]{:S(2)}) collective-permute-start(bf16[136,2048]{1,0:T(8,128)(2,1)S(1)} %collective-permute-done.4.refs_0_), channel_id=1, source_target_pairs={{0,8},{1,9},{2,10},{3,11},{4,12},{5,13},{6,14},{7,15},{8,16},{9,17... | collective-permute-start | bytes 1671176 | tf_op jit(solution)/shard_map/ppermute | solution.py:450
  79.0 9.0 %collective-permute-start.9 = (bf16[72,2048]{1,0:T(8,128)(2,1)S(1)}, bf16[72,2048]{1,0:T(8,128)(2,1)S(1)}, u32[]{:S(2)}, u32[]{:S(2)}) collective-permute-start(bf16[72,2048]{1,0:T(8,128)(2,1)S(1)} %slice.43), channel_id=1, source_target_pairs={{0,56},{1,57},{2,58},{3,59},{4,60},{5,61},{6,62},{7,63},{8,0},{9,1... | collective-permute-start | bytes 884744 | tf_op jit(solution)/shard_map/ppermute | solution.py:454
  80.3 7.7 %collective-permute-start.8 = (bf16[64,2048]{1,0:T(8,128)(2,1)S(1)}, bf16[64,2048]{1,0:T(8,128)(2,1)S(1)}, u32[]{:S(2)}, u32[]{:S(2)}) collective-permute-start(bf16[64,2048]{1,0:T(8,128)(2,1)S(1)} %slice.42), channel_id=1, source_target_pairs={{0,8},{1,9},{2,10},{3,11},{4,12},{5,13},{6,14},{7,15},{8,16},{9,17... | collective-permute-start | bytes 786440 | tf_op jit(solution)/shard_map/ppermute | solution.py:453
  94.0 44.5 %all-to-all-start.2 = ((bf16[8,96,2048]{2,1,0:T(8,128)(2,1)}), bf16[8,96,2048]{2,1,0:T(8,128)(2,1)S(1)}, u32[]{:S(2)}, u32[]{:S(2)}) async-start(bf16[8,96,2048]{2,1,0:T(8,128)(2,1)} %bitcast.45), calls=%async_computation.2 | async-start | bytes 6291456 | tf_op jit(solution)/shard_map/all_to_all | solution.py:66
  99.3 12.9 %collective-permute-start.11 = (bf16[128,2048]{1,0:T(8,128)(2,1)}, bf16[128,2048]{1,0:T(8,128)(2,1)S(1)}, u32[]{:S(2)}, u32[]{:S(2)}) collective-permute-start(bf16[128,2048]{1,0:T(8,128)(2,1)} %copy-done.19), channel_id=1, source_target_pairs={{0,56},{1,57},{2,58},{3,59},{4,60},{5,61},{6,62},{7,63},{8,0},{9,1... | collective-permute-start | bytes 1572872 | tf_op jit(solution)/shard_map/ppermute | solution.py:451
  99.5 13.0 %collective-permute-start.10 = (bf16[128,2048]{1,0:T(8,128)(2,1)}, bf16[128,2048]{1,0:T(8,128)(2,1)S(1)}, u32[]{:S(2)}, u32[]{:S(2)}) collective-permute-start(bf16[128,2048]{1,0:T(8,128)(2,1)} %copy-done.18), channel_id=1, source_target_pairs={{0,8},{1,9},{2,10},{3,11},{4,12},{5,13},{6,14},{7,15},{8,16},{9,17... | collective-permute-start | bytes 1572872 | tf_op jit(solution)/shard_map/ppermute | solution.py:450
  112.2 12.0 %collective-permute-start.13 = (bf16[128,2048]{1,0:T(8,128)(2,1)S(1)}, bf16[128,2048]{1,0:T(8,128)(2,1)S(1)}, u32[]{:S(2)}, u32[]{:S(2)}) collective-permute-start(bf16[128,2048]{1,0:T(8,128)(2,1)S(1)} %collective-permute-done.11.refs_1_), channel_id=1, source_target_pairs={{0,56},{1,57},{2,58},{3,59},{4,60},{5,61},{6,62},{7,63},{8,0},{9,1... | collective-permute-start | bytes 1572872 | tf_op jit(solution)/shard_map/ppermute | solution.py:451
  112.5 13.2 %collective-permute-start.12 = (bf16[128,2048]{1,0:T(8,128)(2,1)S(1)}, bf16[128,2048]{1,0:T(8,128)(2,1)S(1)}, u32[]{:S(2)}, u32[]{:S(2)}) collective-permute-start(bf16[128,2048]{1,0:T(8,128)(2,1)S(1)} %collective-permute-done.10.refs_0_), channel_id=1, source_target_pairs={{0,8},{1,9},{2,10},{3,11},{4,12},{5,13},{6,14},{7,15},{8,16},{9,17... | collective-permute-start | bytes 1572872 | tf_op jit(solution)/shard_map/ppermute | solution.py:450
  124.2 6.5 %collective-permute-start.15 = (bf16[64,2048]{1,0:T(8,128)(2,1)S(1)}, bf16[64,2048]{1,0:T(8,128)(2,1)S(1)}, u32[]{:S(2)}, u32[]{:S(2)}) collective-permute-start(bf16[64,2048]{1,0:T(8,128)(2,1)S(1)} %slice.45), channel_id=1, source_target_pairs={{0,56},{1,57},{2,58},{3,59},{4,60},{5,61},{6,62},{7,63},{8,0},{9,1... | collective-permute-start | bytes 786440 | tf_op jit(solution)/shard_map/ppermute | solution.py:454
  125.7 7.7 %collective-permute-start.14 = (bf16[64,2048]{1,0:T(8,128)(2,1)S(1)}, bf16[64,2048]{1,0:T(8,128)(2,1)S(1)}, u32[]{:S(2)}, u32[]{:S(2)}) collective-permute-start(bf16[64,2048]{1,0:T(8,128)(2,1)S(1)} %slice.44), channel_id=1, source_target_pairs={{0,8},{1,9},{2,10},{3,11},{4,12},{5,13},{6,14},{7,15},{8,16},{9,17... | collective-permute-start | bytes 786440 | tf_op jit(solution)/shard_map/ppermute | solution.py:453
  140.2 44.5 %all-to-all-start.3 = ((bf16[8,96,2048]{2,1,0:T(8,128)(2,1)}), bf16[8,96,2048]{2,1,0:T(8,128)(2,1)}, u32[]{:S(2)}, u32[]{:S(2)}) async-start(bf16[8,96,2048]{2,1,0:T(8,128)(2,1)} %bitcast.47), calls=%async_computation.3 | async-start | bytes 6291456 | tf_op jit(solution)/shard_map/all_to_all | solution.py:66
  197.9 46.7 %all-to-all-start.4 = ((bf16[8,96,2048]{2,1,0:T(8,128)(2,1)}), bf16[8,96,2048]{2,1,0:T(8,128)(2,1)}, u32[]{:S(2)}, u32[]{:S(2)}) async-start(bf16[8,96,2048]{2,1,0:T(8,128)(2,1)} %bitcast.46), calls=%async_computation.4 | async-start | bytes 6291456 | tf_op jit(solution)/shard_map/all_to_all | solution.py:66
  218.4 61.4 %collective-permute-start.24 = (bf16[2,3,512,384]{3,2,1,0:T(8,128)(2,1)}, bf16[2,3,512,384]{3,2,1,0:T(8,128)(2,1)}, u32[]{:S(2)}, u32[]{:S(2)}) collective-permute-start(bf16[2,3,512,384]{3,2,1,0:T(8,128)(2,1)} %get-tuple-element.88), channel_id=1, source_target_pairs={{0,64},{64,0},{128,192},{192,128},{1,65},{65,1},{129,193},{193,129... | collective-permute-start | bytes 7077896 | tf_op jit(solution)/shard_map/ppermute | solution.py:360
  250.0 7.0 %collective-permute-start.20 = (bf16[72,2048]{1,0:T(8,128)(2,1)S(1)}, bf16[72,2048]{1,0:T(8,128)(2,1)S(1)}, u32[]{:S(2)}, u32[]{:S(2)}) collective-permute-start(bf16[72,2048]{1,0:T(8,128)(2,1)S(1)} %get-tuple-element.82), channel_id=1, source_target_pairs={{0,56},{1,57},{2,58},{3,59},{4,60},{5,61},{6,62},{7,63},{8,0},{9,1... | collective-permute-start | bytes 884744 | tf_op jit(solution)/shard_map/ppermute | solution.py:468
  252.6 12.6 %collective-permute-start.16 = (bf16[64,2048]{1,0:T(8,128)(2,1)S(1)}, bf16[64,2048]{1,0:T(8,128)(2,1)}, u32[]{:S(2)}, u32[]{:S(2)}) collective-permute-start(bf16[64,2048]{1,0:T(8,128)(2,1)S(1)} %get-tuple-element.78), channel_id=1, source_target_pairs={{0,8},{1,9},{2,10},{3,11},{4,12},{5,13},{6,14},{7,15},{8,16},{9,17... | collective-permute-start | bytes 786440 | tf_op jit(solution)/shard_map/ppermute | solution.py:467
  257.1 12.8 %collective-permute-start.21 = (bf16[136,2048]{1,0:T(8,128)(2,1)S(1)}, bf16[136,2048]{1,0:T(8,128)(2,1)S(1)}, u32[]{:S(2)}, u32[]{:S(2)}) collective-permute-start(bf16[136,2048]{1,0:T(8,128)(2,1)S(1)} %add_convert_fusion.4), channel_id=1, source_target_pairs={{0,56},{1,57},{2,58},{3,59},{4,60},{5,61},{6,62},{7,63},{8,0},{9,1... | collective-permute-start | bytes 1671176 | tf_op jit(solution)/shard_map/ppermute | solution.py:473
  260.9 27.3 %all-to-all-start.5 = ((bf16[8,56,2048]{2,1,0:T(8,128)(2,1)}), bf16[8,56,2048]{2,1,0:T(8,128)(2,1)}, u32[]{:S(2)}, u32[]{:S(2)}) async-start(bf16[8,56,2048]{2,1,0:T(8,128)(2,1)} %bitcast.17), calls=%async_computation.5 | async-start | bytes 3670016 | tf_op jit(solution)/shard_map/all_to_all | solution.py:66
  266.2 12.6 %collective-permute-start.17 = (bf16[136,2048]{1,0:T(8,128)(2,1)S(1)}, bf16[136,2048]{1,0:T(8,128)(2,1)S(1)}, u32[]{:S(2)}, u32[]{:S(2)}) collective-permute-start(bf16[136,2048]{1,0:T(8,128)(2,1)S(1)} %add_convert_fusion.7), channel_id=1, source_target_pairs={{0,8},{1,9},{2,10},{3,11},{4,12},{5,13},{6,14},{7,15},{8,16},{9,17... | collective-permute-start | bytes 1671176 | tf_op jit(solution)/shard_map/ppermute | solution.py:472
  273.0 18.2 %collective-permute-start.22 = (bf16[136,2048]{1,0:T(8,128)(2,1)}, bf16[136,2048]{1,0:T(8,128)(2,1)S(1)}, u32[]{:S(2)}, u32[]{:S(2)}) collective-permute-start(bf16[136,2048]{1,0:T(8,128)(2,1)} %add_convert_fusion.3), channel_id=1, source_target_pairs={{0,56},{1,57},{2,58},{3,59},{4,60},{5,61},{6,62},{7,63},{8,0},{9,1... | collective-permute-start | bytes 1671176 | tf_op jit(solution)/shard_map/ppermute | solution.py:473
  279.8 12.0 %collective-permute-start.18 = (bf16[136,2048]{1,0:T(8,128)(2,1)}, bf16[136,2048]{1,0:T(8,128)(2,1)S(1)}, u32[]{:S(2)}, u32[]{:S(2)}) collective-permute-start(bf16[136,2048]{1,0:T(8,128)(2,1)} %add_convert_fusion.6), channel_id=1, source_target_pairs={{0,8},{1,9},{2,10},{3,11},{4,12},{5,13},{6,14},{7,15},{8,16},{9,17... | collective-permute-start | bytes 1671176 | tf_op jit(solution)/shard_map/ppermute | solution.py:472
  282.4 24.1 %collective-permute-start.25 = (bf16[3,512,384]{2,1,0:T(8,128)(2,1)}, bf16[3,512,384]{2,1,0:T(8,128)(2,1)}, u32[]{:S(2)}, u32[]{:S(2)}) collective-permute-start(bf16[3,512,384]{2,1,0:T(8,128)(2,1)} %fusion.2), channel_id=1, source_target_pairs={{0,128},{64,192},{128,0},{192,64},{1,129},{65,193},{129,1},{193,65... | collective-permute-start | bytes 3538952 | tf_op jit(solution)/shard_map/ppermute | solution.py:362
  291.3 18.6 %collective-permute-start.23 = (bf16[136,2048]{1,0:T(8,128)(2,1)S(1)}, bf16[136,2048]{1,0:T(8,128)(2,1)S(1)}, u32[]{:S(2)}, u32[]{:S(2)}) collective-permute-start(bf16[136,2048]{1,0:T(8,128)(2,1)S(1)} %add_convert_fusion.2), channel_id=1, source_target_pairs={{0,56},{1,57},{2,58},{3,59},{4,60},{5,61},{6,62},{7,63},{8,0},{9,1... | collective-permute-start | bytes 1671176 | tf_op jit(solution)/shard_map/ppermute | solution.py:475
  291.9 18.1 %collective-permute-start.19 = (bf16[136,2048]{1,0:T(8,128)(2,1)S(1)}, bf16[136,2048]{1,0:T(8,128)(2,1)S(1)}, u32[]{:S(2)}, u32[]{:S(2)}) collective-permute-start(bf16[136,2048]{1,0:T(8,128)(2,1)S(1)} %add_convert_fusion.5), channel_id=1, source_target_pairs={{0,8},{1,9},{2,10},{3,11},{4,12},{5,13},{6,14},{7,15},{8,16},{9,17... | collective-permute-start | bytes 1671176 | tf_op jit(solution)/shard_map/ppermute | solution.py:474
  (36 other events, 85.9 us)

commit v3 on v2

--- a/solution.py
+++ b/solution.py
@@ -33,6 +33,14 @@
 
 def cost(flops, nbytes):
     return pl.CostEstimate(flops=flops, bytes_accessed=nbytes, transcendentals=0)
+
+
+def far_memory(shape, dtype=BF):
+    return pltpu.HBM(shape, dtype)
+
+
+def pinned(*arrays):
+    return [pltpu.with_memory_space_constraint(a, pltpu.HBM) for a in arrays]
 
 
 def forward_pairs():
@@ -147,7 +155,7 @@
         + [pl.BlockSpec((b.shape[0], COLS), lambda i: (0, i)) for b in blocks],
         out_specs=[pl.BlockSpec((rows, COLS), lambda i: (0, i)), small, small, small],
         out_shape=[
-            jax.ShapeDtypeStruct((rows, D), BF),
+            far_memory((rows, D)),
             jax.ShapeDtypeStruct((PLANE, tokens), jnp.int32),
             jax.ShapeDtypeStruct((PLANE, tokens), F32),
             jax.ShapeDtypeStruct((PLANE, tokens), F32),
@@ -187,7 +195,7 @@
         in_specs=[small, small]
         + [pl.BlockSpec((b.shape[0], COLS), lambda i: (0, i)) for b in blocks],
         out_specs=pl.BlockSpec((rows, COLS), lambda i: (0, i)),
-        out_shape=jax.ShapeDtypeStruct((rows, D), BF),
+        out_shape=far_memory((rows, D)),
         scratch_shapes=[pltpu.VMEM((rows, tokens), BF), pltpu.VMEM((tokens, COLS), BF)],
         compiler_params=params(),
         cost_estimate=cost(2 * rows * tokens * D, 2 * D * (rows + tokens)),
@@ -237,11 +245,11 @@
         grid=(rows // tile,),
         in_specs=[pl.BlockSpec((tile, D), lambda i: (i, 0)), resident()],
         out_specs=pl.BlockSpec((tile, 2 * FF), lambda i: (i, 0)),
-        out_shape=jax.ShapeDtypeStruct((rows, 2 * FF), F32),
+        out_shape=far_memory((rows, 2 * FF), F32),
         compiler_params=params(),
         cost_estimate=cost(4 * rows * D * FF, 2 * D * (rows + 2 * FF)),
         name="expert_forward",
-    )(x, joined)
+    )(*pinned(x), joined)
 
 
 def backward_body(per_dest, gate_row, sc_ref, p_ref, w_ref, wd_ref, rows_ref, d_ref, h_ref):
@@ -289,14 +297,14 @@
         ],
         out_specs=[wide, pl.BlockSpec((tile, 2 * FF), lambda i: (i, 0)), slim],
         out_shape=[
-            jax.ShapeDtypeStruct((rows, D), BF),
-            jax.ShapeDtypeStruct((rows, 2 * FF), BF),
-            jax.ShapeDtypeStruct((rows, FF), BF),
+            far_memory((rows, D)),
+            far_memory((rows, 2 * FF)),
+            far_memory((rows, FF)),
         ],
         compiler_params=params(),
         cost_estimate=cost(6 * rows * D * FF, 4 * D * rows + 6 * D * FF),
         name="expert_backward",
-    )(scaled, pre, joined, down)
+    )(*pinned(scaled, pre), joined, down)
 
 
 def weight_grad_body(sec_ref, xn, xf, sn, sf, dn, df, hn, hf, sent_ref, kept_ref):
@@ -335,7 +343,7 @@
             else:
                 specs.append(pl.BlockSpec(v.shape, lambda i, sec: (0, 0)))
     rows = near[0].shape[0] + far[0].shape[0]
-    out = jax.ShapeDtypeStruct((2, 3, tile, FF), BF)
+    out = far_memory((2, 3, tile, FF))
     return pl.pallas_call(
         weight_grad_body,
         grid_spec=pltpu.PrefetchScalarGridSpec(
@@ -351,16 +359,24 @@
         compiler_params=params(),
         cost_estimate=cost(6 * rows * D * FF, 4 * rows * D + 6 * D * FF),
         name="weight_grads",
-    )(section, *args)
-
-
-def section_mean(sent, kept):
+    )(section, *pinned(*args))
+
+
+def section_mean(sent, kept, back):
     other_core = [(s, s ^ 1) for s in range(4)]
     other_chip = [(s, s ^ 2) for s in range(4)]
     got = lax.ppermute(sent, "section", other_core)
     onward = added(kept[1], got[1])
-    last = lax.ppermute(onward, "section", other_chip)
-    total = kept[0].astype(F32) + got[0].astype(F32) + last.astype(F32)
+    onward, back = ordered(onward, back)
+    half = onward.shape[1] // 2
+    first = lax.ppermute(onward[:, :half], "section", other_chip)
+    second = lax.ppermute(onward[:, half:], "section", other_chip)
+    return (kept[0], got[0], first, second), back
+
+
+def mean_of(own, core, first, second):
+    chip = jnp.concatenate([first, second], axis=1)
+    total = own.astype(F32) + core.astype(F32) + chip.astype(F32)
     return (total / 4.0)[:, None]
 
 
@@ -434,7 +450,7 @@
             pl.BlockSpec((rows, COLS), lambda i: (0, i)),
         ],
         out_specs=[pl.BlockSpec((n, COLS), lambda i: (0, i)) for n in sizes],
-        out_shape=[jax.ShapeDtypeStruct((n, D), BF) for n in sizes],
+        out_shape=[far_memory((n, D)) for n in sizes],
         scratch_shapes=[pltpu.VMEM((rows, tokens), BF)],
         compiler_params=params(),
         cost_estimate=cost(2 * rows * tokens * D, 2 * D * (rows + tokens)),
@@ -508,13 +524,16 @@
     back_n = exchange(rows_n, NEAR_ROWS)
 
     sent, kept = weight_grad(section, (xn, sn, dn, hn), (xf, sf, df, hf))
+    (mine, core, first, second), back_f = section_mean(sent, kept, back_f)
     far_sizes = [ROWS] * 4 + [HALF, HALF + META]
-    far_parts = combine(z, qf, wf, rf, back_f, far_sizes, FAR_ROWS, len(FAR), far_gate)
+    far_parts = list(combine(z, qf, wf, rf, back_f, far_sizes, FAR_ROWS, len(FAR), far_gate))
+    far_parts[3], first = ordered(far_parts[3], first)
+    far_parts[1], second = ordered(far_parts[1], second)
     near_parts = combine(z, qn, wn, rn, back_n, [ROWS] * 3, NEAR_ROWS, len(NEAR), near_gate)
     total = ring_scatter(near_parts, far_parts)
     token_grads = total[:TOK].astype(BF)[None]
     gate_grads = total[TOK:, :TOK].T.astype(BF)[None]
-    return token_grads, gate_grads, section_mean(sent, kept)
+    return token_grads, gate_grads, mean_of(mine, core, first, second)
 
 
 def solution(mesh):

time: 313 us -> 302 us (0.965)
  local copies, waits for them, and re-layouts: 32.8 us -> 10.2 us
  Pallas kernels: 47.8 us -> 59.5 us
  starting transfers between devices: 63.9 us -> 59.3 us
  waiting for transfers between devices: 155 us -> 159 us
    unnamed x72 -> x28, local copies, waits for them, and re-layouts: 31.4 us -> 7.58 us
    all_to_all x6, waiting for transfers between devices: 52.6 us -> 46.3 us  [exchange(): lax.all_to_all(sent, ('section', 'expert'), 0, 0, axis_index_groups=plane...]
    ppermute x1, waiting for transfers between devices: 0.01 us -> 5.13 us  [ring_scatter(): behind = lax.ppermute(behind, 'expert', bw)]
    pallas_call x2, Pallas kernels: 4.55 us -> 9.6 us  [forward(): pl.pallas_call(forward_body, grid=(rows // tile,), in_specs=[pl.BlockSpec...]
    ppermute x1, waiting for transfers between devices: 0.01 us -> 4.74 us  [section_mean(): got = lax.ppermute(sent, 'section', other_core)]
    ppermute x1, waiting for transfers between devices: 4.37 us -> 0.01 us  [ring_scatter(): low = lax.ppermute(far[-1], 'expert', bw)]
    ppermute x1, waiting for transfers between devices: 0.01 us -> 4.3 us  [ring_scatter(): ahead = lax.ppermute(ahead, 'expert', fw)]
    ppermute x2, starting transfers between devices: 7.46 us -> 3.29 us  [ring_scatter(): behind = added(part[-step], lax.ppermute(behind, 'expert', bw))]
  transfers between devices with their start and end apart: 32 -> 33, of which waited for: 21 -> 23; matrix products, arithmetic and copies ran while one was open for 3% -> 4% of each run, Pallas kernels for 12% -> 14%
where the time goes in v3:
time: 302 us; the launch traced here: 301 us
  waiting for transfers between devices  159 us (53%)
  Pallas kernels  59.5 us (20%)
  starting transfers between devices  59.3 us (20%)
  other arithmetic  11.7 us (4%)
  local copies, waits for them, and re-layouts  10.2 us (3%)
    ppermute x6, waiting for transfers between devices, ring_gather(): up = lax.ppermute(up, 'expert', bw)  58.7 us
    all_to_all x6, waiting for transfers between devices, exchange(): lax.all_to_all(sent, ('section', 'expert'), 0, 0, axis_index_groups=plane...  46.3 us
    all_to_all x6, starting transfers between devices, exchange(): lax.all_to_all(sent, ('section', 'expert'), 0, 0, axis_index_groups=plane...  28.1 us
    pallas_call x2, Pallas kernels, backward(): pl.pallas_call(functools.partial(backward_body, per_dest, gate_row), grid...  14.2 us
    pallas_call x1, Pallas kernels, weight_grad(): pl.pallas_call(weight_grad_body, grid_spec=pltpu.PrefetchScalarGridSpec(n...  12.7 us
    pallas_call x2, Pallas kernels, forward(): pl.pallas_call(forward_body, grid=(rows // tile,), in_specs=[pl.BlockSpec...  9.6 us
    convert_element_type x7, other arithmetic, added(): return (a.astype(F32) + b.astype(F32)).astype(BF)  9.55 us
    ppermute x2, waiting for transfers between devices, ring_gather(): top = lax.ppermute(down[:HALF], 'expert', fw)  8.74 us
  transfers between devices with their start and end apart: 33, of which 23 were waited for; matrix products, arithmetic and copies ran while one was open for 4% of the time, Pallas kernels for 14%

profile of v3, /device:TPU:8, one launch (start us, length us, event | category | flops | bytes accessed | tf_op | source)
XLA Modules:
  0.0 301.0 jit_solution(12182607817676290224)
XLA Ops:
  3.1 5.9 %collective-permute-start.1 = (bf16[136,2048]{1,0:T(8,128)(2,1)S(1)}, bf16[136,2048]{1,0:T(8,128)(2,1)}, u32[]{:S(2)}, u32[]{:S(2)}) collective-permute-start(bf16[136,2048]{1,0:T(8,128)(2,1)S(1)} %pack_rows.1.refs_0_), channel_id=1, source_target_pairs={{0,56},{1,57},{2,58},{3,59},{4,60},{5,61},{6,62},{7,63},{8,0},{9,1... | collective-permute-start | bytes 1671176 | tf_op jit(solution)/shard_map/ppermute | solution.py:467
  9.0 11.9 %collective-permute-done.1.refs_2_ = bf16[136,2048]{1,0:T(8,128)(2,1)} collective-permute-done((bf16[136,2048]{1,0:T(8,128)(2,1)S(1)}, bf16[136,2048]{1,0:T(8,128)(2,1)}, u32[]{:S(2)}, u32[]{:S(2)}) %collective-permute-start.1) | collective-permute-done | bytes 557088 | tf_op jit(solution)/shard_map/ppermute | solution.py:467
  24.3 3.5 %select_tokens.2 = (bf16[448,2048]{1,0:T(8,128)(2,1)}, s32[8,384]{1,0:T(8,128)S(1)}, f32[8,384]{1,0:T(8,128)S(1)}, f32[8,384]{1,0:T(8,128)S(1)}) custom-call(s32[1]{0:T(128)} %bitcast.z_ref, bf16[136,2048]{1,0:T(8,128)(2,1)S(1)} %pack_rows.1.refs_0_, bf16[136,2048]{1,0:T(8,128)(2,1)S(1)} %collective-permute-done.refs_1_, ...), custom_call_target="tpu_custom_call" | custom-call | flops 704643072 | bytes 3407872 | tf_op jit(solution)/shard_map/select_tokens/pallas_call | solution.py:151
  27.8 5.4 %all-to-all-start = ((bf16[8,56,2048]{2,1,0:T(8,128)(2,1)}), bf16[8,56,2048]{2,1,0:T(8,128)(2,1)}, u32[]{:S(2)}, u32[]{:S(2)}) async-start(bf16[8,56,2048]{2,1,0:T(8,128)(2,1)} %bitcast.53), calls=%async_computation | async-start | bytes 3670016 | tf_op jit(solution)/shard_map/all_to_all | solution.py:74
  37.4 10.8 %collective-permute-done.3.refs_2_ = bf16[128,2048]{1,0:T(8,128)(2,1)S(1)} collective-permute-done((bf16[128,2048]{1,0:T(8,128)(2,1)S(1)}, bf16[128,2048]{1,0:T(8,128)(2,1)S(1)}, u32[]{:S(2)}, u32[]{:S(2)}) %collective-permute-start.3) | collective-permute-done | bytes 524320 | tf_op jit(solution)/shard_map/ppermute | solution.py:467
  52.3 5.2 %collective-permute-done.5.refs_1_ = bf16[136,2048]{1,0:T(8,128)(2,1)S(1)} collective-permute-done((bf16[136,2048]{1,0:T(8,128)(2,1)}, bf16[136,2048]{1,0:T(8,128)(2,1)S(1)}, u32[]{:S(2)}, u32[]{:S(2)}) %collective-permute-start.5) | collective-permute-done | bytes 557088 | tf_op jit(solution)/shard_map/ppermute | solution.py:467
  59.1 5.3 %all-to-all-start.1 = ((bf16[8,56,2048]{2,1,0:T(8,128)(2,1)}), bf16[8,56,2048]{2,1,0:T(8,128)(2,1)}, u32[]{:S(2)}, u32[]{:S(2)}) async-start(bf16[8,56,2048]{2,1,0:T(8,128)(2,1)} %bitcast.48), calls=%async_computation.1 | async-start | bytes 3670016 | tf_op jit(solution)/shard_map/all_to_all | solution.py:74
  66.5 10.6 %collective-permute-done.7.refs_3_ = bf16[136,2048]{1,0:T(8,128)(2,1)S(1)} collective-permute-done((bf16[136,2048]{1,0:T(8,128)(2,1)S(1)}, bf16[136,2048]{1,0:T(8,128)(2,1)S(1)}, u32[]{:S(2)}, u32[]{:S(2)}) %collective-permute-start.7) | collective-permute-done | bytes 557088 | tf_op jit(solution)/shard_map/ppermute | solution.py:467
  79.3 6.9 %collective-permute-done.8.refs_4_ = bf16[64,2048]{1,0:T(8,128)(2,1)S(1)} collective-permute-done((bf16[64,2048]{1,0:T(8,128)(2,1)S(1)}, bf16[64,2048]{1,0:T(8,128)(2,1)S(1)}, u32[]{:S(2)}, u32[]{:S(2)}) %collective-permute-start.8) | collective-permute-done | bytes 262176 | tf_op jit(solution)/shard_map/ppermute | solution.py:469
  86.2 4.8 %select_tokens.3 = (bf16[768,2048]{1,0:T(8,128)(2,1)}, s32[8,640]{1,0:T(8,128)S(1)}, f32[8,640]{1,0:T(8,128)S(1)}, f32[8,640]{1,0:T(8,128)S(1)}) custom-call(s32[1]{0:T(128)} %bitcast.z_ref, bf16[136,2048]{1,0:T(8,128)(2,1)S(1)} %collective-permute-done.4.refs_0_, bf16[136,2048]{1,0:T(8,128)(2,1)S(1)} %collective-permute-done.5.refs_1_, ...), custom_call_target="tpu_custom_call" | custom-call | flops 2013265920 | bytes 5767168 | tf_op jit(solution)/shard_map/select_tokens/pallas_call | solution.py:151
  91.0 5.3 %all-to-all-start.2 = ((bf16[8,96,2048]{2,1,0:T(8,128)(2,1)}), bf16[8,96,2048]{2,1,0:T(8,128)(2,1)}, u32[]{:S(2)}, u32[]{:S(2)}) async-start(bf16[8,96,2048]{2,1,0:T(8,128)(2,1)} %bitcast.49), calls=%async_computation.2 | async-start | bytes 6291456 | tf_op jit(solution)/shard_map/all_to_all | solution.py:74
  98.3 10.3 %collective-permute-done.11.refs_1_ = bf16[128,2048]{1,0:T(8,128)(2,1)S(1)} collective-permute-done((bf16[128,2048]{1,0:T(8,128)(2,1)S(1)}, bf16[128,2048]{1,0:T(8,128)(2,1)S(1)}, u32[]{:S(2)}, u32[]{:S(2)}) %collective-permute-start.11) | collective-permute-done | bytes 524320 | tf_op jit(solution)/shard_map/ppermute | solution.py:467
  110.6 10.0 %collective-permute-done.13.refs_3_ = bf16[128,2048]{1,0:T(8,128)(2,1)S(1)} collective-permute-done((bf16[128,2048]{1,0:T(8,128)(2,1)S(1)}, bf16[128,2048]{1,0:T(8,128)(2,1)S(1)}, u32[]{:S(2)}, u32[]{:S(2)}) %collective-permute-start.13) | collective-permute-done | bytes 524320 | tf_op jit(solution)/shard_map/ppermute | solution.py:467
  122.8 4.2 %collective-permute-done.15.refs_5_ = bf16[64,2048]{1,0:T(8,128)(2,1)S(1)} collective-permute-done((bf16[64,2048]{1,0:T(8,128)(2,1)S(1)}, bf16[64,2048]{1,0:T(8,128)(2,1)S(1)}, u32[]{:S(2)}, u32[]{:S(2)}) %collective-permute-start.15) | collective-permute-done | bytes 262176 | tf_op jit(solution)/shard_map/ppermute | solution.py:470
  128.9 4.5 %select_cotangents.3 = bf16[768,2048]{1,0:T(8,128)(2,1)} custom-call(s32[8,640]{1,0:T(8,128)S(1)} %get-tuple-element.61.q_ref, f32[8,640]{1,0:T(8,128)S(1)} %get-tuple-element.62.w_ref, bf16[128,2048]{1,0:T(8,128)(2,1)S(1)} %collective-permute-done.10.refs_0_, bf16[128,2048]{1,0:T(8,128)(2,1)S(1)} %collective-permute-done.11.refs_1_, ...), custom_call_target="tpu_custom_call" | custom-call | flops 2013265920 | bytes 5767168 | tf_op jit(solution)/shard_map/select_cotangents/pallas_call | solution.py:192
  135.3 4.8 %all-to-all-start.3 = ((bf16[8,96,2048]{2,1,0:T(8,128)(2,1)}), bf16[8,96,2048]{2,1,0:T(8,128)(2,1)}, u32[]{:S(2)}, u32[]{:S(2)}) async-start(bf16[8,96,2048]{2,1,0:T(8,128)(2,1)} %bitcast.50), calls=%async_computation.3 | async-start | bytes 6291456 | tf_op jit(solution)/shard_map/all_to_all | solution.py:74
  142.9 4.4 %expert_forward.2.p_ref = f32[448,768]{1,0:T(8,128)} custom-call(bf16[448,2048]{1,0:T(8,128)(2,1)} %bitcast.8.x_ref.xn, bf16[2048,768]{1,0:T(8,128)(2,1)S(1)} %get-tuple-element.69.w_ref), custom_call_target="tpu_custom_call" | custom-call | flops 1409286144 | bytes 4980736 | tf_op jit(solution)/shard_map/expert_forward/pallas_call | solution.py:243
  147.3 6.1 %expert_backward.2 = (bf16[448,2048]{1,0:T(8,128)(2,1)}, bf16[448,768]{1,0:T(8,128)(2,1)}, bf16[448,384]{1,0:T(8,128)(2,1)}) custom-call(bf16[448,2048]{1,0:T(8,128)(2,1)} %bitcast.10.sc_ref.sn, f32[448,768]{1,0:T(8,128)} %expert_forward.2.p_ref, bf16[2048,768]{1,0:T(8,128)(2,1)S(1)} %get-tuple-element.69.w_ref, bf16[2048,384]{1,0:T(8,128)(2,1)S(1)} %get-tuple-element.70.wd_ref), custom_call_target="tpu_custom_call" | custom-call | flops 2113929216 | bytes 8388608 | tf_op jit(solution)/shard_map/expert_backward/pallas_call | solution.py:289
  153.4 5.2 %expert_forward.3.p_ref = f32[768,768]{1,0:T(8,128)} custom-call(bf16[768,2048]{1,0:T(8,128)(2,1)} %bitcast.12.x_ref.xf, bf16[2048,768]{1,0:T(8,128)(2,1)S(1)} %get-tuple-element.69.w_ref), custom_call_target="tpu_custom_call" | custom-call | flops 2415919104 | bytes 6291456 | tf_op jit(solution)/shard_map/expert_forward/pallas_call | solution.py:243
  158.6 23.0 %all-to-all-done.3 = bf16[8,96,2048]{2,1,0:T(8,128)(2,1)} async-done(((bf16[8,96,2048]{2,1,0:T(8,128)(2,1)}), bf16[8,96,2048]{2,1,0:T(8,128)(2,1)}, u32[]{:S(2)}, u32[]{:S(2)}) %all-to-all-start.3) | async-done | bytes 3145760 | tf_op jit(solution)/shard_map/all_to_all | solution.py:74
  183.0 8.1 %expert_backward.3 = (bf16[768,2048]{1,0:T(8,128)(2,1)}, bf16[768,768]{1,0:T(8,128)(2,1)}, bf16[768,384]{1,0:T(8,128)(2,1)}) custom-call(bf16[768,2048]{1,0:T(8,128)(2,1)} %bitcast.14.sc_ref.sf, f32[768,768]{1,0:T(8,128)} %expert_forward.3.p_ref, bf16[2048,768]{1,0:T(8,128)(2,1)S(1)} %get-tuple-element.69.w_ref, bf16[2048,384]{1,0:T(8,128)(2,1)S(1)} %copy-done.2), custom_call_target="tpu_custom_call" | custom-call | flops 3623878656 | bytes 11010048 | tf_op jit(solution)/shard_map/expert_backward/pallas_call | solution.py:289
  191.1 3.6 %all-to-all-start.4 = ((bf16[8,96,2048]{2,1,0:T(8,128)(2,1)}), bf16[8,96,2048]{2,1,0:T(8,128)(2,1)S(1)}, u32[]{:S(2)}, u32[]{:S(2)}) async-start(bf16[8,96,2048]{2,1,0:T(8,128)(2,1)} %bitcast.51), calls=%async_computation.4 | async-start | bytes 6291456 | tf_op jit(solution)/shard_map/all_to_all | solution.py:74
  194.8 12.7 %weight_grads.1 = (bf16[2,3,512,384]{3,2,1,0:T(8,128)(2,1)}, bf16[2,3,512,384]{3,2,1,0:T(8,128)(2,1)}) custom-call(s32[1]{0:T(128)} %bitcast.19.sec_ref, bf16[448,2048]{1,0:T(8,128)(2,1)} %bitcast.8.x_ref.xn, bf16[768,2048]{1,0:T(8,128)(2,1)} %bitcast.12.x_ref.xf, bf16[448,2048]{1,0:T(8,128)(2,1)} %bitcast.10.sc_ref.sn, ...), custom_call_target="tpu_custom_call" | custom-call | flops 5737807872 | bytes 14680064 | tf_op jit(solution)/shard_map/weight_grads/pallas_call | solution.py:347
  207.5 4.7 %collective-permute-done.16 = bf16[2,3,512,384]{3,2,1,0:T(8,128)(2,1)S(1)} collective-permute-done((bf16[2,3,512,384]{3,2,1,0:T(8,128)(2,1)}, bf16[2,3,512,384]{3,2,1,0:T(8,128)(2,1)S(1)}, u32[]{:S(2)}, u32[]{:S(2)}) %collective-permute-start.16) | collective-permute-done | bytes 2359328 | tf_op jit(solution)/shard_map/ppermute | solution.py:368
  216.3 21.3 %all-to-all-done.4 = bf16[8,96,2048]{2,1,0:T(8,128)(2,1)S(1)} async-done(((bf16[8,96,2048]{2,1,0:T(8,128)(2,1)}), bf16[8,96,2048]{2,1,0:T(8,128)(2,1)S(1)}, u32[]{:S(2)}, u32[]{:S(2)}) %all-to-all-start.4) | async-done | bytes 3145760 | tf_op jit(solution)/shard_map/all_to_all | solution.py:74
  237.6 4.5 %combine_rows.3 = (bf16[136,2048]{1,0:T(8,128)(2,1)}, bf16[136,2048]{1,0:T(8,128)(2,1)}, bf16[136,2048]{1,0:T(8,128)(2,1)}, bf16[136,2048]{1,0:T(8,128)(2,1)}, b...) custom-call(s32[1]{0:T(128)} %bitcast.z_ref, s32[8,640]{1,0:T(8,128)S(1)} %get-tuple-element.61.q_ref, ...), custom_call_target="tpu_custom_call" | custom-call | flops 2013265920 | bytes 5767168 | tf_op jit(solution)/shard_map/combine_rows/pallas_call | solution.py:442
  245.4 3.6 %all-to-all-start.5 = ((bf16[8,56,2048]{2,1,0:T(8,128)(2,1)}), bf16[8,56,2048]{2,1,0:T(8,128)(2,1)S(1)}, u32[]{:S(2)}, u32[]{:S(2)}) async-start(bf16[8,56,2048]{2,1,0:T(8,128)(2,1)} %bitcast.52), calls=%async_computation.5 | async-start | bytes 3670016 | tf_op jit(solution)/shard_map/all_to_all | solution.py:74
  254.8 6.3 %collective-permute-done.18 = bf16[3,256,384]{2,1,0:T(8,128)(2,1)S(1)} collective-permute-done((bf16[3,256,384]{2,1,0:T(8,128)(2,1)}, bf16[3,256,384]{2,1,0:T(8,128)(2,1)S(1)}, u32[]{:S(2)}, u32[]{:S(2)}) %collective-permute-start.18) | collective-permute-done | bytes 589856 | tf_op jit(solution)/shard_map/ppermute | solution.py:372
  263.0 7.4 %collective-permute-done.17 = bf16[3,256,384]{2,1,0:T(8,128)(2,1)S(1)} collective-permute-done((bf16[3,256,384]{2,1,0:T(8,128)(2,1)}, bf16[3,256,384]{2,1,0:T(8,128)(2,1)S(1)}, u32[]{:S(2)}, u32[]{:S(2)}) %collective-permute-start.17) | collective-permute-done | bytes 589856 | tf_op jit(solution)/shard_map/ppermute | solution.py:373
  277.2 5.9 %collective-permute-done.25 = bf16[136,2048]{1,0:T(8,128)(2,1)} collective-permute-done((bf16[136,2048]{1,0:T(8,128)(2,1)}, bf16[136,2048]{1,0:T(8,128)(2,1)}, u32[]{:S(2)}, u32[]{:S(2)}) %collective-permute-start.25) | collective-permute-done | bytes 557088 | tf_op jit(solution)/shard_map/ppermute | solution.py:489
  289.9 5.1 %collective-permute-done.26 = bf16[136,2048]{1,0:T(8,128)(2,1)S(1)} collective-permute-done((bf16[136,2048]{1,0:T(8,128)(2,1)S(1)}, bf16[136,2048]{1,0:T(8,128)(2,1)S(1)}, u32[]{:S(2)}, u32[]{:S(2)}) %collective-permute-start.26) | collective-permute-done | bytes 557088 | tf_op jit(solution)/shard_map/ppermute | solution.py:491
  295.1 4.3 %collective-permute-done.22 = bf16[136,2048]{1,0:T(8,128)(2,1)S(1)} collective-permute-done((bf16[136,2048]{1,0:T(8,128)(2,1)S(1)}, bf16[136,2048]{1,0:T(8,128)(2,1)S(1)}, u32[]{:S(2)}, u32[]{:S(2)}) %collective-permute-start.22) | collective-permute-done | bytes 557088 | tf_op jit(solution)/shard_map/ppermute | solution.py:490
  (91 shorter events, 64.4 us)
Async XLA Ops:
  3.1 17.8 %collective-permute-start.1 = (bf16[136,2048]{1,0:T(8,128)(2,1)S(1)}, bf16[136,2048]{1,0:T(8,128)(2,1)}, u32[]{:S(2)}, u32[]{:S(2)}) collective-permute-start(bf16[136,2048]{1,0:T(8,128)(2,1)S(1)} %pack_rows.1.refs_0_), channel_id=1, source_target_pairs={{0,56},{1,57},{2,58},{3,59},{4,60},{5,61},{6,62},{7,63},{8,0},{9,1... | collective-permute-start | bytes 1671176 | tf_op jit(solution)/shard_map/ppermute | solution.py:467
  9.0 15.3 %collective-permute-start = (bf16[136,2048]{1,0:T(8,128)(2,1)S(1)}, bf16[136,2048]{1,0:T(8,128)(2,1)S(1)}, u32[]{:S(2)}, u32[]{:S(2)}) collective-permute-start(bf16[136,2048]{1,0:T(8,128)(2,1)S(1)} %pack_rows.1.refs_0_), channel_id=1, source_target_pairs={{0,8},{1,9},{2,10},{3,11},{4,12},{5,13},{6,14},{7,15},{8,16},{9,17... | collective-permute-start | bytes 1671176 | tf_op jit(solution)/shard_map/ppermute | solution.py:466
  27.8 31.3 %all-to-all-start = ((bf16[8,56,2048]{2,1,0:T(8,128)(2,1)}), bf16[8,56,2048]{2,1,0:T(8,128)(2,1)}, u32[]{:S(2)}, u32[]{:S(2)}) async-start(bf16[8,56,2048]{2,1,0:T(8,128)(2,1)} %bitcast.53), calls=%async_computation | async-start | bytes 3670016 | tf_op jit(solution)/shard_map/all_to_all | solution.py:74
  33.3 14.9 %collective-permute-start.3 = (bf16[128,2048]{1,0:T(8,128)(2,1)S(1)}, bf16[128,2048]{1,0:T(8,128)(2,1)S(1)}, u32[]{:S(2)}, u32[]{:S(2)}) collective-permute-start(bf16[128,2048]{1,0:T(8,128)(2,1)S(1)} %bitcast.43), channel_id=1, source_target_pairs={{0,56},{1,57},{2,58},{3,59},{4,60},{5,61},{6,62},{7,63},{8,0},{9,1... | collective-permute-start | bytes 1572872 | tf_op jit(solution)/shard_map/ppermute | solution.py:467
  33.7 16.1 %collective-permute-start.2 = (bf16[128,2048]{1,0:T(8,128)(2,1)S(1)}, bf16[128,2048]{1,0:T(8,128)(2,1)S(1)}, u32[]{:S(2)}, u32[]{:S(2)}) collective-permute-start(bf16[128,2048]{1,0:T(8,128)(2,1)S(1)} %bitcast.44), channel_id=1, source_target_pairs={{0,8},{1,9},{2,10},{3,11},{4,12},{5,13},{6,14},{7,15},{8,16},{9,17... | collective-permute-start | bytes 1572872 | tf_op jit(solution)/shard_map/ppermute | solution.py:466
  35.4 22.1 %collective-permute-start.5 = (bf16[136,2048]{1,0:T(8,128)(2,1)}, bf16[136,2048]{1,0:T(8,128)(2,1)S(1)}, u32[]{:S(2)}, u32[]{:S(2)}) collective-permute-start(bf16[136,2048]{1,0:T(8,128)(2,1)} %collective-permute-done.1.refs_2_), channel_id=1, source_target_pairs={{0,56},{1,57},{2,58},{3,59},{4,60},{5,61},{6,62},{7,63},{8,0},{9,1... | collective-permute-start | bytes 1671176 | tf_op jit(solution)/shard_map/ppermute | solution.py:467
  37.0 22.1 %collective-permute-start.4 = (bf16[136,2048]{1,0:T(8,128)(2,1)S(1)}, bf16[136,2048]{1,0:T(8,128)(2,1)S(1)}, u32[]{:S(2)}, u32[]{:S(2)}) collective-permute-start(bf16[136,2048]{1,0:T(8,128)(2,1)S(1)} %collective-permute-done.refs_1_), channel_id=1, source_target_pairs={{0,8},{1,9},{2,10},{3,11},{4,12},{5,13},{6,14},{7,15},{8,16},{9,17... | collective-permute-start | bytes 1671176 | tf_op jit(solution)/shard_map/ppermute | solution.py:466
  59.1 31.9 %all-to-all-start.1 = ((bf16[8,56,2048]{2,1,0:T(8,128)(2,1)}), bf16[8,56,2048]{2,1,0:T(8,128)(2,1)}, u32[]{:S(2)}, u32[]{:S(2)}) async-start(bf16[8,56,2048]{2,1,0:T(8,128)(2,1)} %bitcast.48), calls=%async_computation.1 | async-start | bytes 3670016 | tf_op jit(solution)/shard_map/all_to_all | solution.py:74
  64.5 12.6 %collective-permute-start.7 = (bf16[136,2048]{1,0:T(8,128)(2,1)S(1)}, bf16[136,2048]{1,0:T(8,128)(2,1)S(1)}, u32[]{:S(2)}, u32[]{:S(2)}) collective-permute-start(bf16[136,2048]{1,0:T(8,128)(2,1)S(1)} %collective-permute-done.5.refs_1_), channel_id=1, source_target_pairs={{0,56},{1,57},{2,58},{3,59},{4,60},{5,61},{6,62},{7,63},{8,0},{9,1... | collective-permute-start | bytes 1671176 | tf_op jit(solution)/shard_map/ppermute | solution.py:467
  64.8 13.7 %collective-permute-start.6 = (bf16[136,2048]{1,0:T(8,128)(2,1)S(1)}, bf16[136,2048]{1,0:T(8,128)(2,1)S(1)}, u32[]{:S(2)}, u32[]{:S(2)}) collective-permute-start(bf16[136,2048]{1,0:T(8,128)(2,1)S(1)} %collective-permute-done.4.refs_0_), channel_id=1, source_target_pairs={{0,8},{1,9},{2,10},{3,11},{4,12},{5,13},{6,14},{7,15},{8,16},{9,17... | collective-permute-start | bytes 1671176 | tf_op jit(solution)/shard_map/ppermute | solution.py:466
  77.1 9.1 %collective-permute-start.9 = (bf16[72,2048]{1,0:T(8,128)(2,1)S(1)}, bf16[72,2048]{1,0:T(8,128)(2,1)S(1)}, u32[]{:S(2)}, u32[]{:S(2)}) collective-permute-start(bf16[72,2048]{1,0:T(8,128)(2,1)S(1)} %slice.51), channel_id=1, source_target_pairs={{0,56},{1,57},{2,58},{3,59},{4,60},{5,61},{6,62},{7,63},{8,0},{9,1... | collective-permute-start | bytes 884744 | tf_op jit(solution)/shard_map/ppermute | solution.py:470
  78.5 7.7 %collective-permute-start.8 = (bf16[64,2048]{1,0:T(8,128)(2,1)S(1)}, bf16[64,2048]{1,0:T(8,128)(2,1)S(1)}, u32[]{:S(2)}, u32[]{:S(2)}) collective-permute-start(bf16[64,2048]{1,0:T(8,128)(2,1)S(1)} %slice.50), channel_id=1, source_target_pairs={{0,8},{1,9},{2,10},{3,11},{4,12},{5,13},{6,14},{7,15},{8,16},{9,17... | collective-permute-start | bytes 786440 | tf_op jit(solution)/shard_map/ppermute | solution.py:469
  91.0 44.3 %all-to-all-start.2 = ((bf16[8,96,2048]{2,1,0:T(8,128)(2,1)}), bf16[8,96,2048]{2,1,0:T(8,128)(2,1)}, u32[]{:S(2)}, u32[]{:S(2)}) async-start(bf16[8,96,2048]{2,1,0:T(8,128)(2,1)} %bitcast.49), calls=%async_computation.2 | async-start | bytes 6291456 | tf_op jit(solution)/shard_map/all_to_all | solution.py:74
  96.2 12.4 %collective-permute-start.11 = (bf16[128,2048]{1,0:T(8,128)(2,1)S(1)}, bf16[128,2048]{1,0:T(8,128)(2,1)S(1)}, u32[]{:S(2)}, u32[]{:S(2)}) collective-permute-start(bf16[128,2048]{1,0:T(8,128)(2,1)S(1)} %collective-permute-done.3.refs_2_), channel_id=1, source_target_pairs={{0,56},{1,57},{2,58},{3,59},{4,60},{5,61},{6,62},{7,63},{8,0},{9,1... | collective-permute-start | bytes 1572872 | tf_op jit(solution)/shard_map/ppermute | solution.py:467
  96.5 12.1 %collective-permute-start.10 = (bf16[128,2048]{1,0:T(8,128)(2,1)S(1)}, bf16[128,2048]{1,0:T(8,128)(2,1)S(1)}, u32[]{:S(2)}, u32[]{:S(2)}) collective-permute-start(bf16[128,2048]{1,0:T(8,128)(2,1)S(1)} %collective-permute-done.2.refs_1_), channel_id=1, source_target_pairs={{0,8},{1,9},{2,10},{3,11},{4,12},{5,13},{6,14},{7,15},{8,16},{9,17... | collective-permute-start | bytes 1572872 | tf_op jit(solution)/shard_map/ppermute | solution.py:466
  108.6 12.0 %collective-permute-start.13 = (bf16[128,2048]{1,0:T(8,128)(2,1)S(1)}, bf16[128,2048]{1,0:T(8,128)(2,1)S(1)}, u32[]{:S(2)}, u32[]{:S(2)}) collective-permute-start(bf16[128,2048]{1,0:T(8,128)(2,1)S(1)} %collective-permute-done.11.refs_1_), channel_id=1, source_target_pairs={{0,56},{1,57},{2,58},{3,59},{4,60},{5,61},{6,62},{7,63},{8,0},{9,1... | collective-permute-start | bytes 1572872 | tf_op jit(solution)/shard_map/ppermute | solution.py:467
  108.6 12.6 %collective-permute-start.12 = (bf16[128,2048]{1,0:T(8,128)(2,1)S(1)}, bf16[128,2048]{1,0:T(8,128)(2,1)S(1)}, u32[]{:S(2)}, u32[]{:S(2)}) collective-permute-start(bf16[128,2048]{1,0:T(8,128)(2,1)S(1)} %collective-permute-done.10.refs_0_), channel_id=1, source_target_pairs={{0,8},{1,9},{2,10},{3,11},{4,12},{5,13},{6,14},{7,15},{8,16},{9,17... | collective-permute-start | bytes 1572872 | tf_op jit(solution)/shard_map/ppermute | solution.py:466
  120.6 6.5 %collective-permute-start.15 = (bf16[64,2048]{1,0:T(8,128)(2,1)S(1)}, bf16[64,2048]{1,0:T(8,128)(2,1)S(1)}, u32[]{:S(2)}, u32[]{:S(2)}) collective-permute-start(bf16[64,2048]{1,0:T(8,128)(2,1)S(1)} %slice.53), channel_id=1, source_target_pairs={{0,56},{1,57},{2,58},{3,59},{4,60},{5,61},{6,62},{7,63},{8,0},{9,1... | collective-permute-start | bytes 786440 | tf_op jit(solution)/shard_map/ppermute | solution.py:470
  121.3 7.7 %collective-permute-start.14 = (bf16[64,2048]{1,0:T(8,128)(2,1)S(1)}, bf16[64,2048]{1,0:T(8,128)(2,1)S(1)}, u32[]{:S(2)}, u32[]{:S(2)}) collective-permute-start(bf16[64,2048]{1,0:T(8,128)(2,1)S(1)} %slice.52), channel_id=1, source_target_pairs={{0,8},{1,9},{2,10},{3,11},{4,12},{5,13},{6,14},{7,15},{8,16},{9,17... | collective-permute-start | bytes 786440 | tf_op jit(solution)/shard_map/ppermute | solution.py:469
  135.3 46.3 %all-to-all-start.3 = ((bf16[8,96,2048]{2,1,0:T(8,128)(2,1)}), bf16[8,96,2048]{2,1,0:T(8,128)(2,1)}, u32[]{:S(2)}, u32[]{:S(2)}) async-start(bf16[8,96,2048]{2,1,0:T(8,128)(2,1)} %bitcast.50), calls=%async_computation.3 | async-start | bytes 6291456 | tf_op jit(solution)/shard_map/all_to_all | solution.py:74
  191.1 46.5 %all-to-all-start.4 = ((bf16[8,96,2048]{2,1,0:T(8,128)(2,1)}), bf16[8,96,2048]{2,1,0:T(8,128)(2,1)S(1)}, u32[]{:S(2)}, u32[]{:S(2)}) async-start(bf16[8,96,2048]{2,1,0:T(8,128)(2,1)} %bitcast.51), calls=%async_computation.4 | async-start | bytes 6291456 | tf_op jit(solution)/shard_map/all_to_all | solution.py:74
  242.1 8.9 %collective-permute-start.23 = (bf16[72,2048]{1,0:T(8,128)(2,1)}, bf16[72,2048]{1,0:T(8,128)(2,1)S(1)}, u32[]{:S(2)}, u32[]{:S(2)}) collective-permute-start(bf16[72,2048]{1,0:T(8,128)(2,1)} %get-tuple-element.98), channel_id=1, source_target_pairs={{0,56},{1,57},{2,58},{3,59},{4,60},{5,61},{6,62},{7,63},{8,0},{9,1... | collective-permute-start | bytes 884744 | tf_op jit(solution)/shard_map/ppermute | solution.py:484
  244.6 16.5 %collective-permute-start.18 = (bf16[3,256,384]{2,1,0:T(8,128)(2,1)}, bf16[3,256,384]{2,1,0:T(8,128)(2,1)S(1)}, u32[]{:S(2)}, u32[]{:S(2)}) collective-permute-start(bf16[3,256,384]{2,1,0:T(8,128)(2,1)} %get-tuple-element.105), channel_id=1, source_target_pairs={{0,128},{64,192},{128,0},{192,64},{1,129},{65,193},{129,1},{193,65... | collective-permute-start | bytes 1769480 | tf_op jit(solution)/shard_map/ppermute | solution.py:372
  245.4 29.0 %all-to-all-start.5 = ((bf16[8,56,2048]{2,1,0:T(8,128)(2,1)}), bf16[8,56,2048]{2,1,0:T(8,128)(2,1)S(1)}, u32[]{:S(2)}, u32[]{:S(2)}) async-start(bf16[8,56,2048]{2,1,0:T(8,128)(2,1)} %bitcast.52), calls=%async_computation.5 | async-start | bytes 3670016 | tf_op jit(solution)/shard_map/all_to_all | solution.py:74
  249.0 12.0 %collective-permute-start.19 = (bf16[64,2048]{1,0:T(8,128)(2,1)}, bf16[64,2048]{1,0:T(8,128)(2,1)S(1)}, u32[]{:S(2)}, u32[]{:S(2)}) collective-permute-start(bf16[64,2048]{1,0:T(8,128)(2,1)} %get-tuple-element.94), channel_id=1, source_target_pairs={{0,8},{1,9},{2,10},{3,11},{4,12},{5,13},{6,14},{7,15},{8,16},{9,17... | collective-permute-start | bytes 786440 | tf_op jit(solution)/shard_map/ppermute | solution.py:483
  249.1 21.3 %collective-permute-start.17 = (bf16[3,256,384]{2,1,0:T(8,128)(2,1)}, bf16[3,256,384]{2,1,0:T(8,128)(2,1)S(1)}, u32[]{:S(2)}, u32[]{:S(2)}) collective-permute-start(bf16[3,256,384]{2,1,0:T(8,128)(2,1)} %get-tuple-element.104), channel_id=1, source_target_pairs={{0,128},{64,192},{128,0},{192,64},{1,129},{65,193},{129,1},{193,65... | collective-permute-start | bytes 1769480 | tf_op jit(solution)/shard_map/ppermute | solution.py:373
  252.2 18.3 %collective-permute-start.24 = (bf16[136,2048]{1,0:T(8,128)(2,1)S(1)}, bf16[136,2048]{1,0:T(8,128)(2,1)S(1)}, u32[]{:S(2)}, u32[]{:S(2)}) collective-permute-start(bf16[136,2048]{1,0:T(8,128)(2,1)S(1)} %add_convert_fusion.4), channel_id=1, source_target_pairs={{0,56},{1,57},{2,58},{3,59},{4,60},{5,61},{6,62},{7,63},{8,0},{9,1... | collective-permute-start | bytes 1671176 | tf_op jit(solution)/shard_map/ppermute | solution.py:489
  262.2 10.8 %collective-permute-start.20 = (bf16[136,2048]{1,0:T(8,128)(2,1)S(1)}, bf16[136,2048]{1,0:T(8,128)(2,1)S(1)}, u32[]{:S(2)}, u32[]{:S(2)}) collective-permute-start(bf16[136,2048]{1,0:T(8,128)(2,1)S(1)} %add_convert_fusion.7), channel_id=1, source_target_pairs={{0,8},{1,9},{2,10},{3,11},{4,12},{5,13},{6,14},{7,15},{8,16},{9,17... | collective-permute-start | bytes 1671176 | tf_op jit(solution)/shard_map/ppermute | solution.py:488
  271.4 11.7 %collective-permute-start.25 = (bf16[136,2048]{1,0:T(8,128)(2,1)}, bf16[136,2048]{1,0:T(8,128)(2,1)}, u32[]{:S(2)}, u32[]{:S(2)}) collective-permute-start(bf16[136,2048]{1,0:T(8,128)(2,1)} %add_convert_fusion.3), channel_id=1, source_target_pairs={{0,56},{1,57},{2,58},{3,59},{4,60},{5,61},{6,62},{7,63},{8,0},{9,1... | collective-permute-start | bytes 1671176 | tf_op jit(solution)/shard_map/ppermute | solution.py:489
  274.0 12.5 %collective-permute-start.21 = (bf16[136,2048]{1,0:T(8,128)(2,1)}, bf16[136,2048]{1,0:T(8,128)(2,1)}, u32[]{:S(2)}, u32[]{:S(2)}) collective-permute-start(bf16[136,2048]{1,0:T(8,128)(2,1)} %add_convert_fusion.6), channel_id=1, source_target_pairs={{0,8},{1,9},{2,10},{3,11},{4,12},{5,13},{6,14},{7,15},{8,16},{9,17... | collective-permute-start | bytes 1671176 | tf_op jit(solution)/shard_map/ppermute | solution.py:488
  284.5 10.6 %collective-permute-start.26 = (bf16[136,2048]{1,0:T(8,128)(2,1)S(1)}, bf16[136,2048]{1,0:T(8,128)(2,1)S(1)}, u32[]{:S(2)}, u32[]{:S(2)}) collective-permute-start(bf16[136,2048]{1,0:T(8,128)(2,1)S(1)} %add_convert_fusion.2), channel_id=1, source_target_pairs={{0,56},{1,57},{2,58},{3,59},{4,60},{5,61},{6,62},{7,63},{8,0},{9,1... | collective-permute-start | bytes 1671176 | tf_op jit(solution)/shard_map/ppermute | solution.py:491
  287.9 11.5 %collective-permute-start.22 = (bf16[136,2048]{1,0:T(8,128)(2,1)S(1)}, bf16[136,2048]{1,0:T(8,128)(2,1)S(1)}, u32[]{:S(2)}, u32[]{:S(2)}) collective-permute-start(bf16[136,2048]{1,0:T(8,128)(2,1)S(1)} %add_convert_fusion.5), channel_id=1, source_target_pairs={{0,8},{1,9},{2,10},{3,11},{4,12},{5,13},{6,14},{7,15},{8,16},{9,17... | collective-permute-start | bytes 1671176 | tf_op jit(solution)/shard_map/ppermute | solution.py:490
  (15 other events, 106.0 us)

commit v4 on v3

--- a/solution.py
+++ b/solution.py
@@ -479,14 +479,12 @@
 
 def ring_scatter(near, far):
     fw, bw = forward_pairs(), backward_pairs()
-    part = dict(zip(NEAR, near)) | dict(zip(FAR[:-1], far[:-2]))
-    top = lax.ppermute(far[-2], "expert", fw)
-    low = lax.ppermute(far[-1], "expert", bw)
-    ahead = added(part[3], jnp.pad(top, ((0, META + HALF), (0, 0))))
-    behind = added(part[-3], jnp.pad(low, ((HALF, 0), (0, 0))))
-    for step in (2, 1):
+    part = dict(zip(NEAR, near)) | dict(zip(FAR, far))
+    ahead, behind = part[4], part[-3]
+    for step in (3, 2, 1):
         ahead = added(part[step], lax.ppermute(ahead, "expert", fw))
-        behind = added(part[-step], lax.ppermute(behind, "expert", bw))
+        if step < 3:
+            behind = added(part[-step], lax.ppermute(behind, "expert", bw))
     ahead = lax.ppermute(ahead, "expert", fw)
     behind = lax.ppermute(behind, "expert", bw)
     return part[0].astype(F32) + ahead.astype(F32) + behind.astype(F32)
@@ -525,7 +523,7 @@
 
     sent, kept = weight_grad(section, (xn, sn, dn, hn), (xf, sf, df, hf))
     (mine, core, first, second), back_f = section_mean(sent, kept, back_f)
-    far_sizes = [ROWS] * 4 + [HALF, HALF + META]
+    far_sizes = [ROWS] * 5
     far_parts = list(combine(z, qf, wf, rf, back_f, far_sizes, FAR_ROWS, len(FAR), far_gate))
     far_parts[3], first = ordered(far_parts[3], first)
     far_parts[1], second = ordered(far_parts[1], second)

time: 302 us -> 300 us (level)
  waiting for transfers between devices: 159 us -> 155 us
    ppermute x2 -> x3, waiting for transfers between devices: 0.91 us -> 14.3 us  [ring_scatter(): ahead = added(part[step], lax.ppermute(ahead, 'expert', fw))]
    ppermute x1, waiting for transfers between devices: 7.45 us -> 0.01 us  [section_mean(): second = lax.ppermute(onward[:, half:], 'section', other_chip)]
    ppermute x1, waiting for transfers between devices: 6.27 us -> 1.72 us  [section_mean(): first = lax.ppermute(onward[:, :half], 'section', other_chip)]
    ppermute x1, waiting for transfers between devices: 5.13 us -> 0.62 us  [ring_scatter(): behind = lax.ppermute(behind, 'expert', bw)]
    ppermute x2, waiting for transfers between devices: 5.93 us -> 1.64 us  [ring_scatter(): behind = added(part[-step], lax.ppermute(behind, 'expert', bw))]
    ppermute x2, starting transfers between devices: 3.29 us -> 6.87 us  [ring_scatter(): behind = added(part[-step], lax.ppermute(behind, 'expert', bw))]
    ppermute x1, waiting for transfers between devices: 4.3 us -> 7.34 us  [ring_scatter(): ahead = lax.ppermute(ahead, 'expert', fw)]
    convert_element_type x7 -> x6, other arithmetic: 9.55 us -> 7.89 us  [added(): return (a.astype(F32) + b.astype(F32)).astype(BF)]
  transfers between devices with their start and end apart: 33 -> 32, of which waited for: 23 -> 24; matrix products, arithmetic and copies ran while one was open for 4% -> 4% of each run, Pallas kernels for 14% -> 16%
where the time goes in v4:
time: 300 us; the launch traced here: 299 us
  waiting for transfers between devices  155 us (52%)
  starting transfers between devices  61 us (20%)
  Pallas kernels  59.5 us (20%)
  local copies, waits for them, and re-layouts  11.5 us (4%)
  other arithmetic  11.1 us (4%)
    ppermute x6, waiting for transfers between devices, ring_gather(): up = lax.ppermute(up, 'expert', bw)  58.7 us
    all_to_all x6, waiting for transfers between devices, exchange(): lax.all_to_all(sent, ('section', 'expert'), 0, 0, axis_index_groups=plane...  46.6 us
    all_to_all x6, starting transfers between devices, exchange(): lax.all_to_all(sent, ('section', 'expert'), 0, 0, axis_index_groups=plane...  28.1 us
    ppermute x3, waiting for transfers between devices, ring_scatter(): ahead = added(part[step], lax.ppermute(ahead, 'expert', fw))  14.3 us
    pallas_call x2, Pallas kernels, backward(): pl.pallas_call(functools.partial(backward_body, per_dest, gate_row), grid...  14.2 us
    pallas_call x1, Pallas kernels, weight_grad(): pl.pallas_call(weight_grad_body, grid_spec=pltpu.PrefetchScalarGridSpec(n...  12.7 us
    pallas_call x2, Pallas kernels, forward(): pl.pallas_call(forward_body, grid=(rows // tile,), in_specs=[pl.BlockSpec...  9.59 us
    ppermute x2, waiting for transfers between devices, ring_gather(): top = lax.ppermute(down[:HALF], 'expert', fw)  8.73 us
  transfers between devices with their start and end apart: 32, of which 24 were waited for; matrix products, arithmetic and copies ran while one was open for 4% of the time, Pallas kernels for 16%

profile of v4, /device:TPU:8, one launch (start us, length us, event | category | flops | bytes accessed | tf_op | source)
XLA Modules:
  0.0 299.4 jit_solution(1361511858395782393)
XLA Ops:
  3.1 5.9 %collective-permute-start.1 = (bf16[136,2048]{1,0:T(8,128)(2,1)S(1)}, bf16[136,2048]{1,0:T(8,128)(2,1)}, u32[]{:S(2)}, u32[]{:S(2)}) collective-permute-start(bf16[136,2048]{1,0:T(8,128)(2,1)S(1)} %pack_rows.1.refs_0_), channel_id=1, source_target_pairs={{0,56},{1,57},{2,58},{3,59},{4,60},{5,61},{6,62},{7,63},{8,0},{9,1... | collective-permute-start | bytes 1671176 | tf_op jit(solution)/shard_map/ppermute | solution.py:467
  9.0 11.9 %collective-permute-done.1.refs_2_ = bf16[136,2048]{1,0:T(8,128)(2,1)} collective-permute-done((bf16[136,2048]{1,0:T(8,128)(2,1)S(1)}, bf16[136,2048]{1,0:T(8,128)(2,1)}, u32[]{:S(2)}, u32[]{:S(2)}) %collective-permute-start.1) | collective-permute-done | bytes 557088 | tf_op jit(solution)/shard_map/ppermute | solution.py:467
  20.9 3.4 %collective-permute-done.refs_1_ = bf16[136,2048]{1,0:T(8,128)(2,1)S(1)} collective-permute-done((bf16[136,2048]{1,0:T(8,128)(2,1)S(1)}, bf16[136,2048]{1,0:T(8,128)(2,1)S(1)}, u32[]{:S(2)}, u32[]{:S(2)}) %collective-permute-start) | collective-permute-done | bytes 557088 | tf_op jit(solution)/shard_map/ppermute | solution.py:466
  24.3 3.5 %select_tokens.2 = (bf16[448,2048]{1,0:T(8,128)(2,1)}, s32[8,384]{1,0:T(8,128)S(1)}, f32[8,384]{1,0:T(8,128)S(1)}, f32[8,384]{1,0:T(8,128)S(1)}) custom-call(s32[1]{0:T(128)} %bitcast.z_ref, bf16[136,2048]{1,0:T(8,128)(2,1)S(1)} %pack_rows.1.refs_0_, bf16[136,2048]{1,0:T(8,128)(2,1)S(1)} %collective-permute-done.refs_1_, ...), custom_call_target="tpu_custom_call" | custom-call | flops 704643072 | bytes 3407872 | tf_op jit(solution)/shard_map/select_tokens/pallas_call | solution.py:151
  27.8 5.4 %all-to-all-start = ((bf16[8,56,2048]{2,1,0:T(8,128)(2,1)}), bf16[8,56,2048]{2,1,0:T(8,128)(2,1)}, u32[]{:S(2)}, u32[]{:S(2)}) async-start(bf16[8,56,2048]{2,1,0:T(8,128)(2,1)} %bitcast.53), calls=%async_computation | async-start | bytes 3670016 | tf_op jit(solution)/shard_map/all_to_all | solution.py:74
  37.4 10.8 %collective-permute-done.3.refs_2_ = bf16[128,2048]{1,0:T(8,128)(2,1)S(1)} collective-permute-done((bf16[128,2048]{1,0:T(8,128)(2,1)S(1)}, bf16[128,2048]{1,0:T(8,128)(2,1)S(1)}, u32[]{:S(2)}, u32[]{:S(2)}) %collective-permute-start.3) | collective-permute-done | bytes 524320 | tf_op jit(solution)/shard_map/ppermute | solution.py:467
  52.3 5.2 %collective-permute-done.5.refs_1_ = bf16[136,2048]{1,0:T(8,128)(2,1)S(1)} collective-permute-done((bf16[136,2048]{1,0:T(8,128)(2,1)}, bf16[136,2048]{1,0:T(8,128)(2,1)S(1)}, u32[]{:S(2)}, u32[]{:S(2)}) %collective-permute-start.5) | collective-permute-done | bytes 557088 | tf_op jit(solution)/shard_map/ppermute | solution.py:467
  59.1 5.3 %all-to-all-start.1 = ((bf16[8,56,2048]{2,1,0:T(8,128)(2,1)}), bf16[8,56,2048]{2,1,0:T(8,128)(2,1)}, u32[]{:S(2)}, u32[]{:S(2)}) async-start(bf16[8,56,2048]{2,1,0:T(8,128)(2,1)} %bitcast.48), calls=%async_computation.1 | async-start | bytes 3670016 | tf_op jit(solution)/shard_map/all_to_all | solution.py:74
  66.5 10.6 %collective-permute-done.7.refs_3_ = bf16[136,2048]{1,0:T(8,128)(2,1)S(1)} collective-permute-done((bf16[136,2048]{1,0:T(8,128)(2,1)S(1)}, bf16[136,2048]{1,0:T(8,128)(2,1)S(1)}, u32[]{:S(2)}, u32[]{:S(2)}) %collective-permute-start.7) | collective-permute-done | bytes 557088 | tf_op jit(solution)/shard_map/ppermute | solution.py:467
  79.3 6.9 %collective-permute-done.8.refs_4_ = bf16[64,2048]{1,0:T(8,128)(2,1)S(1)} collective-permute-done((bf16[64,2048]{1,0:T(8,128)(2,1)S(1)}, bf16[64,2048]{1,0:T(8,128)(2,1)S(1)}, u32[]{:S(2)}, u32[]{:S(2)}) %collective-permute-start.8) | collective-permute-done | bytes 262176 | tf_op jit(solution)/shard_map/ppermute | solution.py:469
  86.2 4.8 %select_tokens.3 = (bf16[768,2048]{1,0:T(8,128)(2,1)}, s32[8,640]{1,0:T(8,128)S(1)}, f32[8,640]{1,0:T(8,128)S(1)}, f32[8,640]{1,0:T(8,128)S(1)}) custom-call(s32[1]{0:T(128)} %bitcast.z_ref, bf16[136,2048]{1,0:T(8,128)(2,1)S(1)} %collective-permute-done.4.refs_0_, bf16[136,2048]{1,0:T(8,128)(2,1)S(1)} %collective-permute-done.5.refs_1_, ...), custom_call_target="tpu_custom_call" | custom-call | flops 2013265920 | bytes 5767168 | tf_op jit(solution)/shard_map/select_tokens/pallas_call | solution.py:151
  91.0 5.3 %all-to-all-start.2 = ((bf16[8,96,2048]{2,1,0:T(8,128)(2,1)}), bf16[8,96,2048]{2,1,0:T(8,128)(2,1)}, u32[]{:S(2)}, u32[]{:S(2)}) async-start(bf16[8,96,2048]{2,1,0:T(8,128)(2,1)} %bitcast.49), calls=%async_computation.2 | async-start | bytes 6291456 | tf_op jit(solution)/shard_map/all_to_all | solution.py:74
  98.3 10.3 %collective-permute-done.11.refs_1_ = bf16[128,2048]{1,0:T(8,128)(2,1)S(1)} collective-permute-done((bf16[128,2048]{1,0:T(8,128)(2,1)S(1)}, bf16[128,2048]{1,0:T(8,128)(2,1)S(1)}, u32[]{:S(2)}, u32[]{:S(2)}) %collective-permute-start.11) | collective-permute-done | bytes 524320 | tf_op jit(solution)/shard_map/ppermute | solution.py:467
  110.6 10.0 %collective-permute-done.13.refs_3_ = bf16[128,2048]{1,0:T(8,128)(2,1)S(1)} collective-permute-done((bf16[128,2048]{1,0:T(8,128)(2,1)S(1)}, bf16[128,2048]{1,0:T(8,128)(2,1)S(1)}, u32[]{:S(2)}, u32[]{:S(2)}) %collective-permute-start.13) | collective-permute-done | bytes 524320 | tf_op jit(solution)/shard_map/ppermute | solution.py:467
  122.8 4.2 %collective-permute-done.15.refs_5_ = bf16[64,2048]{1,0:T(8,128)(2,1)S(1)} collective-permute-done((bf16[64,2048]{1,0:T(8,128)(2,1)S(1)}, bf16[64,2048]{1,0:T(8,128)(2,1)S(1)}, u32[]{:S(2)}, u32[]{:S(2)}) %collective-permute-start.15) | collective-permute-done | bytes 262176 | tf_op jit(solution)/shard_map/ppermute | solution.py:470
  128.9 4.4 %select_cotangents.3 = bf16[768,2048]{1,0:T(8,128)(2,1)} custom-call(s32[8,640]{1,0:T(8,128)S(1)} %get-tuple-element.60.q_ref, f32[8,640]{1,0:T(8,128)S(1)} %get-tuple-element.61.w_ref, bf16[128,2048]{1,0:T(8,128)(2,1)S(1)} %collective-permute-done.10.refs_0_, bf16[128,2048]{1,0:T(8,128)(2,1)S(1)} %collective-permute-done.11.refs_1_, ...), custom_call_target="tpu_custom_call" | custom-call | flops 2013265920 | bytes 5767168 | tf_op jit(solution)/shard_map/select_cotangents/pallas_call | solution.py:192
  135.3 4.7 %all-to-all-start.3 = ((bf16[8,96,2048]{2,1,0:T(8,128)(2,1)}), bf16[8,96,2048]{2,1,0:T(8,128)(2,1)}, u32[]{:S(2)}, u32[]{:S(2)}) async-start(bf16[8,96,2048]{2,1,0:T(8,128)(2,1)} %bitcast.50), calls=%async_computation.3 | async-start | bytes 6291456 | tf_op jit(solution)/shard_map/all_to_all | solution.py:74
  142.8 4.4 %expert_forward.2.p_ref = f32[448,768]{1,0:T(8,128)} custom-call(bf16[448,2048]{1,0:T(8,128)(2,1)} %bitcast.8.x_ref.xn, bf16[2048,768]{1,0:T(8,128)(2,1)S(1)} %get-tuple-element.68.w_ref), custom_call_target="tpu_custom_call" | custom-call | flops 1409286144 | bytes 4980736 | tf_op jit(solution)/shard_map/expert_forward/pallas_call | solution.py:243
  147.2 6.1 %expert_backward.2 = (bf16[448,2048]{1,0:T(8,128)(2,1)}, bf16[448,768]{1,0:T(8,128)(2,1)}, bf16[448,384]{1,0:T(8,128)(2,1)}) custom-call(bf16[448,2048]{1,0:T(8,128)(2,1)} %bitcast.10.sc_ref.sn, f32[448,768]{1,0:T(8,128)} %expert_forward.2.p_ref, bf16[2048,768]{1,0:T(8,128)(2,1)S(1)} %get-tuple-element.68.w_ref, bf16[2048,384]{1,0:T(8,128)(2,1)S(1)} %get-tuple-element.69.wd_ref), custom_call_target="tpu_custom_call" | custom-call | flops 2113929216 | bytes 8388608 | tf_op jit(solution)/shard_map/expert_backward/pallas_call | solution.py:289
  153.3 5.2 %expert_forward.3.p_ref = f32[768,768]{1,0:T(8,128)} custom-call(bf16[768,2048]{1,0:T(8,128)(2,1)} %bitcast.12.x_ref.xf, bf16[2048,768]{1,0:T(8,128)(2,1)S(1)} %get-tuple-element.68.w_ref), custom_call_target="tpu_custom_call" | custom-call | flops 2415919104 | bytes 6291456 | tf_op jit(solution)/shard_map/expert_forward/pallas_call | solution.py:243
  158.5 23.2 %all-to-all-done.3 = bf16[8,96,2048]{2,1,0:T(8,128)(2,1)} async-done(((bf16[8,96,2048]{2,1,0:T(8,128)(2,1)}), bf16[8,96,2048]{2,1,0:T(8,128)(2,1)}, u32[]{:S(2)}, u32[]{:S(2)}) %all-to-all-start.3) | async-done | bytes 3145760 | tf_op jit(solution)/shard_map/all_to_all | solution.py:74
  183.1 8.1 %expert_backward.3 = (bf16[768,2048]{1,0:T(8,128)(2,1)}, bf16[768,768]{1,0:T(8,128)(2,1)}, bf16[768,384]{1,0:T(8,128)(2,1)}) custom-call(bf16[768,2048]{1,0:T(8,128)(2,1)} %bitcast.14.sc_ref.sf, f32[768,768]{1,0:T(8,128)} %expert_forward.3.p_ref, bf16[2048,768]{1,0:T(8,128)(2,1)S(1)} %get-tuple-element.68.w_ref, bf16[2048,384]{1,0:T(8,128)(2,1)S(1)} %copy-done.2), custom_call_target="tpu_custom_call" | custom-call | flops 3623878656 | bytes 11010048 | tf_op jit(solution)/shard_map/expert_backward/pallas_call | solution.py:289
  191.2 3.6 %all-to-all-start.4 = ((bf16[8,96,2048]{2,1,0:T(8,128)(2,1)}), bf16[8,96,2048]{2,1,0:T(8,128)(2,1)S(1)}, u32[]{:S(2)}, u32[]{:S(2)}) async-start(bf16[8,96,2048]{2,1,0:T(8,128)(2,1)} %bitcast.51), calls=%async_computation.4 | async-start | bytes 6291456 | tf_op jit(solution)/shard_map/all_to_all | solution.py:74
  194.9 12.7 %weight_grads.1 = (bf16[2,3,512,384]{3,2,1,0:T(8,128)(2,1)}, bf16[2,3,512,384]{3,2,1,0:T(8,128)(2,1)}) custom-call(s32[1]{0:T(128)} %bitcast.19.sec_ref, bf16[448,2048]{1,0:T(8,128)(2,1)} %bitcast.8.x_ref.xn, bf16[768,2048]{1,0:T(8,128)(2,1)} %bitcast.12.x_ref.xf, bf16[448,2048]{1,0:T(8,128)(2,1)} %bitcast.10.sc_ref.sn, ...), custom_call_target="tpu_custom_call" | custom-call | flops 5737807872 | bytes 14680064 | tf_op jit(solution)/shard_map/weight_grads/pallas_call | solution.py:347
  207.6 4.7 %collective-permute-done.16 = bf16[2,3,512,384]{3,2,1,0:T(8,128)(2,1)S(1)} collective-permute-done((bf16[2,3,512,384]{3,2,1,0:T(8,128)(2,1)}, bf16[2,3,512,384]{3,2,1,0:T(8,128)(2,1)S(1)}, u32[]{:S(2)}, u32[]{:S(2)}) %collective-permute-start.16) | collective-permute-done | bytes 2359328 | tf_op jit(solution)/shard_map/ppermute | solution.py:368
  216.3 21.4 %all-to-all-done.4 = bf16[8,96,2048]{2,1,0:T(8,128)(2,1)S(1)} async-done(((bf16[8,96,2048]{2,1,0:T(8,128)(2,1)}), bf16[8,96,2048]{2,1,0:T(8,128)(2,1)S(1)}, u32[]{:S(2)}, u32[]{:S(2)}) %all-to-all-start.4) | async-done | bytes 3145760 | tf_op jit(solution)/shard_map/all_to_all | solution.py:74
  240.1 4.5 %combine_rows.3 = (bf16[136,2048]{1,0:T(8,128)(2,1)}, bf16[136,2048]{1,0:T(8,128)(2,1)}, bf16[136,2048]{1,0:T(8,128)(2,1)}, bf16[136,2048]{1,0:T(8,128)(2,1)}, bf16[136,2048]{1,0:T(8,128)(2,1)}) custom-call(s32[1]{0:T(128)} %bitcast.z_ref, s32[8,640]{1,0:T(8,128)S(1)} %get-tuple-element.60.q_ref, f32[8,640]{1,0:T(8,128)S(1)} %get-tuple-element.61.w_ref, ...), custom_call_target="tpu_custom_call" | custom-call | flops 2013265920 | bytes 5767168 | tf_op jit(solution)/shard_map/combine_rows/pallas_call | solution.py:442
  244.7 3.7 %all-to-all-start.5 = ((bf16[8,56,2048]{2,1,0:T(8,128)(2,1)}), bf16[8,56,2048]{2,1,0:T(8,128)(2,1)S(1)}, u32[]{:S(2)}, u32[]{:S(2)}) async-start(bf16[8,56,2048]{2,1,0:T(8,128)(2,1)} %bitcast.52), calls=%async_computation.5 | async-start | bytes 3670016 | tf_op jit(solution)/shard_map/all_to_all | solution.py:74
  262.8 3.6 %collective-permute-start.24 = (bf16[136,2048]{1,0:T(8,128)(2,1)}, bf16[136,2048]{1,0:T(8,128)(2,1)}, u32[]{:S(2)}, u32[]{:S(2)}) collective-permute-start(bf16[136,2048]{1,0:T(8,128)(2,1)} %add_convert_fusion.3), channel_id=1, source_target_pairs={{0,56},{1,57},{2,58},{3,59},{4,60},{5,61},{6,62},{7,63},{8,0},{9,1... | collective-permute-start | bytes 1671176 | tf_op jit(solution)/shard_map/ppermute | solution.py:487
  266.4 6.6 %collective-permute-done.20 = bf16[136,2048]{1,0:T(8,128)(2,1)S(1)} collective-permute-done((bf16[136,2048]{1,0:T(8,128)(2,1)S(1)}, bf16[136,2048]{1,0:T(8,128)(2,1)S(1)}, u32[]{:S(2)}, u32[]{:S(2)}) %collective-permute-start.20) | collective-permute-done | bytes 557088 | tf_op jit(solution)/shard_map/ppermute | solution.py:485
  280.8 4.4 %collective-permute-done.21 = bf16[136,2048]{1,0:T(8,128)(2,1)} collective-permute-done((bf16[136,2048]{1,0:T(8,128)(2,1)S(1)}, bf16[136,2048]{1,0:T(8,128)(2,1)}, u32[]{:S(2)}, u32[]{:S(2)}) %collective-permute-start.21) | collective-permute-done | bytes 557088 | tf_op jit(solution)/shard_map/ppermute | solution.py:485
  290.3 7.3 %collective-permute-done.22 = bf16[136,2048]{1,0:T(8,128)(2,1)S(1)} collective-permute-done((bf16[136,2048]{1,0:T(8,128)(2,1)S(1)}, bf16[136,2048]{1,0:T(8,128)(2,1)S(1)}, u32[]{:S(2)}, u32[]{:S(2)}) %collective-permute-start.22) | collective-permute-done | bytes 557088 | tf_op jit(solution)/shard_map/ppermute | solution.py:488
  (88 shorter events, 66.1 us)
Async XLA Ops:
  3.1 17.8 %collective-permute-start.1 = (bf16[136,2048]{1,0:T(8,128)(2,1)S(1)}, bf16[136,2048]{1,0:T(8,128)(2,1)}, u32[]{:S(2)}, u32[]{:S(2)}) collective-permute-start(bf16[136,2048]{1,0:T(8,128)(2,1)S(1)} %pack_rows.1.refs_0_), channel_id=1, source_target_pairs={{0,56},{1,57},{2,58},{3,59},{4,60},{5,61},{6,62},{7,63},{8,0},{9,1... | collective-permute-start | bytes 1671176 | tf_op jit(solution)/shard_map/ppermute | solution.py:467
  9.0 15.3 %collective-permute-start = (bf16[136,2048]{1,0:T(8,128)(2,1)S(1)}, bf16[136,2048]{1,0:T(8,128)(2,1)S(1)}, u32[]{:S(2)}, u32[]{:S(2)}) collective-permute-start(bf16[136,2048]{1,0:T(8,128)(2,1)S(1)} %pack_rows.1.refs_0_), channel_id=1, source_target_pairs={{0,8},{1,9},{2,10},{3,11},{4,12},{5,13},{6,14},{7,15},{8,16},{9,17... | collective-permute-start | bytes 1671176 | tf_op jit(solution)/shard_map/ppermute | solution.py:466
  27.8 31.3 %all-to-all-start = ((bf16[8,56,2048]{2,1,0:T(8,128)(2,1)}), bf16[8,56,2048]{2,1,0:T(8,128)(2,1)}, u32[]{:S(2)}, u32[]{:S(2)}) async-start(bf16[8,56,2048]{2,1,0:T(8,128)(2,1)} %bitcast.53), calls=%async_computation | async-start | bytes 3670016 | tf_op jit(solution)/shard_map/all_to_all | solution.py:74
  33.3 14.9 %collective-permute-start.3 = (bf16[128,2048]{1,0:T(8,128)(2,1)S(1)}, bf16[128,2048]{1,0:T(8,128)(2,1)S(1)}, u32[]{:S(2)}, u32[]{:S(2)}) collective-permute-start(bf16[128,2048]{1,0:T(8,128)(2,1)S(1)} %bitcast.43), channel_id=1, source_target_pairs={{0,56},{1,57},{2,58},{3,59},{4,60},{5,61},{6,62},{7,63},{8,0},{9,1... | collective-permute-start | bytes 1572872 | tf_op jit(solution)/shard_map/ppermute | solution.py:467
  33.7 16.1 %collective-permute-start.2 = (bf16[128,2048]{1,0:T(8,128)(2,1)S(1)}, bf16[128,2048]{1,0:T(8,128)(2,1)S(1)}, u32[]{:S(2)}, u32[]{:S(2)}) collective-permute-start(bf16[128,2048]{1,0:T(8,128)(2,1)S(1)} %bitcast.44), channel_id=1, source_target_pairs={{0,8},{1,9},{2,10},{3,11},{4,12},{5,13},{6,14},{7,15},{8,16},{9,17... | collective-permute-start | bytes 1572872 | tf_op jit(solution)/shard_map/ppermute | solution.py:466
  35.4 22.1 %collective-permute-start.5 = (bf16[136,2048]{1,0:T(8,128)(2,1)}, bf16[136,2048]{1,0:T(8,128)(2,1)S(1)}, u32[]{:S(2)}, u32[]{:S(2)}) collective-permute-start(bf16[136,2048]{1,0:T(8,128)(2,1)} %collective-permute-done.1.refs_2_), channel_id=1, source_target_pairs={{0,56},{1,57},{2,58},{3,59},{4,60},{5,61},{6,62},{7,63},{8,0},{9,1... | collective-permute-start | bytes 1671176 | tf_op jit(solution)/shard_map/ppermute | solution.py:467
  37.0 22.1 %collective-permute-start.4 = (bf16[136,2048]{1,0:T(8,128)(2,1)S(1)}, bf16[136,2048]{1,0:T(8,128)(2,1)S(1)}, u32[]{:S(2)}, u32[]{:S(2)}) collective-permute-start(bf16[136,2048]{1,0:T(8,128)(2,1)S(1)} %collective-permute-done.refs_1_), channel_id=1, source_target_pairs={{0,8},{1,9},{2,10},{3,11},{4,12},{5,13},{6,14},{7,15},{8,16},{9,17... | collective-permute-start | bytes 1671176 | tf_op jit(solution)/shard_map/ppermute | solution.py:466
  59.1 31.9 %all-to-all-start.1 = ((bf16[8,56,2048]{2,1,0:T(8,128)(2,1)}), bf16[8,56,2048]{2,1,0:T(8,128)(2,1)}, u32[]{:S(2)}, u32[]{:S(2)}) async-start(bf16[8,56,2048]{2,1,0:T(8,128)(2,1)} %bitcast.48), calls=%async_computation.1 | async-start | bytes 3670016 | tf_op jit(solution)/shard_map/all_to_all | solution.py:74
  64.5 12.6 %collective-permute-start.7 = (bf16[136,2048]{1,0:T(8,128)(2,1)S(1)}, bf16[136,2048]{1,0:T(8,128)(2,1)S(1)}, u32[]{:S(2)}, u32[]{:S(2)}) collective-permute-start(bf16[136,2048]{1,0:T(8,128)(2,1)S(1)} %collective-permute-done.5.refs_1_), channel_id=1, source_target_pairs={{0,56},{1,57},{2,58},{3,59},{4,60},{5,61},{6,62},{7,63},{8,0},{9,1... | collective-permute-start | bytes 1671176 | tf_op jit(solution)/shard_map/ppermute | solution.py:467
  64.8 13.7 %collective-permute-start.6 = (bf16[136,2048]{1,0:T(8,128)(2,1)S(1)}, bf16[136,2048]{1,0:T(8,128)(2,1)S(1)}, u32[]{:S(2)}, u32[]{:S(2)}) collective-permute-start(bf16[136,2048]{1,0:T(8,128)(2,1)S(1)} %collective-permute-done.4.refs_0_), channel_id=1, source_target_pairs={{0,8},{1,9},{2,10},{3,11},{4,12},{5,13},{6,14},{7,15},{8,16},{9,17... | collective-permute-start | bytes 1671176 | tf_op jit(solution)/shard_map/ppermute | solution.py:466
  77.1 9.1 %collective-permute-start.9 = (bf16[72,2048]{1,0:T(8,128)(2,1)S(1)}, bf16[72,2048]{1,0:T(8,128)(2,1)S(1)}, u32[]{:S(2)}, u32[]{:S(2)}) collective-permute-start(bf16[72,2048]{1,0:T(8,128)(2,1)S(1)} %slice.51), channel_id=1, source_target_pairs={{0,56},{1,57},{2,58},{3,59},{4,60},{5,61},{6,62},{7,63},{8,0},{9,1... | collective-permute-start | bytes 884744 | tf_op jit(solution)/shard_map/ppermute | solution.py:470
  78.5 7.7 %collective-permute-start.8 = (bf16[64,2048]{1,0:T(8,128)(2,1)S(1)}, bf16[64,2048]{1,0:T(8,128)(2,1)S(1)}, u32[]{:S(2)}, u32[]{:S(2)}) collective-permute-start(bf16[64,2048]{1,0:T(8,128)(2,1)S(1)} %slice.50), channel_id=1, source_target_pairs={{0,8},{1,9},{2,10},{3,11},{4,12},{5,13},{6,14},{7,15},{8,16},{9,17... | collective-permute-start | bytes 786440 | tf_op jit(solution)/shard_map/ppermute | solution.py:469
  91.0 44.3 %all-to-all-start.2 = ((bf16[8,96,2048]{2,1,0:T(8,128)(2,1)}), bf16[8,96,2048]{2,1,0:T(8,128)(2,1)}, u32[]{:S(2)}, u32[]{:S(2)}) async-start(bf16[8,96,2048]{2,1,0:T(8,128)(2,1)} %bitcast.49), calls=%async_computation.2 | async-start | bytes 6291456 | tf_op jit(solution)/shard_map/all_to_all | solution.py:74
  96.3 12.4 %collective-permute-start.11 = (bf16[128,2048]{1,0:T(8,128)(2,1)S(1)}, bf16[128,2048]{1,0:T(8,128)(2,1)S(1)}, u32[]{:S(2)}, u32[]{:S(2)}) collective-permute-start(bf16[128,2048]{1,0:T(8,128)(2,1)S(1)} %collective-permute-done.3.refs_2_), channel_id=1, source_target_pairs={{0,56},{1,57},{2,58},{3,59},{4,60},{5,61},{6,62},{7,63},{8,0},{9,1... | collective-permute-start | bytes 1572872 | tf_op jit(solution)/shard_map/ppermute | solution.py:467
  96.5 12.1 %collective-permute-start.10 = (bf16[128,2048]{1,0:T(8,128)(2,1)S(1)}, bf16[128,2048]{1,0:T(8,128)(2,1)S(1)}, u32[]{:S(2)}, u32[]{:S(2)}) collective-permute-start(bf16[128,2048]{1,0:T(8,128)(2,1)S(1)} %collective-permute-done.2.refs_1_), channel_id=1, source_target_pairs={{0,8},{1,9},{2,10},{3,11},{4,12},{5,13},{6,14},{7,15},{8,16},{9,17... | collective-permute-start | bytes 1572872 | tf_op jit(solution)/shard_map/ppermute | solution.py:466
  108.6 12.0 %collective-permute-start.13 = (bf16[128,2048]{1,0:T(8,128)(2,1)S(1)}, bf16[128,2048]{1,0:T(8,128)(2,1)S(1)}, u32[]{:S(2)}, u32[]{:S(2)}) collective-permute-start(bf16[128,2048]{1,0:T(8,128)(2,1)S(1)} %collective-permute-done.11.refs_1_), channel_id=1, source_target_pairs={{0,56},{1,57},{2,58},{3,59},{4,60},{5,61},{6,62},{7,63},{8,0},{9,1... | collective-permute-start | bytes 1572872 | tf_op jit(solution)/shard_map/ppermute | solution.py:467
  108.6 12.6 %collective-permute-start.12 = (bf16[128,2048]{1,0:T(8,128)(2,1)S(1)}, bf16[128,2048]{1,0:T(8,128)(2,1)S(1)}, u32[]{:S(2)}, u32[]{:S(2)}) collective-permute-start(bf16[128,2048]{1,0:T(8,128)(2,1)S(1)} %collective-permute-done.10.refs_0_), channel_id=1, source_target_pairs={{0,8},{1,9},{2,10},{3,11},{4,12},{5,13},{6,14},{7,15},{8,16},{9,17... | collective-permute-start | bytes 1572872 | tf_op jit(solution)/shard_map/ppermute | solution.py:466
  120.6 6.5 %collective-permute-start.15 = (bf16[64,2048]{1,0:T(8,128)(2,1)S(1)}, bf16[64,2048]{1,0:T(8,128)(2,1)S(1)}, u32[]{:S(2)}, u32[]{:S(2)}) collective-permute-start(bf16[64,2048]{1,0:T(8,128)(2,1)S(1)} %slice.53), channel_id=1, source_target_pairs={{0,56},{1,57},{2,58},{3,59},{4,60},{5,61},{6,62},{7,63},{8,0},{9,1... | collective-permute-start | bytes 786440 | tf_op jit(solution)/shard_map/ppermute | solution.py:470
  121.3 7.7 %collective-permute-start.14 = (bf16[64,2048]{1,0:T(8,128)(2,1)S(1)}, bf16[64,2048]{1,0:T(8,128)(2,1)S(1)}, u32[]{:S(2)}, u32[]{:S(2)}) collective-permute-start(bf16[64,2048]{1,0:T(8,128)(2,1)S(1)} %slice.52), channel_id=1, source_target_pairs={{0,8},{1,9},{2,10},{3,11},{4,12},{5,13},{6,14},{7,15},{8,16},{9,17... | collective-permute-start | bytes 786440 | tf_op jit(solution)/shard_map/ppermute | solution.py:469
  135.3 46.3 %all-to-all-start.3 = ((bf16[8,96,2048]{2,1,0:T(8,128)(2,1)}), bf16[8,96,2048]{2,1,0:T(8,128)(2,1)}, u32[]{:S(2)}, u32[]{:S(2)}) async-start(bf16[8,96,2048]{2,1,0:T(8,128)(2,1)} %bitcast.50), calls=%async_computation.3 | async-start | bytes 6291456 | tf_op jit(solution)/shard_map/all_to_all | solution.py:74
  191.2 46.5 %all-to-all-start.4 = ((bf16[8,96,2048]{2,1,0:T(8,128)(2,1)}), bf16[8,96,2048]{2,1,0:T(8,128)(2,1)S(1)}, u32[]{:S(2)}, u32[]{:S(2)}) async-start(bf16[8,96,2048]{2,1,0:T(8,128)(2,1)} %bitcast.51), calls=%async_computation.4 | async-start | bytes 6291456 | tf_op jit(solution)/shard_map/all_to_all | solution.py:74
  207.6 4.7 %collective-permute-start.16 = (bf16[2,3,512,384]{3,2,1,0:T(8,128)(2,1)}, bf16[2,3,512,384]{3,2,1,0:T(8,128)(2,1)S(1)}, u32[]{:S(2)}, u32[]{:S(2)}) collective-permute-start(bf16[2,3,512,384]{3,2,1,0:T(8,128)(2,1)} %get-tuple-element.85), channel_id=1, source_target_pairs={{0,64},{64,0},{128,192},{192,128},{1,65},{65,1},{129,193},{193,129... | collective-permute-start | bytes 7077896 | tf_op jit(solution)/shard_map/ppermute | solution.py:368
  240.1 15.3 %collective-permute-start.18 = (bf16[3,256,384]{2,1,0:T(8,128)(2,1)}, bf16[3,256,384]{2,1,0:T(8,128)(2,1)}, u32[]{:S(2)}, u32[]{:S(2)}) collective-permute-start(bf16[3,256,384]{2,1,0:T(8,128)(2,1)} %get-tuple-element.103), channel_id=1, source_target_pairs={{0,128},{64,192},{128,0},{192,64},{1,129},{65,193},{129,1},{193,65... | collective-permute-start | bytes 1769480 | tf_op jit(solution)/shard_map/ppermute | solution.py:372
  244.7 14.1 %collective-permute-start.19 = (bf16[136,2048]{1,0:T(8,128)(2,1)}, bf16[136,2048]{1,0:T(8,128)(2,1)}, u32[]{:S(2)}, u32[]{:S(2)}) collective-permute-start(bf16[136,2048]{1,0:T(8,128)(2,1)} %get-tuple-element.93), channel_id=1, source_target_pairs={{0,8},{1,9},{2,10},{3,11},{4,12},{5,13},{6,14},{7,15},{8,16},{9,17... | collective-permute-start | bytes 1671176 | tf_op jit(solution)/shard_map/ppermute | solution.py:485
  244.7 28.6 %all-to-all-start.5 = ((bf16[8,56,2048]{2,1,0:T(8,128)(2,1)}), bf16[8,56,2048]{2,1,0:T(8,128)(2,1)S(1)}, u32[]{:S(2)}, u32[]{:S(2)}) async-start(bf16[8,56,2048]{2,1,0:T(8,128)(2,1)} %bitcast.52), calls=%async_computation.5 | async-start | bytes 3670016 | tf_op jit(solution)/shard_map/all_to_all | solution.py:74
  248.4 13.4 %collective-permute-start.23 = (bf16[136,2048]{1,0:T(8,128)(2,1)}, bf16[136,2048]{1,0:T(8,128)(2,1)S(1)}, u32[]{:S(2)}, u32[]{:S(2)}) collective-permute-start(bf16[136,2048]{1,0:T(8,128)(2,1)} %get-tuple-element.96), channel_id=1, source_target_pairs={{0,56},{1,57},{2,58},{3,59},{4,60},{5,61},{6,62},{7,63},{8,0},{9,1... | collective-permute-start | bytes 1671176 | tf_op jit(solution)/shard_map/ppermute | solution.py:487
  251.7 14.6 %collective-permute-start.17 = (bf16[3,256,384]{2,1,0:T(8,128)(2,1)S(1)}, bf16[3,256,384]{2,1,0:T(8,128)(2,1)S(1)}, u32[]{:S(2)}, u32[]{:S(2)}) collective-permute-start(bf16[3,256,384]{2,1,0:T(8,128)(2,1)S(1)} %copy-done.10), channel_id=1, source_target_pairs={{0,128},{64,192},{128,0},{192,64},{1,129},{65,193},{129,1},{193,65... | collective-permute-start | bytes 1769480 | tf_op jit(solution)/shard_map/ppermute | solution.py:373
  260.1 12.9 %collective-permute-start.20 = (bf16[136,2048]{1,0:T(8,128)(2,1)S(1)}, bf16[136,2048]{1,0:T(8,128)(2,1)S(1)}, u32[]{:S(2)}, u32[]{:S(2)}) collective-permute-start(bf16[136,2048]{1,0:T(8,128)(2,1)S(1)} %add_convert_fusion.6), channel_id=1, source_target_pairs={{0,8},{1,9},{2,10},{3,11},{4,12},{5,13},{6,14},{7,15},{8,16},{9,17... | collective-permute-start | bytes 1671176 | tf_op jit(solution)/shard_map/ppermute | solution.py:485
  262.8 13.3 %collective-permute-start.24 = (bf16[136,2048]{1,0:T(8,128)(2,1)}, bf16[136,2048]{1,0:T(8,128)(2,1)}, u32[]{:S(2)}, u32[]{:S(2)}) collective-permute-start(bf16[136,2048]{1,0:T(8,128)(2,1)} %add_convert_fusion.3), channel_id=1, source_target_pairs={{0,56},{1,57},{2,58},{3,59},{4,60},{5,61},{6,62},{7,63},{8,0},{9,1... | collective-permute-start | bytes 1671176 | tf_op jit(solution)/shard_map/ppermute | solution.py:487
  273.2 12.1 %collective-permute-start.21 = (bf16[136,2048]{1,0:T(8,128)(2,1)S(1)}, bf16[136,2048]{1,0:T(8,128)(2,1)}, u32[]{:S(2)}, u32[]{:S(2)}) collective-permute-start(bf16[136,2048]{1,0:T(8,128)(2,1)S(1)} %add_convert_fusion.5), channel_id=1, source_target_pairs={{0,8},{1,9},{2,10},{3,11},{4,12},{5,13},{6,14},{7,15},{8,16},{9,17... | collective-permute-start | bytes 1671176 | tf_op jit(solution)/shard_map/ppermute | solution.py:485
  277.6 12.8 %collective-permute-start.25 = (bf16[136,2048]{1,0:T(8,128)(2,1)S(1)}, bf16[136,2048]{1,0:T(8,128)(2,1)S(1)}, u32[]{:S(2)}, u32[]{:S(2)}) collective-permute-start(bf16[136,2048]{1,0:T(8,128)(2,1)S(1)} %add_convert_fusion.2), channel_id=1, source_target_pairs={{0,56},{1,57},{2,58},{3,59},{4,60},{5,61},{6,62},{7,63},{8,0},{9,1... | collective-permute-start | bytes 1671176 | tf_op jit(solution)/shard_map/ppermute | solution.py:489
  286.6 11.1 %collective-permute-start.22 = (bf16[136,2048]{1,0:T(8,128)(2,1)S(1)}, bf16[136,2048]{1,0:T(8,128)(2,1)S(1)}, u32[]{:S(2)}, u32[]{:S(2)}) collective-permute-start(bf16[136,2048]{1,0:T(8,128)(2,1)S(1)} %add_convert_fusion.4), channel_id=1, source_target_pairs={{0,8},{1,9},{2,10},{3,11},{4,12},{5,13},{6,14},{7,15},{8,16},{9,17... | collective-permute-start | bytes 1671176 | tf_op jit(solution)/shard_map/ppermute | solution.py:488
  (14 other events, 97.5 us)
